TPU v7x, 512 devices: a whole 4x4x16 slice. The times are simulated.
512 devices in a mesh: wide: 64 (over y, z_lo, core), narrow: 8 (over x, z_hi).
Axes of the slice: x: 4, y: 4, z: 16 (z_hi: 2, z_lo: 8; z = z_hi * 8 + z_lo), core: 2. Of those that a mesh axis runs over, the one named last changes fastest.
Arguments:
- tensor: bfloat16 [16, 4096, 8192], P('narrow', 'wide'), may hold values from -16 to 16
- factor_a: bfloat16 [32, 4096], P(None, 'wide'), may hold values from -0.21875 to 0.21875
- factor_b: bfloat16 [32, 8192], P(None, 'wide'), may hold values from -0.15625 to 0.15625
- factor_c: bfloat16 [32, 16], P(None, 'narrow'), may hold values from -4 to 4
Outputs:
- step_a: float32 [32, 4096], P(None, 'wide')
- step_b: float32 [32, 8192], P(None, 'wide')
- step_c: float32 [32, 16], P(None, 'narrow')
All inputs are finite; a program needn't handle non-finite values.
Results may differ from a plain program's by a relative error of at most 0.0029.
Values may be sent and summed in bfloat16 or wider, within the bound.
No kernel may reach another device: no remote copies, remote signals or barrier semaphores. Data moves between devices by JAX's collectives and lax.ppermute only.
A program may use at most 64 MiB of HBM per device.

v0:
```python
import jax
import jax.numpy as jnp
from jax import lax
from jax.sharding import PartitionSpec as P

ITERS = 2


damping = 1.0
highest = lax.Precision.HIGHEST


def matmul(left, right):
    return jnp.dot(left, right, precision=highest)


def outer_rows(left, right):
    return lax.dot_general(left, right, (((1,), (1,)), ((), ())), precision=highest)


def combine_dot(wide_part, narrow_part):
    return lax.psum(wide_part, "wide") + lax.psum(narrow_part, "narrow")


def self_inner(triple):
    return combine_dot(
        jnp.sum(triple[0] * triple[0]) + jnp.sum(triple[1] * triple[1]),
        jnp.sum(triple[2] * triple[2]),
    )


def gram_product(factors, grams, directions):
    float_a, float_b, float_c = factors
    gram_a, gram_b, gram_c = grams
    dir_a, dir_b, dir_c = directions
    local_a = outer_rows(float_a, dir_a)
    local_b = outer_rows(float_b, dir_b)
    local_c = outer_rows(float_c, dir_c)
    cross_a, cross_b = lax.psum((local_a, local_b), "wide")
    cross_c = lax.psum(local_c, "narrow")
    hadamard_a = gram_b * gram_c
    hadamard_b = gram_a * gram_c
    hadamard_c = gram_a * gram_b
    mixed_a = cross_b * gram_c + gram_b * cross_c
    mixed_b = cross_a * gram_c + gram_a * cross_c
    mixed_c = cross_a * gram_b + gram_a * cross_b
    image_a = matmul(hadamard_a, dir_a) + matmul(mixed_a, float_a) + damping * dir_a
    image_b = matmul(hadamard_b, dir_b) + matmul(mixed_b, float_b) + damping * dir_b
    image_c = matmul(hadamard_c, dir_c) + matmul(mixed_c, float_c) + damping * dir_c
    curvature = combine_dot(
        jnp.sum(dir_a * image_a) + jnp.sum(dir_b * image_b), jnp.sum(dir_c * image_c)
    )
    return ((image_a, image_b, image_c), curvature)


def on_device(tensor, factor_a, factor_b, factor_c):
    k_local, i_local, j_whole = tensor.shape
    rank = factor_a.shape[0]
    j_local = factor_b.shape[1]
    flattened = tensor.reshape(k_local * i_local, j_whole)
    contracted = lax.dot_general(
        lax.all_gather(factor_b, "wide", axis=1, tiled=True),
        flattened,
        (((1,), (1,)), ((), ())),
        preferred_element_type=jnp.float32,
    ).reshape(rank, k_local, i_local)
    float_a = factor_a.astype(jnp.float32)
    float_b = factor_b.astype(jnp.float32)
    float_c = factor_c.astype(jnp.float32)
    part_a = jnp.einsum("rk,rki->ri", float_c, contracted, precision=highest)
    part_c = jnp.einsum("ri,rki->rk", float_a, contracted, precision=highest)
    own_gram_a = jnp.dot(factor_a, factor_a.T, preferred_element_type=jnp.float32)
    own_gram_b = jnp.dot(factor_b, factor_b.T, preferred_element_type=jnp.float32)
    own_gram_c = jnp.dot(factor_c, factor_c.T, preferred_element_type=jnp.float32)
    mttkrp_a, gram_c = lax.psum((part_a, own_gram_c), "narrow")
    mttkrp_c, gram_a, gram_b = lax.psum((part_c, own_gram_a, own_gram_b), "wide")
    khatri = (
        (float_c[:, :, None] * float_a[:, None, :])
        .reshape(rank, k_local * i_local)
        .astype(jnp.bfloat16)
    )
    partial_b = jnp.dot(khatri, flattened, preferred_element_type=jnp.float32)
    total_b = lax.psum(partial_b, ("wide", "narrow"))
    mttkrp_b = lax.dynamic_slice_in_dim(total_b, lax.axis_index("wide") * j_local, j_local, 1)
    grad_a = matmul(gram_b * gram_c, float_a) - mttkrp_a
    grad_b = matmul(gram_a * gram_c, float_b) - mttkrp_b
    grad_c = matmul(gram_a * gram_b, float_c) - mttkrp_c
    factors = (float_a, float_b, float_c)
    grams = (gram_a, gram_b, gram_c)
    resid = (-grad_a, -grad_b, -grad_c)
    direction = resid
    steps = (jnp.zeros_like(grad_a), jnp.zeros_like(grad_b), jnp.zeros_like(grad_c))
    norm_now = self_inner(resid)
    for iteration in range(ITERS):
        image, curvature = gram_product(factors, grams, direction)
        step_size = norm_now / curvature
        steps = tuple((old + step_size * move for old, move in zip(steps, direction)))
        if iteration + 1 < ITERS:
            resid = tuple((old - step_size * move for old, move in zip(resid, image)))
            norm_next = self_inner(resid)
            momentum = norm_next / norm_now
            direction = tuple((now + momentum * old for now, old in zip(resid, direction)))
            norm_now = norm_next
    return (steps[0], steps[1], steps[2])


def solution(mesh):
    placed = (P("narrow", "wide", None), P(None, "wide"), P(None, "wide"), P(None, "narrow"))
    return jax.shard_map(
        on_device,
        mesh=mesh,
        in_specs=placed,
        out_specs=(P(None, "wide"), P(None, "wide"), P(None, "narrow")),
        check_vma=False,
    )
```

profile of v0, /device:TPU:1, one launch (start us, length us, event | category | flops | bytes accessed | tf_op | source)
XLA Modules:
  0.0 2312.1 jit_solution(18251631645562315056)
XLA Ops:
  7.2 0.8 convert_element_type.12
  8.1 0.7 convert_element_type.11
  8.8 1.6 convolution_bitcast_fusion
  10.6 129.4 %all_gather.3 = bf16[32,8192]{1,0:T(8,128)(2,1)S(1)} all-gather(bf16[32,128]{1,0:T(8,128)(2,1)S(1)} %copy-done.1), channel_id=1, replica_groups=mesh['wide'=64,'narrow'=8] {'wide'}, dimensions={1}, use_global_device_ids=true | all-gather | bytes 532480 | tf_op jit(solution)/shard_map/all_gather | solution.py:62
  140.3 1.1 fusion.12
  141.4 0.3 fusion.16
  141.7 0.2 fusion.14
  141.9 66.7 %all-reduce.6 = (f32[32,32]{1,0:T(8,128)S(1)}, f32[32,64]{1,0:T(8,128)S(1)}) all-reduce(f32[32,32]{1,0:T(8,128)S(1)} %fusion.51, f32[32,64]{1,0:T(8,128)S(1)} %bitcast.63), channel_id=1, replica_groups=mesh['wide'=64,'narrow'=8] {'narrow'}, use_global_device_ids=true, to_apply=%region_1.0 | all-reduce | flops 3072 | bytes 24576 | tf_op jit(solution)/shard_map/psum | solution.py:75
  208.7 415.4 %all-reduce.3 = (f32[32,32]{1,0:T(8,128)S(1)}, f32[32,32]{1,0:T(8,128)S(1)}) all-reduce(f32[32,32]{1,0:T(8,128)S(1)} %fusion.50, f32[32,32]{1,0:T(8,128)S(1)} %fusion.52), channel_id=1, replica_groups=mesh['wide'=64,'narrow'=8] {'wide'}, use_global_device_ids=true, to_apply=%region_0.0 | all-reduce | flops 2048 | bytes 16384 | tf_op jit(solution)/shard_map/psum | solution.py:76
  624.6 0.8 convolution_subtract_fusion
  625.7 418.8 %all-reduce.2 = (f32[32,2]{0,1:T(2,128)S(1)}, f32[32,32]{1,0:T(8,128)S(1)}, f32[32,32]{1,0:T(8,128)S(1)}) all-reduce(f32[32,2]{0,1:T(2,128)S(1)} %bitcast.64, f32[32,32]{1,0:T(8,128)S(1)} %convolution_bitcast_fusion.6, f32[32,32]{1,0:T(8,128)S(1)} %convolution_bitcast_fusion.4), channel_id=1, replica_groups=mesh['wide'=64,'narrow'=8] {'wide'}, use_global_device_ids=true, to_apply=%region_8.0 | all-reduce | flops 2112 | bytes 16896 | tf_op jit(solution)/shard_map/psum | solution.py:76
  1044.6 0.2 convolution_bitcast_fusion.5
  1045.0 0.8 multiply_reduce_fusion.7
  1045.7 60.0 %all-reduce.5 = (f32[32,32]{1,0:T(8,128)S(1)}, f32[]{:T(128)}, f32[]{:T(128)}) all-reduce(f32[32,32]{1,0:T(8,128)S(1)} %convolution_bitcast_fusion.5, f32[]{:T(128)} %get-tuple-element.8, f32[]{:T(128)} %get-tuple-element.7), channel_id=1, replica_groups=mesh['wide'=64,'narrow'=8] {'narrow'}, use_global_device_ids=true, to_apply=%region_12.0 | all-reduce | flops 1026 | bytes 8208 | tf_op jit(solution)/shard_map/psum | solution.py:40
  1105.8 0.8 multiply_reduce_fusion.3
  1106.6 0.8 multiply_reduce_fusion.2
  1109.9 228.5 %all-reduce.1 = (f32[]{:T(128)}, f32[]{:T(128)}) all-reduce(f32[]{:T(128)S(6)} %add.140, f32[]{:T(128)S(6)} %add.148), channel_id=1, replica_groups=mesh['wide'=64,'narrow'=8] {'wide'}, use_global_device_ids=true, to_apply=%region_7.0 | all-reduce | flops 2 | bytes 16 | tf_op jit(solution)/shard_map/psum | solution.py:22
  1341.1 0.6 multiply_reduce_fusion.1
  1341.7 0.6 multiply_reduce_fusion
  1343.6 0.6 multiply_reduce_fusion.6
  1344.2 210.8 %psum.153 = f32[]{:T(128)} all-reduce(f32[]{:T(128)S(6)} %add.153), channel_id=1, replica_groups=mesh['wide'=64,'narrow'=8] {'wide'}, use_global_device_ids=true, to_apply=%region_21.0 | all-reduce | flops 1 | bytes 8 | tf_op jit(solution)/shard_map/psum | solution.py:22
  1555.0 38.4 %psum.154 = f32[]{:T(128)} all-reduce(f32[]{:T(128)} %multiply_reduce_fusion.6), channel_id=1, replica_groups=mesh['wide'=64,'narrow'=8] {'narrow'}, use_global_device_ids=true, to_apply=%region_23.0 | all-reduce | flops 1 | bytes 8 | tf_op jit(solution)/shard_map/psum | solution.py:22
  1595.4 0.2 convolution_bitcast_fusion.2
  1595.6 412.3 %all-reduce = (f32[32,32]{1,0:T(8,128)S(1)}, f32[32,32]{1,0:T(8,128)S(1)}) all-reduce(f32[32,32]{1,0:T(8,128)S(1)} %convolution_bitcast_fusion.3, f32[32,32]{1,0:T(8,128)S(1)} %convolution_bitcast_fusion.1), channel_id=1, replica_groups=mesh['wide'=64,'narrow'=8] {'wide'}, use_global_device_ids=true, to_apply=%region_24.0 | all-reduce | flops 2048 | bytes 16384 | tf_op jit(solution)/shard_map/psum | solution.py:39
  2008.0 0.8 fusion.11
  2008.8 62.2 %all-reduce.4 = (f32[32,32]{1,0:T(8,128)S(1)}, f32[]{:T(128)}) all-reduce(f32[32,32]{1,0:T(8,128)S(1)} %convolution_bitcast_fusion.2, f32[]{:T(128)} %fusion.11), channel_id=1, replica_groups=mesh['wide'=64,'narrow'=8] {'narrow'}, use_global_device_ids=true, to_apply=%region_25.0 | all-reduce | flops 1025 | bytes 8200 | tf_op jit(solution)/shard_map/psum | solution.py:40
  2071.0 0.7 fusion.9
  2071.7 0.7 fusion.10
  2073.7 228.4 %psum.158 = f32[]{:T(128)} all-reduce(f32[]{:T(128)S(6)} %add.164), channel_id=1, replica_groups=mesh['wide'=64,'narrow'=8] {'wide'}, use_global_device_ids=true, to_apply=%region_29.0 | all-reduce | flops 1 | bytes 8 | tf_op jit(solution)/shard_map/psum | solution.py:22
  2303.5 0.6 multiply_add_fusion.1
  2304.1 0.6 multiply_add_fusion
  2304.7 0.6 multiply_add_fusion.4
  (32 shorter events, 2.4 us)
Async XLA Ops:
  7.2 1.6 copy-start
  7.2 617.4 %all-reduce.9.cloned.1.call-start = ((), (), s32[]{:S(2)}) async-start(), calls=%async_computation | async-start | bytes 2097152 | tf_op jit(solution)/shard_map/psum | solution.py:83
  8.8 1.6 copy-start.3
  8.8 1.8 copy-start.1
  8.8 131.3 %copy-start.2 = (bf16[32,64]{1,0:T(8,128)(2,1)S(1)}, bf16[32,64]{1,0:T(8,128)(2,1)}, u32[]{:S(2)}) copy-start(bf16[32,64]{1,0:T(8,128)(2,1)} %param.5) | copy-start | bytes 12292
Sparse Core Ops, SparseCore 0:
  13.4 480.2 all-reduce.8
where the time goes:
time: 2310 us
  blocking collectives  2270 us (98%)
  between operations  24.6 us (1%)
    psum x2, blocking collectives, on_device(): lax.psum((part_c, own_gram_a, own_gram_b), 'wide')  834 us
    psum x4, blocking collectives, combine_dot(): return lax.psum(wide_part, 'wide') + lax.psum(narrow_part, 'narrow')  706 us
    psum x1, blocking collectives, gram_product(): cross_a, cross_b = lax.psum((local_a, local_b), 'wide')  412 us
    all_gather x1, blocking collectives, on_device(): lax.all_gather(factor_b, 'wide', axis=1, tiled=True)  129 us
    psum x2, blocking collectives, gram_product(): cross_c = lax.psum(local_c, 'narrow')  122 us
    psum x1, blocking collectives, on_device(): mttkrp_a, gram_c = lax.psum((part_a, own_gram_c), 'narrow')  66.7 us
  transfers between devices with their start and end apart: 1, of which 0 were waited for; matrix products, arithmetic and copies ran while one was open for 0% of the time, Pallas kernels for 0%

commit v1 on v0

v1 whole, which is shorter than its diff:
```python
import functools

import jax
import jax.numpy as jnp
from jax import lax
from jax.experimental import pallas as pl
from jax.experimental.pallas import tpu as pltpu
from jax.sharding import Mesh
from jax.sharding import PartitionSpec as P

f32 = jnp.float32
bf16 = jnp.bfloat16
LANES = 128
damping = 1.0
highest = lax.Precision.HIGHEST

WIDE = (4, 8, 2)
NARROW = (4, 2)
LINKS = ("y", "z_lo")
OTHER = ("x", "z_hi")


def mul(left, right):
    return jnp.dot(left, right, precision=highest, preferred_element_type=f32)


def mul_t(left, right):
    return lax.dot_general(
        left, right, (((1,), (1,)), ((), ())), precision=highest, preferred_element_type=f32
    )


def t_mul(left, right):
    return lax.dot_general(
        left, right, (((0,), (0,)), ((), ())), precision=highest, preferred_element_type=f32
    )


def lane(rows, width):
    return lax.broadcasted_iota(jnp.int32, (rows, width), 1)


def columns_of(row_block):
    count, rank = row_block.shape
    eye = lax.broadcasted_iota(jnp.int32, (rank, rank), 0) == lane(rank, rank)
    return [
        jnp.sum(jnp.where(eye, row_block[k : k + 1, :], 0.0), axis=1, keepdims=True)
        for k in range(count)
    ]


def partial_b_kernel(peers, t_ref, a_ref, ct_ref, out_ref):
    rank, i_local = a_ref.shape
    factor_a = a_ref[...]
    float_a = factor_a.astype(f32)
    cols = columns_of(ct_ref[...].astype(f32))
    khatri = jnp.concatenate([col * float_a for col in cols], axis=1).astype(bf16)
    per = 8
    for base in range(0, 2 * peers, per):
        part = jnp.dot(
            khatri, t_ref[:, base * LANES : (base + per) * LANES], preferred_element_type=f32
        )
        for step in range(per):
            peer, core = divmod(base + step, 2)
            out_ref[core, peer * rank : (peer + 1) * rank, :] = part[
                :, step * LANES : (step + 1) * LANES
            ]
    gram_a = lax.dot_general(
        factor_a, factor_a, (((1,), (1,)), ((), ())), preferred_element_type=f32
    )
    half = rank // 2
    pad = jnp.zeros((half, LANES - rank), f32)
    for core in range(2):
        out_ref[core, peers * rank :, :] = jnp.concatenate(
            [gram_a[core * half : (core + 1) * half, :], pad], axis=1
        )


def send_links_kernel(peers, pair_ref, b_ref, out_ref):
    rank = b_ref.shape[0]
    half = rank // 2
    quarter = half // 2
    own_b = b_ref[...]
    gram = pair_ref[0, peers * rank :, :rank] + pair_ref[1, peers * rank :, :rank]
    high = gram.astype(bf16)
    low = (gram - high.astype(f32)).astype(bf16)
    packed = jnp.concatenate(
        [high[:quarter].astype(f32), low[:quarter].astype(f32), high[quarter:].astype(f32), low[quarter:].astype(f32)],
        axis=1,
    ).astype(bf16)
    for peer in range(peers):
        rows = pl.ds(peer * rank, rank)
        out_ref[peer, :rank, :] = (pair_ref[0, rows, :] + pair_ref[1, rows, :]).astype(bf16)
        out_ref[peer, rank : 2 * rank, :] = own_b
        out_ref[peer, 2 * rank :, :] = packed


def partials_kernel(peers, others, n_ref, t_ref, a_ref, ct_ref, got_ref, both_ref, out_ref, grams_ref, whole_b):
    rank, i_local = a_ref.shape
    quarter = rank // 4
    sum_b = jnp.zeros((rank, LANES), f32)
    for peer in range(peers):
        sum_b = sum_b + got_ref[peer, :rank, :].astype(f32)
    for core in range(2):
        for peer in range(peers):
            start = (peer * 2 + core) * LANES
            whole_b[:, start : start + LANES] = both_ref[core, peer, :rank, :]
    gram_rows = []
    for core in range(2):
        packed = jnp.zeros((quarter, LANES), f32)
        for peer in range(peers):
            packed = packed + both_ref[core, peer, rank:, :].astype(f32)
        gram_rows.append(packed[:, :rank] + packed[:, rank : 2 * rank])
        gram_rows.append(packed[:, 2 * rank : 3 * rank] + packed[:, 3 * rank :])
    gram_a = jnp.concatenate(gram_rows, axis=0)
    every_b = whole_b[...]
    contracted = lax.dot_general(
        every_b, t_ref[...], (((1,), (1,)), ((), ())), preferred_element_type=f32
    )
    gram_b = lax.dot_general(
        every_b, every_b, (((1,), (1,)), ((), ())), preferred_element_type=f32
    )
    grams_ref[0] = gram_a
    grams_ref[1] = gram_b
    first, second = columns_of(ct_ref[...].astype(f32))
    float_a = a_ref[...].astype(f32)
    spot = lane(rank, LANES)
    low_half = spot < i_local
    scaled = contracted * jnp.where(low_half, first, second)
    part_a = scaled + pltpu.roll(scaled, i_local, 1)
    against_a = contracted * jnp.concatenate([float_a, float_a], axis=1)
    c_first = jnp.sum(jnp.where(low_half, against_a, 0.0), axis=1, keepdims=True)
    c_second = jnp.sum(jnp.where(low_half, 0.0, against_a), axis=1, keepdims=True)
    at = i_local + 2 * n_ref[0]
    k_all = 2 * others
    tail = jnp.where(spot == at, c_first, 0.0)
    tail = jnp.where(spot == at + 1, c_second, tail)
    tail = jnp.where(spot == at + k_all, first, tail)
    tail = jnp.where(spot == at + k_all + 1, second, tail)
    second_tile = jnp.where(low_half, part_a, tail)
    for other in range(others):
        out_ref[other, :, :LANES] = sum_b
        out_ref[other, :, LANES:] = second_tile


def residual_kernel(others, got_ref, a_ref, b_ref, grams_ref, send_ref, ra_ref, rb_ref, ha_ref, hb_ref, c_ref):
    rank, i_local = a_ref.shape
    k_all = 2 * others
    total = got_ref[0]
    for other in range(1, others):
        total = total + got_ref[other]
    mttkrp_b = total[:, :LANES]
    mttkrp_a = total[:, LANES : LANES + i_local]
    part_c = total[:, LANES + i_local : LANES + i_local + k_all]
    factor_c = total[:, LANES + i_local + k_all : LANES + i_local + 2 * k_all]
    c_ref[...] = factor_c
    gram_a = grams_ref[0]
    gram_b = grams_ref[1]
    gram_c = mul_t(factor_c, factor_c)
    had_a = gram_b * gram_c
    had_b = gram_a * gram_c
    float_a = a_ref[...].astype(f32)
    float_b = b_ref[...].astype(f32)
    res_a = mttkrp_a - mul(had_a, float_a)
    res_b = mttkrp_b - mul(had_b, float_b)
    once_a = mul(had_a, res_a)
    once_b = mul(had_b, res_b)
    twice_a = mul(had_a, once_a)
    twice_b = mul(had_b, once_b)
    ra_ref[...] = res_a
    rb_ref[...] = res_b
    ha_ref[...] = once_a
    hb_ref[...] = once_b

    def inner(left_a, right_a, left_b, right_b):
        by_row = jnp.sum(left_a * right_a, axis=1, keepdims=True) + jnp.sum(
            left_b * right_b, axis=1, keepdims=True
        )
        return by_row

    sums = [
        inner(res_a, res_a, res_b, res_b),
        inner(res_a, once_a, res_b, once_b),
        inner(once_a, once_a, once_b, once_b),
        inner(once_a, twice_a, once_b, twice_b),
    ]
    cross_a = mul_t(float_a, res_a)
    cross_b = mul_t(float_b, res_b)
    used = 2 * rank + k_all
    base = jnp.concatenate(
        [cross_a, cross_b, part_c, jnp.zeros((rank, LANES - used), f32)], axis=1
    )
    spot = lane(rank, LANES)
    for k, value in enumerate(sums):
        base = jnp.where(spot == used + k, value, base)
    send_ref[...] = base


def step_kernel(others, n_ref, all_ref, a_ref, b_ref, grams_ref, ra_ref, rb_ref, ha_ref, hb_ref, c_ref, sa_ref, sb_ref, sc_ref):
    rank, i_local = a_ref.shape
    k_all = 2 * others
    used = 2 * rank + k_all
    every = all_ref[...]
    cross_a = every[:, :rank]
    cross_b = every[:, rank : 2 * rank]
    mttkrp_c = every[:, 2 * rank : used]
    gram_a = grams_ref[0]
    gram_b = grams_ref[1]
    factor_c = c_ref[...]
    gram_c = mul_t(factor_c, factor_c)
    had_a = gram_b * gram_c
    had_b = gram_a * gram_c
    had_c = gram_a * gram_b
    res_c = mttkrp_c - mul(had_c, factor_c)
    once_c = mul(had_c, res_c)
    twice_c = mul(had_c, once_c)
    cross_c = mul_t(factor_c, res_c)

    def total(value):
        return jnp.sum(jnp.sum(value, axis=1, keepdims=True), axis=0, keepdims=True)

    own = [
        total(res_c * res_c),
        total(res_c * once_c),
        total(once_c * once_c),
        total(once_c * twice_c),
    ]
    p0, p1, p2, p3 = [
        total(every[:, used + k : used + k + 1]) + own[k] for k in range(4)
    ]

    def mixed(xa, xb, xc):
        return (
            xb * gram_c + gram_b * xc,
            xa * gram_c + gram_a * xc,
            xa * gram_b + gram_a * xb,
        )

    eye = (
        lax.broadcasted_iota(jnp.int32, (rank, rank), 0) == lane(rank, rank)
    ).astype(f32)
    grams = (gram_a, gram_b, gram_c)
    shifted = tuple(had + damping * eye for had in (had_a, had_b, had_c))
    crosses = (cross_a, cross_b, cross_c)
    mix = mixed(*crosses)
    mix_gram = [mul(m, g) for m, g in zip(mix, grams)]
    turned = [mul_t(s, x) for s, x in zip(shifted, crosses)]
    twice_turned = [mul(s, t) for s, t in zip(shifted, turned)]
    shifted_mix = [mul(s, m) for s, m in zip(shifted, mix)]
    image_cross_t = [t + mg for t, mg in zip(turned, mix_gram)]
    image_cross = [
        mul(x, s) + mul_t(g, m) for x, s, g, m in zip(crosses, shifted, grams, mix)
    ]
    image_mix = mixed(*image_cross)
    one = damping
    c0 = p0
    k1 = p1 + one * p0
    k2 = p2 + 2.0 * one * p1 + one * one * p0
    k3 = p3 + 3.0 * one * p2 + 3.0 * one * one * p1 + one * one * one * p0
    c1 = k1
    c2 = k2
    c3 = k3
    crosses_t = [mul_t(eye, x) for x in crosses]
    c1 = c1 + total(sum(m * xt for m, xt in zip(mix, crosses_t)))
    c2 = c2 + total(
        sum(2.0 * m * t + mg * m for m, t, mg in zip(mix, turned, mix_gram))
    )
    c3 = c3 + total(
        sum(
            2.0 * m * tt + mg * sm + im * ict
            for m, tt, mg, sm, im, ict in zip(
                mix, twice_turned, mix_gram, shifted_mix, image_mix, image_cross_t
            )
        )
    )
    alpha = c0 / c1
    fresh = c0 - 2.0 * alpha * c1 + alpha * alpha * c2
    beta = fresh / c0
    keep = 1.0 + beta
    curvature = keep * keep * c1 - 2.0 * keep * alpha * c2 + alpha * alpha * c3
    second = fresh / curvature
    on_res = alpha + second * keep
    on_image = -second * alpha
    float_a = a_ref[...].astype(f32)
    float_b = b_ref[...].astype(f32)
    res_a = ra_ref[...]
    res_b = rb_ref[...]
    image_a = damping * res_a + ha_ref[...] + mul(mix[0], float_a)
    image_b = damping * res_b + hb_ref[...] + mul(mix[1], float_b)
    image_c = damping * res_c + once_c + mul(mix[2], factor_c)
    sa_ref[...] = on_res * res_a + on_image * image_a
    sb_ref[...] = on_res * res_b + on_image * image_b
    step_c = on_res * res_c + on_image * image_c
    at = 2 * n_ref[0]
    spot = lane(rank, k_all)
    square = lax.broadcasted_iota(jnp.int32, (rank, rank), 0) == lane(rank, rank)
    for k in range(2):
        column = jnp.sum(jnp.where(spot == at + k, step_c, 0.0), axis=1, keepdims=True)
        sc_ref[k : k + 1, :] = jnp.sum(jnp.where(square, column, 0.0), axis=0, keepdims=True)


def call(kernel, out_shape, operands, scalar=False, scratch=()):
    vmem = pl.BlockSpec(memory_space=pltpu.VMEM)
    specs = [vmem] * len(operands)
    if scalar:
        specs[0] = pl.BlockSpec(memory_space=pltpu.SMEM)
    outs = out_shape if isinstance(out_shape, tuple) else (out_shape,)
    result = pl.pallas_call(
        kernel,
        out_shape=outs,
        in_specs=specs,
        out_specs=tuple(vmem for _ in outs),
        scratch_shapes=list(scratch),
    )(*operands)
    return result if isinstance(out_shape, tuple) else result[0]


def on_device(tensor, factor_a, factor_b, factor_c):
    k_local, i_local, j_whole = tensor.shape
    rank = factor_a.shape[0]
    peers = j_whole // (2 * LANES)
    others = lax.axis_size(OTHER)
    like = jax.ShapeDtypeStruct
    flattened = tensor.reshape(k_local * i_local, j_whole)
    turned_c = factor_c.T
    own = lax.axis_index(OTHER).astype(jnp.int32).reshape(1)
    half = rank // 2

    pair = call(
        functools.partial(partial_b_kernel, peers),
        like((2, peers * rank + half, LANES), f32),
        (flattened, factor_a, turned_c),
    )
    pair = lax.all_to_all(pair, "core", 0, 0, tiled=True)
    links = call(
        functools.partial(send_links_kernel, peers),
        like((peers, 2 * rank + rank // 4, LANES), bf16),
        (pair, factor_b),
    )
    links = lax.all_to_all(links, LINKS, 0, 0, tiled=True)
    both = lax.all_gather(links[:, rank:, :], "core", axis=0, tiled=False)
    narrow, grams = call(
        functools.partial(partials_kernel, peers, others),
        (like((others, rank, 2 * LANES), f32), like((2, rank, rank), f32)),
        (own, flattened, factor_a, turned_c, links, both),
        scalar=True,
        scratch=(pltpu.VMEM((rank, j_whole), bf16),),
    )
    narrow = lax.all_to_all(narrow, OTHER, 0, 0, tiled=True)
    square = like((rank, LANES), f32)
    thin = like((rank, i_local), f32)
    send, res_a, res_b, once_a, once_b, whole_c = call(
        functools.partial(residual_kernel, others),
        (square, thin, square, thin, square, like((rank, 2 * others), f32)),
        (narrow, factor_a, factor_b, grams),
    )
    send = lax.psum(send, "core")
    send = lax.dynamic_slice_in_dim(send, lax.axis_index("core") * half, half, 0)
    send = jnp.broadcast_to(send, (peers, half, LANES))
    send = lax.all_to_all(send, LINKS, 0, 0, tiled=True)
    every = lax.all_gather(jnp.sum(send, axis=0), "core", axis=0, tiled=True)
    step_a, step_b, turned_step_c = call(
        functools.partial(step_kernel, others),
        (thin, square, like((k_local, rank), f32)),
        (own, every, factor_a, factor_b, grams, res_a, res_b, once_a, once_b, whole_c),
        scalar=True,
    )
    return step_a, step_b, turned_step_c.T


def solution(mesh):
    inner = Mesh(
        mesh.devices.reshape(WIDE + NARROW), ("y", "z_lo", "core", "x", "z_hi")
    )
    wide = ("y", "z_lo", "core")
    return jax.shard_map(
        on_device,
        mesh=inner,
        in_specs=(P(OTHER, wide, None), P(None, wide), P(None, wide), P(None, OTHER)),
        out_specs=(P(None, wide), P(None, wide), P(None, OTHER)),
        check_vma=False,
    )
```

time: 2310 us -> 140 us (0.06)
  blocking collectives: 2270 us -> 55.9 us
  waiting for transfers between devices: 0.04 us -> 47.6 us
  between operations: 24.6 us -> 0.66 us
    psum x10 -> x1, blocking collectives: 2140 us -> 5.43 us  [on_device(): send = lax.psum(send, 'core')]
    all_gather x1 -> x2, blocking collectives: 129 us -> 6.93 us  [the longest x1 3.73 us: on_device(): both = lax.all_gather(links[:, rank:, :], 'core', axis=0, tiled=False)]
    all_to_all x0 -> x2, waiting for transfers between devices: none -> 47.6 us  [the longest x1 32 us: on_device(): links = lax.all_to_all(links, LINKS, 0, 0, tiled=True)]
    all_to_all x0 -> x2, blocking collectives: none -> 43.5 us  [the longest x1 30.5 us: on_device(): send = lax.all_to_all(send, LINKS, 0, 0, tiled=True)]
  transfers between devices with their start and end apart: 1 -> 2, of which waited for: 0 -> 2; matrix products, arithmetic and copies ran while one was open for 0% -> 0% of each run, Pallas kernels for 0% -> 0%
where the time goes in v1:
time: 140 us
  blocking collectives  55.9 us (40%)
  waiting for transfers between devices  47.6 us (34%)
  starting transfers between devices  19.7 us (14%)
  Pallas kernels  15 us (11%)
    all_to_all x1, waiting for transfers between devices, on_device(): links = lax.all_to_all(links, LINKS, 0, 0, tiled=True)  32 us
    all_to_all x1, blocking collectives, on_device(): send = lax.all_to_all(send, LINKS, 0, 0, tiled=True)  30.5 us
    all_to_all x1, waiting for transfers between devices, on_device(): narrow = lax.all_to_all(narrow, OTHER, 0, 0, tiled=True)  15.6 us
    pallas_call x5, Pallas kernels, call(): pl.pallas_call(kernel, out_shape=outs, in_specs=specs, out_specs=tuple((v...  15 us
    all_to_all x1, blocking collectives, on_device(): pair = lax.all_to_all(pair, 'core', 0, 0, tiled=True)  13 us
    all_to_all x1, starting transfers between devices, on_device(): links = lax.all_to_all(links, LINKS, 0, 0, tiled=True)  9.92 us
    all_to_all x1, starting transfers between devices, on_device(): narrow = lax.all_to_all(narrow, OTHER, 0, 0, tiled=True)  9.77 us
    psum x1, blocking collectives, on_device(): send = lax.psum(send, 'core')  5.43 us
  transfers between devices with their start and end apart: 2, of which 2 were waited for; matrix products, arithmetic and copies ran while one was open for 0% of the time, Pallas kernels for 0%

profile of v1, /device:TPU:1, one launch (start us, length us, event | category | flops | bytes accessed | tf_op | source)
XLA Modules:
  0.0 139.7 jit_solution(12966522371839902945)
XLA Ops:
  0.6 3.2 %shard_map.67 = f32[2,1040,128]{2,1,0:T(8,128)} custom-call(bf16[128,8192]{1,0:T(8,128)(2,1)} %bitcast.5, bf16[32,64]{1,0:T(8,128)(2,1)} %a_ref.7, bf16[2,32]{1,0:T(2,128)(2,1)} %bitcast.8), custom_call_target="tpu_custom_call" | custom-call | tf_op jit(solution)/shard_map/pallas_call | solution.py:308
  3.8 13.0 %all_to_all.20.pair_ref = f32[2,1040,128]{2,1,0:T(8,128)} all-to-all(f32[2,1040,128]{2,1,0:T(8,128)} %shard_map.67), channel_id=1, replica_groups=mesh['y'=4,'z_lo'=8,'core'=2,'x'=4,'z_hi'=2] {'core'}, dimensions={0} | all-to-all | bytes 2129920 | tf_op jit(solution)/shard_map/all_to_all | solution.py:334
  16.9 2.1 %shard_map.68 = bf16[32,72,128]{2,1,0:T(8,128)(2,1)} custom-call(f32[2,1040,128]{2,1,0:T(8,128)} %all_to_all.20.pair_ref, bf16[32,128]{1,0:T(8,128)(2,1)} %b_ref.5), custom_call_target="tpu_custom_call" | custom-call | tf_op jit(solution)/shard_map/pallas_call | solution.py:308
  19.0 9.9 %all-to-all-start.1 = ((bf16[32,72,128]{2,1,0:T(8,128)(2,1)}), bf16[32,72,128]{2,1,0:T(8,128)(2,1)S(1)}, u32[]{:S(2)}, u32[]{:S(2)}) async-start(bf16[32,72,128]{2,1,0:T(8,128)(2,1)} %shard_map.68), calls=%async_computation.1 | async-start | bytes 1179648 | tf_op jit(solution)/shard_map/all_to_all | solution.py:340
  29.0 32.0 %all-to-all-done.1.got_ref = bf16[32,72,128]{2,1,0:T(8,128)(2,1)S(1)} async-done(((bf16[32,72,128]{2,1,0:T(8,128)(2,1)}), bf16[32,72,128]{2,1,0:T(8,128)(2,1)S(1)}, u32[]{:S(2)}, u32[]{:S(2)}) %all-to-all-start.1) | async-done | bytes 589856 | tf_op jit(solution)/shard_map/all_to_all | solution.py:340
  61.0 0.0 copy-start
  61.0 3.7 %all-gather = bf16[64,40,128]{2,1,0:T(8,128)(2,1)} all-gather(bf16[32,40,128]{2,1,0:T(8,128)(2,1)S(1)} %slice.4), channel_id=2, replica_groups=mesh['y'=4,'z_lo'=8,'core'=2,'x'=4,'z_hi'=2] {'core'}, dimensions={0}, use_global_device_ids=true | all-gather | bytes 983040 | tf_op jit(solution)/shard_map/all_gather | solution.py:341
  64.7 0.0 copy-done
  64.7 3.7 %shard_map.69 = (f32[8,32,256]{2,1,0:T(8,128)}, f32[2,32,32]{2,1,0:T(8,128)}) custom-call(s32[1]{0:T(128)} %bitcast.n_ref, bf16[128,8192]{1,0:T(8,128)(2,1)} %bitcast.6, bf16[32,64]{1,0:T(8,128)(2,1)} %a_ref.7, bf16[2,32]{1,0:T(2,128)(2,1)} %bitcast.9, bf16[32,72,128]{2,1,0:T(8,128)(2,1)} %copy-done, bf16[2,32,40,128]{3,2,1,0:T(8,128)(2,1)} %bitcast.7), custom_call_target="tpu_custom_call" | custom-call | tf_op jit(solution)/shard_map/pallas_call | solution.py:308
  68.5 9.8 %all-to-all-start.2 = ((f32[8,32,256]{2,1,0:T(8,128)}), f32[8,32,256]{2,1,0:T(8,128)S(1)}, u32[]{:S(2)}, u32[]{:S(2)}) async-start(f32[8,32,256]{2,1,0:T(8,128)} %get-tuple-element.14), calls=%async_computation.2 | async-start | bytes 524288 | tf_op jit(solution)/shard_map/all_to_all | solution.py:349
  78.2 15.6 %all-to-all-done.2.got_ref = f32[8,32,256]{2,1,0:T(8,128)S(1)} async-done(((f32[8,32,256]{2,1,0:T(8,128)}), f32[8,32,256]{2,1,0:T(8,128)S(1)}, u32[]{:S(2)}, u32[]{:S(2)}) %all-to-all-start.2) | async-done | bytes 262176 | tf_op jit(solution)/shard_map/all_to_all | solution.py:349
  93.9 0.0 copy-start.1
  93.9 0.7 copy-done.1
  94.6 2.5 %shard_map.70 = (f32[32,128]{1,0:T(8,128)}, f32[32,64]{1,0:T(8,128)}, f32[32,128]{1,0:T(8,128)}, f32[32,64]{1,0:T(8,128)}, f32[32,128]{1,0:T(8,128)}, /*index=5*/f32[32,16]{1,0:T(8,128)}) custom-call(f32[8,32,256]{2,1,0:T(8,128)} %copy-done.1, bf16[32,64]{1,0:T(8,128)(2,1)} %a_ref.7, bf16[32,128]{1,0:T(8,128)(2,1)} %b_ref.5, ...), custom_call_target="tpu_custom_call" | custom-call | tf_op jit(solution)/shard_map/pallas_call | solution.py:308
  97.0 5.4 %psum.7 = f32[32,128]{1,0:T(8,128)S(1)} all-reduce(f32[32,128]{1,0:T(8,128)} %get-tuple-element.16), channel_id=1, replica_groups=mesh['y'=4,'z_lo'=8,'core'=2,'x'=4,'z_hi'=2] {'core'}, use_global_device_ids=true, to_apply=%region_0.0 | all-reduce | flops 4096 | bytes 32768 | tf_op jit(solution)/shard_map/psum | solution.py:357
  102.5 30.5 %all_to_all.21 = f32[32,16,128]{2,1,0:T(8,128)S(1)} all-to-all(f32[32,16,128]{2,1,0:T(8,128)S(1)} %broadcast_in_dim.3), channel_id=1, replica_groups=mesh['y'=4,'z_lo'=8,'core'=2,'x'=4,'z_hi'=2] {'y','z_lo'}, dimensions={0} | all-to-all | bytes 524288 | tf_op jit(solution)/shard_map/all_to_all | solution.py:360
  133.0 3.2 %all_gather.11.all_ref = f32[32,128]{1,0:T(8,128)} all-gather(f32[16,128]{1,0:T(8,128)S(1)} %reduce_sum.9), channel_id=1, replica_groups=mesh['y'=4,'z_lo'=8,'core'=2,'x'=4,'z_hi'=2] {'core'}, dimensions={0}, use_global_device_ids=true | all-gather | bytes 24576 | tf_op jit(solution)/shard_map/all_gather | solution.py:361
  136.2 3.5 %shard_map.71 = (f32[32,64]{1,0:T(8,128)}, f32[32,128]{1,0:T(8,128)}, f32[2,32]{1,0:T(2,128)}) custom-call(s32[1]{0:T(128)} %bitcast.n_ref, f32[32,128]{1,0:T(8,128)} %all_gather.11.all_ref, bf16[32,64]{1,0:T(8,128)(2,1)} %a_ref.7, bf16[32,128]{1,0:T(8,128)(2,1)} %b_ref.5, f32[2,32,32]{2,1,0:T(8,128)} %get-tuple-element.15.grams_ref, ...), custom_call_target="tpu_custom_call" | custom-call | tf_op jit(solution)/shard_map/pallas_call | solution.py:308
  (4 shorter events, 0.1 us)
Async XLA Ops:
  19.0 41.9 %all-to-all-start.1 = ((bf16[32,72,128]{2,1,0:T(8,128)(2,1)}), bf16[32,72,128]{2,1,0:T(8,128)(2,1)S(1)}, u32[]{:S(2)}, u32[]{:S(2)}) async-start(bf16[32,72,128]{2,1,0:T(8,128)(2,1)} %shard_map.68), calls=%async_computation.1 | async-start | bytes 1179648 | tf_op jit(solution)/shard_map/all_to_all | solution.py:340
  61.0 3.8 %copy-start = (bf16[32,72,128]{2,1,0:T(8,128)(2,1)}, bf16[32,72,128]{2,1,0:T(8,128)(2,1)S(1)}, u32[]{:S(2)}) copy-start(bf16[32,72,128]{2,1,0:T(8,128)(2,1)S(1)} %all-to-all-done.1.got_ref) | copy-start | bytes 1769476
  68.5 25.4 %all-to-all-start.2 = ((f32[8,32,256]{2,1,0:T(8,128)}), f32[8,32,256]{2,1,0:T(8,128)S(1)}, u32[]{:S(2)}, u32[]{:S(2)}) async-start(f32[8,32,256]{2,1,0:T(8,128)} %get-tuple-element.14), calls=%async_computation.2 | async-start | bytes 524288 | tf_op jit(solution)/shard_map/all_to_all | solution.py:349
  93.9 0.7 copy-start.1

commit v2 on v1

--- a/solution.py
+++ b/solution.py
@@ -49,79 +49,89 @@
     ]
 
 
-def partial_b_kernel(peers, t_ref, a_ref, ct_ref, out_ref):
+def spread(square):
+    rows = square.shape[0] // 4
+    return jnp.concatenate([square[k * rows : (k + 1) * rows, :] for k in range(4)], axis=1)
+
+
+def gather_rows(wide_block):
+    width = wide_block.shape[1] // 4
+    return jnp.concatenate([wide_block[:, k * width : (k + 1) * width] for k in range(4)], axis=0)
+
+
+def partial_b_kernel(peers, place_ref, t_ref, a_ref, ct_ref, keep_ref, send_ref):
     rank, i_local = a_ref.shape
+    half = rank // 2
     factor_a = a_ref[...]
     float_a = factor_a.astype(f32)
     cols = columns_of(ct_ref[...].astype(f32))
     khatri = jnp.concatenate([col * float_a for col in cols], axis=1).astype(bf16)
+    first_core = place_ref[0] % 2 == 0
+
+    def put(rows, even, odd):
+        keep_ref[rows, :] = jnp.where(first_core, even, odd)
+        send_ref[rows, :] = jnp.where(first_core, odd, even)
+
     per = 8
     for base in range(0, 2 * peers, per):
         part = jnp.dot(
             khatri, t_ref[:, base * LANES : (base + per) * LANES], preferred_element_type=f32
         )
-        for step in range(per):
-            peer, core = divmod(base + step, 2)
-            out_ref[core, peer * rank : (peer + 1) * rank, :] = part[
-                :, step * LANES : (step + 1) * LANES
-            ]
-    gram_a = lax.dot_general(
+        for step in range(0, per, 2):
+            peer = (base + step) // 2
+            put(
+                pl.ds(peer * rank, rank),
+                part[:, step * LANES : (step + 1) * LANES],
+                part[:, (step + 1) * LANES : (step + 2) * LANES],
+            )
+    gram = lax.dot_general(
         factor_a, factor_a, (((1,), (1,)), ((), ())), preferred_element_type=f32
     )
-    half = rank // 2
-    pad = jnp.zeros((half, LANES - rank), f32)
-    for core in range(2):
-        out_ref[core, peers * rank :, :] = jnp.concatenate(
-            [gram_a[core * half : (core + 1) * half, :], pad], axis=1
-        )
-
-
-def send_links_kernel(peers, pair_ref, b_ref, out_ref):
+    gram = jnp.concatenate([gram, jnp.zeros((rank, LANES - rank), f32)], axis=1)
+    put(pl.ds(peers * rank, half), gram[:half], gram[half:])
+
+
+def send_links_kernel(peers, keep_ref, came_ref, b_ref, out_ref):
     rank = b_ref.shape[0]
-    half = rank // 2
-    quarter = half // 2
+    quarter = rank // 4
     own_b = b_ref[...]
-    gram = pair_ref[0, peers * rank :, :rank] + pair_ref[1, peers * rank :, :rank]
-    high = gram.astype(bf16)
-    low = (gram - high.astype(f32)).astype(bf16)
+    last = pl.ds(peers * rank, 2 * quarter)
+    gram = keep_ref[last, :rank] + came_ref[last, :rank]
+    high = gram.astype(bf16).astype(f32)
+    low = gram - high
     packed = jnp.concatenate(
-        [high[:quarter].astype(f32), low[:quarter].astype(f32), high[quarter:].astype(f32), low[quarter:].astype(f32)],
-        axis=1,
+        [high[:quarter], low[:quarter], high[quarter:], low[quarter:]], axis=1
     ).astype(bf16)
     for peer in range(peers):
         rows = pl.ds(peer * rank, rank)
-        out_ref[peer, :rank, :] = (pair_ref[0, rows, :] + pair_ref[1, rows, :]).astype(bf16)
+        out_ref[peer, :rank, :] = (keep_ref[rows, :] + came_ref[rows, :]).astype(bf16)
         out_ref[peer, rank : 2 * rank, :] = own_b
         out_ref[peer, 2 * rank :, :] = packed
 
 
-def partials_kernel(peers, others, n_ref, t_ref, a_ref, ct_ref, got_ref, both_ref, out_ref, grams_ref, whole_b):
+def partials_kernel(peers, others, place_ref, t_ref, a_ref, ct_ref, got_ref, both_ref, out_ref, grams_ref, whole_b):
     rank, i_local = a_ref.shape
     quarter = rank // 4
-    sum_b = jnp.zeros((rank, LANES), f32)
-    for peer in range(peers):
+    sum_b = got_ref[0, :rank, :].astype(f32)
+    for peer in range(1, peers):
         sum_b = sum_b + got_ref[peer, :rank, :].astype(f32)
-    for core in range(2):
-        for peer in range(peers):
-            start = (peer * 2 + core) * LANES
-            whole_b[:, start : start + LANES] = both_ref[core, peer, :rank, :]
     gram_rows = []
     for core in range(2):
         packed = jnp.zeros((quarter, LANES), f32)
         for peer in range(peers):
+            start = (peer * 2 + core) * LANES
+            whole_b[:, start : start + LANES] = both_ref[core, peer, :rank, :]
             packed = packed + both_ref[core, peer, rank:, :].astype(f32)
         gram_rows.append(packed[:, :rank] + packed[:, rank : 2 * rank])
         gram_rows.append(packed[:, 2 * rank : 3 * rank] + packed[:, 3 * rank :])
-    gram_a = jnp.concatenate(gram_rows, axis=0)
     every_b = whole_b[...]
     contracted = lax.dot_general(
         every_b, t_ref[...], (((1,), (1,)), ((), ())), preferred_element_type=f32
     )
-    gram_b = lax.dot_general(
+    grams_ref[0] = jnp.concatenate(gram_rows, axis=0)
+    grams_ref[1] = lax.dot_general(
         every_b, every_b, (((1,), (1,)), ((), ())), preferred_element_type=f32
     )
-    grams_ref[0] = gram_a
-    grams_ref[1] = gram_b
     first, second = columns_of(ct_ref[...].astype(f32))
     float_a = a_ref[...].astype(f32)
     spot = lane(rank, LANES)
@@ -131,19 +141,19 @@
     against_a = contracted * jnp.concatenate([float_a, float_a], axis=1)
     c_first = jnp.sum(jnp.where(low_half, against_a, 0.0), axis=1, keepdims=True)
     c_second = jnp.sum(jnp.where(low_half, 0.0, against_a), axis=1, keepdims=True)
-    at = i_local + 2 * n_ref[0]
+    at = i_local + 2 * (place_ref[0] // 2)
     k_all = 2 * others
     tail = jnp.where(spot == at, c_first, 0.0)
     tail = jnp.where(spot == at + 1, c_second, tail)
     tail = jnp.where(spot == at + k_all, first, tail)
     tail = jnp.where(spot == at + k_all + 1, second, tail)
-    second_tile = jnp.where(low_half, part_a, tail)
+    tile = jnp.where(low_half, part_a, tail)
     for other in range(others):
         out_ref[other, :, :LANES] = sum_b
-        out_ref[other, :, LANES:] = second_tile
-
-
-def residual_kernel(others, got_ref, a_ref, b_ref, grams_ref, send_ref, ra_ref, rb_ref, ha_ref, hb_ref, c_ref):
+        out_ref[other, :, LANES:] = tile
+
+
+def residual_kernel(others, place_ref, got_ref, a_ref, b_ref, grams_ref, send_ref, second_ref, ra_ref, rb_ref, ha_ref, hb_ref, c_ref):
     rank, i_local = a_ref.shape
     k_all = 2 * others
     total = got_ref[0]
@@ -186,24 +196,22 @@
     ]
     cross_a = mul_t(float_a, res_a)
     cross_b = mul_t(float_b, res_b)
-    used = 2 * rank + k_all
-    base = jnp.concatenate(
-        [cross_a, cross_b, part_c, jnp.zeros((rank, LANES - used), f32)], axis=1
-    )
-    spot = lane(rank, LANES)
-    for k, value in enumerate(sums):
-        base = jnp.where(spot == used + k, value, base)
-    send_ref[...] = base
-
-
-def step_kernel(others, n_ref, all_ref, a_ref, b_ref, grams_ref, ra_ref, rb_ref, ha_ref, hb_ref, c_ref, sa_ref, sb_ref, sc_ref):
+    last = jnp.concatenate(
+        [part_c, *sums, jnp.zeros((rank, rank - k_all - len(sums)), f32)], axis=1
+    )
+    second_ref[...] = jnp.zeros(second_ref.shape, f32) + (place_ref[0] % 2).astype(f32)
+    send_ref[0] = spread(cross_a)
+    send_ref[1] = spread(cross_b)
+    send_ref[2] = spread(last)
+
+
+def step_kernel(others, place_ref, all_ref, a_ref, b_ref, grams_ref, ra_ref, rb_ref, ha_ref, hb_ref, c_ref, sa_ref, sb_ref, sc_ref):
     rank, i_local = a_ref.shape
     k_all = 2 * others
-    used = 2 * rank + k_all
-    every = all_ref[...]
-    cross_a = every[:, :rank]
-    cross_b = every[:, rank : 2 * rank]
-    mttkrp_c = every[:, 2 * rank : used]
+    cross_a = gather_rows(all_ref[0])
+    cross_b = gather_rows(all_ref[1])
+    last = gather_rows(all_ref[2])
+    mttkrp_c = last[:, :k_all]
     gram_a = grams_ref[0]
     gram_b = grams_ref[1]
     factor_c = c_ref[...]
@@ -226,7 +234,7 @@
         total(once_c * twice_c),
     ]
     p0, p1, p2, p3 = [
-        total(every[:, used + k : used + k + 1]) + own[k] for k in range(4)
+        total(last[:, k_all + k : k_all + k + 1]) + own[k] for k in range(4)
     ]
 
     def mixed(xa, xb, xc):
@@ -291,7 +299,7 @@
     sa_ref[...] = on_res * res_a + on_image * image_a
     sb_ref[...] = on_res * res_b + on_image * image_b
     step_c = on_res * res_c + on_image * image_c
-    at = 2 * n_ref[0]
+    at = 2 * (place_ref[0] // 2)
     spot = lane(rank, k_all)
     square = lax.broadcasted_iota(jnp.int32, (rank, rank), 0) == lane(rank, rank)
     for k in range(2):
@@ -299,7 +307,7 @@
         sc_ref[k : k + 1, :] = jnp.sum(jnp.where(square, column, 0.0), axis=0, keepdims=True)
 
 
-def call(kernel, out_shape, operands, scalar=False, scratch=()):
+def call(kernel, out_shape, operands, scalar=False, scratch=(), room=16):
     vmem = pl.BlockSpec(memory_space=pltpu.VMEM)
     specs = [vmem] * len(operands)
     if scalar:
@@ -311,6 +319,7 @@
         in_specs=specs,
         out_specs=tuple(vmem for _ in outs),
         scratch_shapes=list(scratch),
+        compiler_params=pltpu.CompilerParams(vmem_limit_bytes=room << 20),
     )(*operands)
     return result if isinstance(out_shape, tuple) else result[0]
 
@@ -323,46 +332,49 @@
     like = jax.ShapeDtypeStruct
     flattened = tensor.reshape(k_local * i_local, j_whole)
     turned_c = factor_c.T
-    own = lax.axis_index(OTHER).astype(jnp.int32).reshape(1)
+    place = (lax.axis_index("core") + 2 * lax.axis_index(OTHER)).astype(jnp.int32).reshape(1)
     half = rank // 2
 
-    pair = call(
+    rows = like((peers * rank + half, LANES), f32)
+    keep, send = call(
         functools.partial(partial_b_kernel, peers),
-        like((2, peers * rank + half, LANES), f32),
-        (flattened, factor_a, turned_c),
-    )
-    pair = lax.all_to_all(pair, "core", 0, 0, tiled=True)
+        (rows, rows),
+        (place, flattened, factor_a, turned_c),
+        scalar=True,
+    )
+    came = lax.ppermute(send, "core", [(0, 1), (1, 0)])
     links = call(
         functools.partial(send_links_kernel, peers),
         like((peers, 2 * rank + rank // 4, LANES), bf16),
-        (pair, factor_b),
+        (keep, came, factor_b),
     )
     links = lax.all_to_all(links, LINKS, 0, 0, tiled=True)
     both = lax.all_gather(links[:, rank:, :], "core", axis=0, tiled=False)
     narrow, grams = call(
         functools.partial(partials_kernel, peers, others),
         (like((others, rank, 2 * LANES), f32), like((2, rank, rank), f32)),
-        (own, flattened, factor_a, turned_c, links, both),
+        (place, flattened, factor_a, turned_c, links, both),
         scalar=True,
         scratch=(pltpu.VMEM((rank, j_whole), bf16),),
     )
     narrow = lax.all_to_all(narrow, OTHER, 0, 0, tiled=True)
     square = like((rank, LANES), f32)
     thin = like((rank, i_local), f32)
-    send, res_a, res_b, once_a, once_b, whole_c = call(
+    send, second, res_a, res_b, once_a, once_b, whole_c = call(
         functools.partial(residual_kernel, others),
-        (square, thin, square, thin, square, like((rank, 2 * others), f32)),
-        (narrow, factor_a, factor_b, grams),
-    )
-    send = lax.psum(send, "core")
-    send = lax.dynamic_slice_in_dim(send, lax.axis_index("core") * half, half, 0)
-    send = jnp.broadcast_to(send, (peers, half, LANES))
+        (like((3, 8, LANES), f32), like((4, LANES), f32), thin, square, thin, square, like((rank, 2 * others), f32)),
+        (place, narrow, factor_a, factor_b, grams),
+        scalar=True,
+    )
+    send = lax.psum(send, "core").reshape(6, 4, LANES)
+    send = jnp.where(second > 0.5, send[3:], send[:3])
+    send = jnp.broadcast_to(send, (peers, 3, 4, LANES))
     send = lax.all_to_all(send, LINKS, 0, 0, tiled=True)
     every = lax.all_gather(jnp.sum(send, axis=0), "core", axis=0, tiled=True)
     step_a, step_b, turned_step_c = call(
         functools.partial(step_kernel, others),
         (thin, square, like((k_local, rank), f32)),
-        (own, every, factor_a, factor_b, grams, res_a, res_b, once_a, once_b, whole_c),
+        (place, every.reshape(3, 8, LANES), factor_a, factor_b, grams, res_a, res_b, once_a, once_b, whole_c),
         scalar=True,
     )
     return step_a, step_b, turned_step_c.T

time: 140 us -> 125 us (0.89)
  blocking collectives: 55.9 us -> 106 us
  waiting for transfers between devices: 47.6 us -> 1.53 us
  starting transfers between devices: 19.7 us -> 8.75 us
  Pallas kernels: 15 us -> 4.73 us
  local copies, waits for them, and re-layouts: 0.75 us -> 3.01 us
    all_to_all x1 -> x2, blocking collectives: 13 us -> 67.1 us  [the longest x1 41.9 us: on_device(): links = lax.all_to_all(links, LINKS, 0, 0, tiled=True)]
    all_to_all x2 -> x0, waiting for transfers between devices: 47.6 us -> none  [the longest x1 32 us: on_device(): links = lax.all_to_all(links, LINKS, 0, 0, tiled=True)]
    all_to_all x2 -> x0, starting transfers between devices: 19.7 us -> none  [the longest x1 9.92 us: on_device(): links = lax.all_to_all(links, LINKS, 0, 0, tiled=True)]
    pallas_call x5, Pallas kernels: 15 us -> 4.73 us  [call(): pl.pallas_call(kernel, out_shape=outs, in_specs=specs, out_specs=tuple((v...]
    ppermute x0 -> x1, starting transfers between devices: none -> 8.75 us  [on_device(): came = lax.ppermute(send, 'core', [(0, 1), (1, 0)])]
    all_to_all x1, blocking collectives: 30.5 us -> 27.5 us  [on_device(): send = lax.all_to_all(send, LINKS, 0, 0, tiled=True)]
    unnamed x4 -> x12, local copies, waits for them, and re-layouts: 0.69 us -> 2.95 us
    ppermute x0 -> x1, waiting for transfers between devices: none -> 1.53 us  [on_device(): came = lax.ppermute(send, 'core', [(0, 1), (1, 0)])]
  transfers between devices with their start and end apart: 2 -> 1, of which waited for: 2 -> 1; matrix products, arithmetic and copies ran while one was open for 0% -> 0% of each run, Pallas kernels for 0% -> 0%
where the time goes in v2:
time: 125 us
  blocking collectives  106 us (85%)
  starting transfers between devices  8.75 us (7%)
  Pallas kernels  4.73 us (4%)
  local copies, waits for them, and re-layouts  3.01 us (2%)
  waiting for transfers between devices  1.53 us (1%)
    all_to_all x1, blocking collectives, on_device(): links = lax.all_to_all(links, LINKS, 0, 0, tiled=True)  41.9 us
    all_to_all x1, blocking collectives, on_device(): send = lax.all_to_all(send, LINKS, 0, 0, tiled=True)  27.5 us
    all_to_all x1, blocking collectives, on_device(): narrow = lax.all_to_all(narrow, OTHER, 0, 0, tiled=True)  25.2 us
    ppermute x1, starting transfers between devices, on_device(): came = lax.ppermute(send, 'core', [(0, 1), (1, 0)])  8.75 us
    pallas_call x5, Pallas kernels, call(): pl.pallas_call(kernel, out_shape=outs, in_specs=specs, out_specs=tuple((v...  4.73 us
    psum x1, blocking collectives, on_device(): send = lax.psum(send, 'core').reshape(6, 4, LANES)  4.73 us
    all_gather x1, blocking collectives, on_device(): both = lax.all_gather(links[:, rank:, :], 'core', axis=0, tiled=False)  3.6 us
    all_gather x1, blocking collectives, on_device(): every = lax.all_gather(jnp.sum(send, axis=0), 'core', axis=0, tiled=True)  3.43 us
  transfers between devices with their start and end apart: 1, of which 1 were waited for; matrix products, arithmetic and copies ran while one was open for 0% of the time, Pallas kernels for 0%

profile of v2, /device:TPU:1, one launch (start us, length us, event | category | flops | bytes accessed | tf_op | source)
XLA Modules:
  0.0 125.1 jit_solution(2517450310423450268)
XLA Ops:
  0.6 0.0 copy-start.4
  0.6 0.0 copy-start
  0.7 1.6 %copy-done = bf16[2,64,8192]{2,1,0:T(8,128)(2,1)S(1)} copy-done((bf16[2,64,8192]{2,1,0:T(8,128)(2,1)S(1)}, bf16[2,64,8192]{2,1,0:T(8,128)(2,1)}, u32[]{:S(2)}) %copy-start) | copy-done | bytes 2097176
  2.2 0.0 copy-start.2
  2.2 0.7 copy-done.2
  2.9 0.0 copy-start.5
  2.9 0.7 copy-done.5
  3.6 0.5 shard_map.67
  4.1 8.7 %collective-permute-start = (f32[1040,128]{1,0:T(8,128)S(1)}, f32[1040,128]{1,0:T(8,128)S(1)}, u32[]{:S(2)}, u32[]{:S(2)}) collective-permute-start(f32[1040,128]{1,0:T(8,128)S(1)} %get-tuple-element.18), channel_id=1, source_target_pairs={{0,8},{8,0},{1,9},{9,1},{2,10},{10,2},{3,11},{11,3},{4,12},{12,4},... | collective-permute-start | bytes 1597448 | tf_op jit(solution)/shard_map/ppermute | solution.py:345
  12.9 1.5 %collective-permute-done.came_ref = f32[1040,128]{1,0:T(8,128)S(1)} collective-permute-done((f32[1040,128]{1,0:T(8,128)S(1)}, f32[1040,128]{1,0:T(8,128)S(1)}, u32[]{:S(2)}, u32[]{:S(2)}) %collective-permute-start) | collective-permute-done | bytes 532512 | tf_op jit(solution)/shard_map/ppermute | solution.py:345
  14.4 0.0 copy-done.4
  14.4 0.0 copy-start.1
  14.4 0.1 shard_map.68
  14.5 41.9 %all_to_all.15.got_ref = bf16[32,72,128]{2,1,0:T(8,128)(2,1)S(1)} all-to-all(bf16[32,72,128]{2,1,0:T(8,128)(2,1)S(1)} %shard_map.68), channel_id=1, replica_groups=mesh['y'=4,'z_lo'=8,'core'=2,'x'=4,'z_hi'=2] {'y','z_lo'}, dimensions={0} | all-to-all | bytes 1179648 | tf_op jit(solution)/shard_map/all_to_all | solution.py:351
  56.4 3.6 %all-gather = bf16[64,40,128]{2,1,0:T(8,128)(2,1)S(1)} all-gather(bf16[32,40,128]{2,1,0:T(8,128)(2,1)S(1)} %slice.12), channel_id=2, replica_groups=mesh['y'=4,'z_lo'=8,'core'=2,'x'=4,'z_hi'=2] {'core'}, dimensions={0}, use_global_device_ids=true | all-gather | bytes 983040 | tf_op jit(solution)/shard_map/all_gather | solution.py:352
  60.0 0.0 copy-done.1
  60.0 0.0 copy-start.3
  60.0 1.1 shard_map.69
  61.1 25.2 %all_to_all.16.got_ref = f32[8,32,256]{2,1,0:T(8,128)S(1)} all-to-all(f32[8,32,256]{2,1,0:T(8,128)S(1)} %get-tuple-element.19), channel_id=1, replica_groups=mesh['y'=4,'z_lo'=8,'core'=2,'x'=4,'z_hi'=2] {'x','z_hi'}, dimensions={0} | all-to-all | bytes 524288 | tf_op jit(solution)/shard_map/all_to_all | solution.py:360
  86.3 0.9 shard_map.70
  87.2 4.7 %psum.7 = f32[6,4,128]{2,1,0:T(4,128)S(1)} all-reduce(f32[6,4,128]{2,1,0:T(4,128)S(1)} %bitcast.11), channel_id=1, replica_groups=mesh['y'=4,'z_lo'=8,'core'=2,'x'=4,'z_hi'=2] {'core'}, use_global_device_ids=true, to_apply=%region_0.0 | all-reduce | flops 3072 | bytes 24576 | tf_op jit(solution)/shard_map/psum | solution.py:369
  92.0 27.5 %all_to_all.17 = f32[32,3,4,128]{3,2,1,0:T(4,128)S(1)} all-to-all(f32[32,3,4,128]{3,2,1,0:T(4,128)S(1)} %broadcast_in_dim.8), channel_id=1, replica_groups=mesh['y'=4,'z_lo'=8,'core'=2,'x'=4,'z_hi'=2] {'y','z_lo'}, dimensions={0} | all-to-all | bytes 393216 | tf_op jit(solution)/shard_map/all_to_all | solution.py:372
  119.5 0.1 reduce_sum.9
  119.5 3.4 %all_gather.11 = f32[6,4,128]{2,1,0:T(4,128)S(1)} all-gather(f32[3,4,128]{2,1,0:T(4,128)S(1)} %reduce_sum.9), channel_id=1, replica_groups=mesh['y'=4,'z_lo'=8,'core'=2,'x'=4,'z_hi'=2] {'core'}, dimensions={0}, use_global_device_ids=true | all-gather | bytes 18432 | tf_op jit(solution)/shard_map/all_gather | solution.py:373
  123.0 0.0 copy-done.3
  123.0 2.1 %shard_map.71 = (f32[32,64]{1,0:T(8,128)}, f32[32,128]{1,0:T(8,128)}, f32[2,32]{1,0:T(2,128)}) custom-call(s32[1]{0:T(128)} %bitcast.place_ref, f32[3,8,128]{2,1,0:T(8,128)S(1)} %bitcast.10, bf16[32,64]{1,0:T(8,128)(2,1)S(1)} %copy-done.3, bf16[32,128]{1,0:T(8,128)(2,1)S(1)} %copy-done.4, f32[2,32,32]{2,1,0:T(8,128)S(1)} %get-tuple-element.20.grams_ref, ...), custom_call_target="tpu_custom_call" | custom-call | tf_op jit(solution)/shard_map/pallas_call | solution.py:316
  (4 shorter events, 0.1 us)
Async XLA Ops:
  0.6 13.8 %copy-start.4 = (bf16[32,128]{1,0:T(8,128)(2,1)S(1)}, bf16[32,128]{1,0:T(8,128)(2,1)}, u32[]{:S(2)}) copy-start(bf16[32,128]{1,0:T(8,128)(2,1)} %b_ref.5) | copy-start | bytes 24580
  0.6 1.6 %copy-start = (bf16[2,64,8192]{2,1,0:T(8,128)(2,1)S(1)}, bf16[2,64,8192]{2,1,0:T(8,128)(2,1)}, u32[]{:S(2)}) copy-start(bf16[2,64,8192]{2,1,0:T(8,128)(2,1)} %param.4) | copy-start | bytes 6291460
  2.2 0.7 copy-start.2
  2.9 0.7 copy-start.5
  4.1 10.3 %collective-permute-start = (f32[1040,128]{1,0:T(8,128)S(1)}, f32[1040,128]{1,0:T(8,128)S(1)}, u32[]{:S(2)}, u32[]{:S(2)}) collective-permute-start(f32[1040,128]{1,0:T(8,128)S(1)} %get-tuple-element.18), channel_id=1, source_target_pairs={{0,8},{8,0},{1,9},{9,1},{2,10},{10,2},{3,11},{11,3},{4,12},{12,4},... | collective-permute-start | bytes 1597448 | tf_op jit(solution)/shard_map/ppermute | solution.py:345
  14.4 45.6 %copy-start.1 = (bf16[2,64,8192]{2,1,0:T(8,128)(2,1)S(1)}, bf16[2,64,8192]{2,1,0:T(8,128)(2,1)}, u32[]{:S(2)}) copy-start(bf16[2,64,8192]{2,1,0:T(8,128)(2,1)} %param.4) | copy-start | bytes 6291460
  60.0 62.9 %copy-start.3 = (bf16[32,64]{1,0:T(8,128)(2,1)S(1)}, bf16[32,64]{1,0:T(8,128)(2,1)}, u32[]{:S(2)}) copy-start(bf16[32,64]{1,0:T(8,128)(2,1)} %a_ref.7) | copy-start | bytes 12292

commit v3 on v2

v3 whole, which is shorter than its diff:
```python
import functools

import jax
import jax.numpy as jnp
from jax import lax
from jax.experimental import pallas as pl
from jax.experimental.pallas import tpu as pltpu
from jax.sharding import Mesh
from jax.sharding import PartitionSpec as P


f32 = jnp.float32
bf16 = jnp.bfloat16
LANES = 128
damping = 1.0
highest = lax.Precision.HIGHEST

WIDE = (4, 2, 4, 2)
NARROW = (4, 2)
NEAR = ("y", "z_near")
LINKS = ("y", "z_far", "z_near")
OTHER = ("x", "z_hi")


def mul(left, right):
    return jnp.dot(left, right, precision=highest, preferred_element_type=f32)


def mul_t(left, right):
    return lax.dot_general(
        left, right, (((1,), (1,)), ((), ())), precision=highest, preferred_element_type=f32
    )


def lane(rows, width):
    return lax.broadcasted_iota(jnp.int32, (rows, width), 1)


def columns_of(row_block):
    count, rank = row_block.shape
    eye = lax.broadcasted_iota(jnp.int32, (rank, rank), 0) == lane(rank, rank)
    return [
        jnp.sum(jnp.where(eye, row_block[k : k + 1, :], 0.0), axis=1, keepdims=True)
        for k in range(count)
    ]


def spread(square):
    rows = square.shape[0] // 4
    return jnp.concatenate([square[k * rows : (k + 1) * rows, :] for k in range(4)], axis=1)


def gather_rows(wide_block):
    width = wide_block.shape[1] // 4
    return jnp.concatenate([wide_block[:, k * width : (k + 1) * width] for k in range(4)], axis=0)


def share_kernel(a_hbm, b_hbm, ct_hbm, own_ref, khatri_ref, a_ref, b_ref, ct_ref, sems):
    copies = [
        pltpu.make_async_copy(source, target, sems.at[k])
        for k, (source, target) in enumerate(((a_hbm, a_ref), (b_hbm, b_ref), (ct_hbm, ct_ref)))
    ]
    for copy in copies:
        copy.start()
    for copy in copies:
        copy.wait()
    rank = a_ref.shape[0]
    factor_a = a_ref[...]
    own_ref[:rank, :] = b_ref[...]
    own_ref[rank:, :] = two_terms(
        lax.dot_general(
            factor_a, factor_a, (((1,), (1,)), ((), ())), preferred_element_type=f32
        )
    )
    float_a = factor_a.astype(f32)
    cols = columns_of(ct_ref[...].astype(f32))
    khatri_ref[...] = jnp.concatenate([col * float_a for col in cols], axis=1).astype(bf16)


def two_terms(square):
    half = square.shape[0] // 2
    high = square.astype(bf16).astype(f32)
    low = square - high
    return jnp.concatenate([high[:half], high[half:], low[:half], low[half:]], axis=1).astype(bf16)


def one_square(packed):
    width = packed.shape[1] // 4
    return jnp.concatenate(
        [
            packed[:, :width] + packed[:, 2 * width : 3 * width],
            packed[:, width : 2 * width] + packed[:, 3 * width :],
        ],
        axis=0,
    )


def partial_b_kernel(place_ref, khatri_ref, t_ref, keep_ref, send_ref):
    khatri = khatri_ref[...]
    pieces = 4
    width = t_ref.shape[1] // pieces
    first_core = place_ref[0] % 2 == 0
    per = width // LANES
    for piece in range(pieces):
        part = jnp.dot(
            khatri, t_ref[:, piece * width : (piece + 1) * width], preferred_element_type=f32
        )
        for step in range(0, per, 2):
            chunk = (piece * per + step) // 2
            even = part[:, step * LANES : (step + 1) * LANES]
            odd = part[:, (step + 1) * LANES : (step + 2) * LANES]
            keep_ref[chunk] = jnp.where(first_core, even, odd)
            send_ref[chunk] = jnp.where(first_core, odd, even)


def send_near_kernel(nears, place_ref, keep_ref, came_ref, own_ref, far_ref, out_ref):
    rank = keep_ref.shape[1]
    near_z = WIDE[2]
    first_far = (place_ref[0] // 2) % 2 == 0
    own_b = own_ref[:rank, :]
    far_b = far_ref[:rank, :]
    low_b = jnp.where(first_far, own_b.astype(f32), far_b.astype(f32)).astype(bf16)
    high_b = jnp.where(first_far, far_b.astype(f32), own_b.astype(f32)).astype(bf16)
    gram = two_terms(
        one_square(own_ref[rank:, :].astype(f32)) + one_square(far_ref[rank:, :].astype(f32))
    )
    for near in range(nears):
        y, z = divmod(near, near_z)
        for far in range(2):
            chunk = (y * 2 + far) * near_z + z
            out_ref[near, far * rank : (far + 1) * rank, :] = (
                keep_ref[chunk] + came_ref[chunk]
            ).astype(bf16)
        out_ref[near, 2 * rank : 3 * rank, :] = low_b
        out_ref[near, 3 * rank : 4 * rank, :] = high_b
        out_ref[near, 4 * rank :, :] = gram


def sum_b_kernel(nears, place_ref, got_ref, keep_ref, send_ref):
    rank = keep_ref.shape[0]
    first_far = (place_ref[0] // 2) % 2 == 0
    sums = []
    for far in range(2):
        rows = pl.ds(far * rank, rank)
        total = got_ref[0, rows, :].astype(f32)
        for near in range(1, nears):
            total = total + got_ref[near, rows, :].astype(f32)
        sums.append(total)
    keep_ref[...] = jnp.where(first_far, sums[0], sums[1])
    send_ref[...] = jnp.where(first_far, sums[1], sums[0])


def partials_kernel(nears, others, place_ref, t_ref, a_ref, ct_ref, both_ref, tile_ref, grams_ref, whole_b):
    rank, i_local = a_ref.shape
    near_z = WIDE[2]
    packed = jnp.zeros((rank // 2, LANES), f32)
    for core in range(2):
        for near in range(nears):
            y, z = divmod(near, near_z)
            for far in range(2):
                start = (((y * 2 + far) * near_z + z) * 2 + core) * LANES
                whole_b[:, start : start + LANES] = both_ref[
                    core, near, far * rank : (far + 1) * rank, :
                ]
            packed = packed + both_ref[core, near, 2 * rank :, :].astype(f32)
    every_b = whole_b[...]
    contracted = lax.dot_general(
        every_b, t_ref[...], (((1,), (1,)), ((), ())), preferred_element_type=f32
    )
    grams_ref[0] = one_square(packed)
    grams_ref[1] = lax.dot_general(
        every_b, every_b, (((1,), (1,)), ((), ())), preferred_element_type=f32
    )
    first, second = columns_of(ct_ref[...].astype(f32))
    float_a = a_ref[...].astype(f32)
    spot = lane(rank, LANES)
    low_half = spot < i_local
    scaled = contracted * jnp.where(low_half, first, second)
    part_a = scaled + pltpu.roll(scaled, i_local, 1)
    against_a = contracted * jnp.concatenate([float_a, float_a], axis=1)
    c_first = jnp.sum(jnp.where(low_half, against_a, 0.0), axis=1, keepdims=True)
    c_second = jnp.sum(jnp.where(low_half, 0.0, against_a), axis=1, keepdims=True)
    at = i_local + 2 * (place_ref[0] // 4)
    k_all = 2 * others
    tail = jnp.where(spot == at, c_first, 0.0)
    tail = jnp.where(spot == at + 1, c_second, tail)
    tail = jnp.where(spot == at + k_all, first, tail)
    tail = jnp.where(spot == at + k_all + 1, second, tail)
    tile_ref[...] = jnp.where(low_half, part_a, tail)


def send_narrow_kernel(others, keep_ref, came_ref, tile_ref, out_ref):
    sum_b = keep_ref[...] + came_ref[...]
    tile = tile_ref[...]
    for other in range(others):
        out_ref[other, :, :LANES] = sum_b
        out_ref[other, :, LANES:] = tile


def residual_kernel(others, got_ref, a_ref, b_ref, grams_ref, send_ref, ra_ref, rb_ref, ha_ref, hb_ref, c_ref):
    rank, i_local = a_ref.shape
    k_all = 2 * others
    total = got_ref[0]
    for other in range(1, others):
        total = total + got_ref[other]
    mttkrp_b = total[:, :LANES]
    mttkrp_a = total[:, LANES : LANES + i_local]
    part_c = total[:, LANES + i_local : LANES + i_local + k_all]
    factor_c = total[:, LANES + i_local + k_all : LANES + i_local + 2 * k_all]
    c_ref[...] = factor_c
    gram_a = grams_ref[0]
    gram_b = grams_ref[1]
    gram_c = mul_t(factor_c, factor_c)
    had_a = gram_b * gram_c
    had_b = gram_a * gram_c
    float_a = a_ref[...].astype(f32)
    float_b = b_ref[...].astype(f32)
    res_a = mttkrp_a - mul(had_a, float_a)
    res_b = mttkrp_b - mul(had_b, float_b)
    once_a = mul(had_a, res_a)
    once_b = mul(had_b, res_b)
    twice_a = mul(had_a, once_a)
    twice_b = mul(had_b, once_b)
    ra_ref[...] = res_a
    rb_ref[...] = res_b
    ha_ref[...] = once_a
    hb_ref[...] = once_b

    def inner(left_a, right_a, left_b, right_b):
        by_row = jnp.sum(left_a * right_a, axis=1, keepdims=True) + jnp.sum(
            left_b * right_b, axis=1, keepdims=True
        )
        return by_row

    sums = [
        inner(res_a, res_a, res_b, res_b),
        inner(res_a, once_a, res_b, once_b),
        inner(once_a, once_a, once_b, once_b),
        inner(once_a, twice_a, once_b, twice_b),
    ]
    cross_a = mul_t(float_a, res_a)
    cross_b = mul_t(float_b, res_b)
    last = jnp.concatenate(
        [part_c, *sums, jnp.zeros((rank, rank - k_all - len(sums)), f32)], axis=1
    )
    send_ref[0] = spread(cross_a)
    send_ref[1] = spread(cross_b)
    send_ref[2] = spread(last)


def send_links_kernel(links, place_ref, pair_ref, out_ref):
    first_core = place_ref[0] % 2 == 0
    last = pair_ref[2]
    high = last.astype(bf16).astype(f32)
    cross = jnp.where(first_core, pair_ref[0], pair_ref[1])
    tail = jnp.where(first_core, high, last - high)
    packed = jnp.concatenate([cross, tail], axis=0).astype(bf16)
    for link in range(links):
        out_ref[link] = packed


def step_kernel(others, place_ref, all_ref, a_ref, b_ref, grams_ref, ra_ref, rb_ref, ha_ref, hb_ref, c_ref, sa_ref, sb_ref, sc_ref):
    rank, _ = a_ref.shape
    k_all = 2 * others
    sums = []
    for core in range(2):
        total_sum = all_ref[core, 0].astype(f32)
        for link in range(1, all_ref.shape[1]):
            total_sum = total_sum + all_ref[core, link].astype(f32)
        sums.append(total_sum)
    slab = rank // 4
    cross_a = gather_rows(sums[0][:slab])
    cross_b = gather_rows(sums[1][:slab])
    last = gather_rows(sums[0][slab:] + sums[1][slab:])
    mttkrp_c = last[:, :k_all]
    gram_a = grams_ref[0]
    gram_b = grams_ref[1]
    factor_c = c_ref[...]
    gram_c = mul_t(factor_c, factor_c)
    had_a = gram_b * gram_c
    had_b = gram_a * gram_c
    had_c = gram_a * gram_b
    res_c = mttkrp_c - mul(had_c, factor_c)
    once_c = mul(had_c, res_c)
    twice_c = mul(had_c, once_c)
    cross_c = mul_t(factor_c, res_c)

    def total(value):
        return jnp.sum(jnp.sum(value, axis=1, keepdims=True), axis=0, keepdims=True)

    own = [
        total(res_c * res_c),
        total(res_c * once_c),
        total(once_c * once_c),
        total(once_c * twice_c),
    ]
    p0, p1, p2, p3 = [
        total(last[:, k_all + k : k_all + k + 1]) + own[k] for k in range(4)
    ]

    def mixed(xa, xb, xc):
        return (
            xb * gram_c + gram_b * xc,
            xa * gram_c + gram_a * xc,
            xa * gram_b + gram_a * xb,
        )

    eye = (
        lax.broadcasted_iota(jnp.int32, (rank, rank), 0) == lane(rank, rank)
    ).astype(f32)
    grams = (gram_a, gram_b, gram_c)
    shifted = tuple(had + damping * eye for had in (had_a, had_b, had_c))
    crosses = (cross_a, cross_b, cross_c)
    mix = mixed(*crosses)
    mix_gram = [mul(m, g) for m, g in zip(mix, grams)]
    turned = [mul_t(s, x) for s, x in zip(shifted, crosses)]
    twice_turned = [mul(s, t) for s, t in zip(shifted, turned)]
    shifted_mix = [mul(s, m) for s, m in zip(shifted, mix)]
    image_cross_t = [t + mg for t, mg in zip(turned, mix_gram)]
    image_cross = [
        mul(x, s) + mul_t(g, m) for x, s, g, m in zip(crosses, shifted, grams, mix)
    ]
    image_mix = mixed(*image_cross)
    one = damping
    c0 = p0
    k1 = p1 + one * p0
    k2 = p2 + 2.0 * one * p1 + one * one * p0
    k3 = p3 + 3.0 * one * p2 + 3.0 * one * one * p1 + one * one * one * p0
    c1 = k1
    c2 = k2
    c3 = k3
    crosses_t = [mul_t(eye, x) for x in crosses]
    c1 = c1 + total(sum(m * xt for m, xt in zip(mix, crosses_t)))
    c2 = c2 + total(
        sum(2.0 * m * t + mg * m for m, t, mg in zip(mix, turned, mix_gram))
    )
    c3 = c3 + total(
        sum(
            2.0 * m * tt + mg * sm + im * ict
            for m, tt, mg, sm, im, ict in zip(
                mix, twice_turned, mix_gram, shifted_mix, image_mix, image_cross_t
            )
        )
    )
    alpha = c0 / c1
    fresh = c0 - 2.0 * alpha * c1 + alpha * alpha * c2
    beta = fresh / c0
    keep = 1.0 + beta
    curvature = keep * keep * c1 - 2.0 * keep * alpha * c2 + alpha * alpha * c3
    second = fresh / curvature
    on_res = alpha + second * keep
    on_image = -second * alpha
    float_a = a_ref[...].astype(f32)
    float_b = b_ref[...].astype(f32)
    res_a = ra_ref[...]
    res_b = rb_ref[...]
    image_a = damping * res_a + ha_ref[...] + mul(mix[0], float_a)
    image_b = damping * res_b + hb_ref[...] + mul(mix[1], float_b)
    image_c = damping * res_c + once_c + mul(mix[2], factor_c)
    sa_ref[...] = on_res * res_a + on_image * image_a
    sb_ref[...] = on_res * res_b + on_image * image_b
    step_c = on_res * res_c + on_image * image_c
    at = 2 * (place_ref[0] // 4)
    spot = lane(rank, k_all)
    square = lax.broadcasted_iota(jnp.int32, (rank, rank), 0) == lane(rank, rank)
    for k in range(2):
        column = jnp.sum(jnp.where(spot == at + k, step_c, 0.0), axis=1, keepdims=True)
        sc_ref[k : k + 1, :] = jnp.sum(jnp.where(square, column, 0.0), axis=0, keepdims=True)


VMEM_BYTES = 67043328


def call(kernel, out_shape, operands, scalar=False, scratch=(), limit=16 << 20, fetch=()):
    vmem = pl.BlockSpec(memory_space=pltpu.VMEM)
    specs = [vmem] * len(operands)
    for k in fetch:
        specs[k] = pl.BlockSpec(memory_space=pltpu.HBM)
    if scalar:
        specs[0] = pl.BlockSpec(memory_space=pltpu.SMEM)
    outs = out_shape if isinstance(out_shape, tuple) else (out_shape,)
    result = pl.pallas_call(
        kernel,
        out_shape=outs,
        in_specs=specs,
        out_specs=tuple(vmem for _ in outs),
        scratch_shapes=list(scratch),
        compiler_params=pltpu.CompilerParams(vmem_limit_bytes=limit),
    )(*operands)
    return result if isinstance(out_shape, tuple) else result[0]


def stages(tensor, factor_a, factor_b, factor_c):
    k_local, i_local, j_whole = tensor.shape
    rank = factor_a.shape[0]
    chunks = j_whole // (2 * LANES)
    nears = chunks // 2
    others = lax.axis_size(OTHER)
    like = jax.ShapeDtypeStruct
    flattened = tensor.reshape(k_local * i_local, j_whole)
    turned_c = factor_c.T
    place = (
        lax.axis_index("core") + 2 * lax.axis_index("z_far") + 4 * lax.axis_index(OTHER)
    ).astype(jnp.int32).reshape(1)
    half = rank // 2
    square = like((rank, LANES), f32)
    thin = like((rank, i_local), f32)

    own, khatri = call(
        share_kernel,
        (like((rank + half, LANES), bf16), like((rank, k_local * i_local), bf16)),
        (factor_a, factor_b, turned_c),
        scratch=(
            pltpu.VMEM(factor_a.shape, bf16),
            pltpu.VMEM(factor_b.shape, bf16),
            pltpu.VMEM(turned_c.shape, bf16),
            pltpu.SemaphoreType.DMA((3,)),
        ),
        limit=VMEM_BYTES,
        fetch=(0, 1, 2),
    )
    far = lax.ppermute(own, "z_far", [(0, 1), (1, 0)])
    block = like((chunks, rank, LANES), f32)
    keep, send = call(
        partial_b_kernel,
        (block, block),
        (place, khatri, flattened),
        scalar=True,
    )
    came = lax.ppermute(send, "core", [(0, 1), (1, 0)])
    near = call(
        functools.partial(send_near_kernel, nears),
        like((nears, 4 * rank + half, LANES), bf16),
        (place, keep, came, own, far),
        scalar=True,
    )
    near = lax.all_to_all(near, NEAR, 0, 0, tiled=True)
    keep, send = call(
        functools.partial(sum_b_kernel, nears), (square, square), (place, near), scalar=True
    )
    came = lax.ppermute(send, "z_far", [(0, 1), (1, 0)])
    both = lax.all_gather(near[:, 2 * rank :, :], "core", axis=0, tiled=False)
    tile, grams = call(
        functools.partial(partials_kernel, nears, others),
        (square, like((2, rank, rank), f32)),
        (place, flattened, factor_a, turned_c, both),
        scalar=True,
        scratch=(pltpu.VMEM((rank, j_whole), bf16),),
    )
    narrow = call(
        functools.partial(send_narrow_kernel, others),
        like((others, rank, 2 * LANES), f32),
        (keep, came, tile),
    )
    narrow = lax.all_to_all(narrow, OTHER, 0, 0, tiled=True)
    send, res_a, res_b, once_a, once_b, whole_c = call(
        functools.partial(residual_kernel, others),
        (like((3, 8, LANES), f32), thin, square, thin, square, like((rank, 2 * others), f32)),
        (narrow, factor_a, factor_b, grams),
    )
    send = lax.psum(send, "core")
    send = call(
        functools.partial(send_links_kernel, chunks),
        like((chunks, half, LANES), bf16),
        (place, send),
        scalar=True,
    )
    send = lax.all_to_all(send, LINKS, 0, 0, tiled=True)
    every = lax.all_gather(send, "core", axis=0, tiled=False)
    step_a, step_b, turned_step_c = call(
        functools.partial(step_kernel, others),
        (thin, square, like((k_local, rank), f32)),
        (place, every, factor_a, factor_b, grams, res_a, res_b, once_a, once_b, whole_c),
        scalar=True,
    )
    return step_a, step_b, turned_step_c.T


def solution(mesh):
    wide = ("y", "z_far", "z_near", "core")
    inner = Mesh(mesh.devices.reshape(WIDE + NARROW), wide + OTHER)
    return jax.shard_map(
        stages,
        mesh=inner,
        in_specs=(P(OTHER, wide, None), P(None, wide), P(None, wide), P(None, OTHER)),
        out_specs=(P(None, wide), P(None, wide), P(None, OTHER)),
        check_vma=False,
    )
```

time: 125 us -> 120 us (0.960)
  blocking collectives: 106 us -> 85.9 us
  starting transfers between devices: 8.75 us -> 19.6 us
  waiting for transfers between devices: 1.53 us -> 4.87 us
  Pallas kernels: 4.73 us -> 6.35 us
    all_to_all x3, blocking collectives: 94.6 us -> 69.7 us  [the longest x1 24.4 us: stages(): narrow = lax.all_to_all(narrow, OTHER, 0, 0, tiled=True)]
    ppermute x1 -> x3, starting transfers between devices: 8.75 us -> 19.6 us  [the longest x1 8.75 us: stages(): came = lax.ppermute(send, 'core', [(0, 1), (1, 0)])]
    ppermute x1 -> x3, waiting for transfers between devices: 1.53 us -> 4.87 us  [the longest x1 4.86 us: stages(): far = lax.ppermute(own, 'z_far', [(0, 1), (1, 0)])]
    psum x1, blocking collectives: 4.73 us -> 7.18 us  [stages(): send = lax.psum(send, 'core')]
    all_gather x2, blocking collectives: 7.03 us -> 8.99 us  [the longest x1 5.09 us: stages(): every = lax.all_gather(send, 'core', axis=0, tiled=False)]
    pallas_call x5 -> x9, Pallas kernels: 4.73 us -> 6.35 us  [call(): pl.pallas_call(kernel, out_shape=outs, in_specs=specs, out_specs=tuple((v...]
    unnamed x12 -> x14, local copies, waits for them, and re-layouts: 2.95 us -> 2.31 us
  transfers between devices with their start and end apart: 1 -> 3, of which waited for: 1 -> 1; matrix products, arithmetic and copies ran while one was open for 0% -> 0% of each run, Pallas kernels for 0% -> 1%
where the time goes in v3:
time: 120 us
  blocking collectives  85.9 us (72%)
  starting transfers between devices  19.6 us (16%)
  Pallas kernels  6.35 us (5%)
  waiting for transfers between devices  4.87 us (4%)
  local copies, waits for them, and re-layouts  2.33 us (2%)
    all_to_all x1, blocking collectives, stages(): narrow = lax.all_to_all(narrow, OTHER, 0, 0, tiled=True)  24.4 us
    all_to_all x1, blocking collectives, stages(): send = lax.all_to_all(send, LINKS, 0, 0, tiled=True)  23.7 us
    all_to_all x1, blocking collectives, stages(): near = lax.all_to_all(near, NEAR, 0, 0, tiled=True)  21.7 us
    ppermute x1, starting transfers between devices, stages(): came = lax.ppermute(send, 'core', [(0, 1), (1, 0)])  8.75 us
    ppermute x1, starting transfers between devices, stages(): came = lax.ppermute(send, 'z_far', [(0, 1), (1, 0)])  7.4 us
    psum x1, blocking collectives, stages(): send = lax.psum(send, 'core')  7.18 us
    pallas_call x9, Pallas kernels, call(): pl.pallas_call(kernel, out_shape=outs, in_specs=specs, out_specs=tuple((v...  6.35 us
    all_gather x1, blocking collectives, stages(): every = lax.all_gather(send, 'core', axis=0, tiled=False)  5.09 us
  transfers between devices with their start and end apart: 3, of which 1 were waited for; matrix products, arithmetic and copies ran while one was open for 0% of the time, Pallas kernels for 1%

profile of v3, /device:TPU:1, one launch (start us, length us, event | category | flops | bytes accessed | tf_op | source)
XLA Modules:
  0.0 119.8 jit_solution(16451881842209022310)
XLA Ops:
  0.6 1.5 %shard_map.67 = (bf16[48,128]{1,0:T(8,128)(2,1)}, bf16[32,128]{1,0:T(8,128)(2,1)}) custom-call(bf16[32,64]{1,0:T(8,128)(2,1)} %a_ref.5, bf16[32,128]{1,0:T(8,128)(2,1)} %b_ref.3, bf16[2,32]{1,0:T(2,128)(2,1)} %bitcast.10), custom_call_target="tpu_custom_call" | custom-call | tf_op jit(solution)/shard_map/pallas_call | solution.py:382
  2.2 0.0 copy-start
  2.2 1.6 %copy-done = bf16[2,64,8192]{2,1,0:T(8,128)(2,1)S(1)} copy-done((bf16[2,64,8192]{2,1,0:T(8,128)(2,1)S(1)}, bf16[2,64,8192]{2,1,0:T(8,128)(2,1)}, u32[]{:S(2)}) %copy-start) | copy-done | bytes 2097176
  3.8 0.0 copy-start.5
  3.8 0.7 copy-done.5
  4.5 0.0 copy-start.4
  4.5 0.4 shard_map.68
  4.9 8.7 %collective-permute-start = (f32[32,32,128]{2,1,0:T(8,128)S(1)}, f32[32,32,128]{2,1,0:T(8,128)S(1)}, u32[]{:S(2)}, u32[]{:S(2)}) collective-permute-start(f32[32,32,128]{2,1,0:T(8,128)S(1)} %get-tuple-element.22), channel_id=1, source_target_pairs={{0,8},{8,0},{1,9},{9,1},{2,10},{10,2},{3,11},{11,3},{4,12},{12,4},... | collective-permute-start | bytes 1572872 | tf_op jit(solution)/shard_map/ppermute | solution.py:430
  13.6 0.0 copy-done.4
  13.7 3.5 %collective-permute-start.1 = (bf16[48,128]{1,0:T(8,128)(2,1)S(1)}, bf16[48,128]{1,0:T(8,128)(2,1)S(1)}, u32[]{:S(2)}, u32[]{:S(2)}) collective-permute-start(bf16[48,128]{1,0:T(8,128)(2,1)S(1)} %copy-done.4), channel_id=1, source_target_pairs={{0,64},{64,0},{1,65},{65,1},{2,66},{66,2},{3,67},{67,3},{4,68},{68... | collective-permute-start | bytes 36872 | tf_op jit(solution)/shard_map/ppermute | solution.py:422
  17.1 4.9 %collective-permute-done.1.far_ref = bf16[48,128]{1,0:T(8,128)(2,1)S(1)} collective-permute-done((bf16[48,128]{1,0:T(8,128)(2,1)S(1)}, bf16[48,128]{1,0:T(8,128)(2,1)S(1)}, u32[]{:S(2)}, u32[]{:S(2)}) %collective-permute-start.1) | collective-permute-done | bytes 12320 | tf_op jit(solution)/shard_map/ppermute | solution.py:422
  22.0 0.0 collective-permute-done.came_ref
  22.0 0.2 shard_map.69
  22.2 0.0 copy-start.1
  22.2 0.0 copy-start.2
  22.3 0.0 copy-start.6
  22.3 21.7 %all_to_all.15.got_ref = bf16[16,144,128]{2,1,0:T(8,128)(2,1)S(1)} all-to-all(bf16[16,144,128]{2,1,0:T(8,128)(2,1)S(1)} %shard_map.69), channel_id=1, replica_groups=mesh['y'=4,'z_far'=2,'z_near'=4,'core'=2,'x'=4,'z_hi'=2] {'y','z_near'}, dimensions={0} | all-to-all | bytes 1179648 | tf_op jit(solution)/shard_map/all_to_all | solution.py:437
  44.0 7.4 %collective-permute-start.2 = (f32[32,128]{1,0:T(8,128)S(1)}, f32[32,128]{1,0:T(8,128)S(1)}, u32[]{:S(2)}, u32[]{:S(2)}) collective-permute-start(f32[32,128]{1,0:T(8,128)S(1)} %get-tuple-element.25), channel_id=1, source_target_pairs={{0,64},{64,0},{1,65},{65,1},{2,66},{66,2},{3,67},{67,3},{4,68},{68... | collective-permute-start | bytes 49160 | tf_op jit(solution)/shard_map/ppermute | solution.py:441
  51.4 0.0 copy-start.3
  51.4 3.9 %all-gather = bf16[32,80,128]{2,1,0:T(8,128)(2,1)S(1)} all-gather(bf16[16,80,128]{2,1,0:T(8,128)(2,1)S(1)} %slice.4), channel_id=2, replica_groups=mesh['y'=4,'z_far'=2,'z_near'=4,'core'=2,'x'=4,'z_hi'=2] {'core'}, dimensions={0}, use_global_device_ids=true | all-gather | bytes 983040 | tf_op jit(solution)/shard_map/all_gather | solution.py:442
  55.3 0.0 copy-done.1
  55.3 0.0 copy-done.2
  55.3 0.0 copy-done.6
  55.3 1.0 shard_map.71
  56.4 0.0 collective-permute-done.2.came_ref
  56.4 24.4 %all_to_all.16.got_ref = f32[8,32,256]{2,1,0:T(8,128)S(1)} all-to-all(f32[8,32,256]{2,1,0:T(8,128)S(1)} %shard_map.72), channel_id=1, replica_groups=mesh['y'=4,'z_far'=2,'z_near'=4,'core'=2,'x'=4,'z_hi'=2] {'x','z_hi'}, dimensions={0} | all-to-all | bytes 524288 | tf_op jit(solution)/shard_map/all_to_all | solution.py:455
  80.9 0.0 copy-done.3
  80.9 0.9 shard_map.73
  81.8 7.2 %psum.7.pair_ref = f32[3,8,128]{2,1,0:T(8,128)S(1)} all-reduce(f32[3,8,128]{2,1,0:T(8,128)S(1)} %get-tuple-element.28), channel_id=1, replica_groups=mesh['y'=4,'z_far'=2,'z_near'=4,'core'=2,'x'=4,'z_hi'=2] {'core'}, use_global_device_ids=true, to_apply=%region_0.0 | all-reduce | flops 3072 | bytes 24576 | tf_op jit(solution)/shard_map/psum | solution.py:461
  89.0 23.7 %all_to_all.17 = bf16[32,16,128]{2,1,0:T(8,128)(2,1)S(1)} all-to-all(bf16[32,16,128]{2,1,0:T(8,128)(2,1)S(1)} %shard_map.74), channel_id=1, replica_groups=mesh['y'=4,'z_far'=2,'z_near'=4,'core'=2,'x'=4,'z_hi'=2] {'y','z_far','z..., dimensions={0} | all-to-all | bytes 262144 | tf_op jit(solution)/shard_map/all_to_all | solution.py:468
  112.6 5.1 %all-gather.1 = bf16[64,16,128]{2,1,0:T(8,128)(2,1)S(1)} all-gather(bf16[32,16,128]{2,1,0:T(8,128)(2,1)S(1)} %all_to_all.17), channel_id=3, replica_groups=mesh['y'=4,'z_far'=2,'z_near'=4,'core'=2,'x'=4,'z_hi'=2] {'core'}, dimensions={0}, use_global_device_ids=true | all-gather | bytes 393216 | tf_op jit(solution)/shard_map/all_gather | solution.py:469
  117.7 2.1 %shard_map.75 = (f32[32,64]{1,0:T(8,128)}, f32[32,128]{1,0:T(8,128)}, f32[2,32]{1,0:T(2,128)}) custom-call(s32[1]{0:T(128)} %bitcast.place_ref, bf16[2,32,16,128]{3,2,1,0:T(8,128)(2,1)S(1)} %bitcast.9, bf16[32,64]{1,0:T(8,128)(2,1)S(1)} %copy-done.2, bf16[32,128]{1,0:T(8,128)(2,1)S(1)} %copy-done.3, f32[2,32,32]{2,1,0:T(8,128)S(1)} %get-tuple-element.27.grams_ref, ...), custom_call_target="tpu_custom_call" | custom-call | tf_op jit(solution)/shard_map/pallas_call | solution.py:382
  (4 shorter events, 0.1 us)
Async XLA Ops:
  2.2 1.6 %copy-start = (bf16[2,64,8192]{2,1,0:T(8,128)(2,1)S(1)}, bf16[2,64,8192]{2,1,0:T(8,128)(2,1)}, u32[]{:S(2)}) copy-start(bf16[2,64,8192]{2,1,0:T(8,128)(2,1)} %param.4) | copy-start | bytes 6291460
  3.8 0.7 copy-start.5
  4.5 9.2 %copy-start.4 = (bf16[48,128]{1,0:T(8,128)(2,1)S(1)}, bf16[48,128]{1,0:T(8,128)(2,1)}, u32[]{:S(2)}) copy-start(bf16[48,128]{1,0:T(8,128)(2,1)} %get-tuple-element.23.own_ref) | copy-start | bytes 36868
  4.9 17.1 %collective-permute-start = (f32[32,32,128]{2,1,0:T(8,128)S(1)}, f32[32,32,128]{2,1,0:T(8,128)S(1)}, u32[]{:S(2)}, u32[]{:S(2)}) collective-permute-start(f32[32,32,128]{2,1,0:T(8,128)S(1)} %get-tuple-element.22), channel_id=1, source_target_pairs={{0,8},{8,0},{1,9},{9,1},{2,10},{10,2},{3,11},{11,3},{4,12},{12,4},... | collective-permute-start | bytes 1572872 | tf_op jit(solution)/shard_map/ppermute | solution.py:430
  13.7 8.3 %collective-permute-start.1 = (bf16[48,128]{1,0:T(8,128)(2,1)S(1)}, bf16[48,128]{1,0:T(8,128)(2,1)S(1)}, u32[]{:S(2)}, u32[]{:S(2)}) collective-permute-start(bf16[48,128]{1,0:T(8,128)(2,1)S(1)} %copy-done.4), channel_id=1, source_target_pairs={{0,64},{64,0},{1,65},{65,1},{2,66},{66,2},{3,67},{67,3},{4,68},{68... | collective-permute-start | bytes 36872 | tf_op jit(solution)/shard_map/ppermute | solution.py:422
  22.2 33.1 %copy-start.1 = (bf16[2,64,8192]{2,1,0:T(8,128)(2,1)S(1)}, bf16[2,64,8192]{2,1,0:T(8,128)(2,1)}, u32[]{:S(2)}) copy-start(bf16[2,64,8192]{2,1,0:T(8,128)(2,1)} %param.4) | copy-start | bytes 6291460
  22.2 33.1 %copy-start.2 = (bf16[32,64]{1,0:T(8,128)(2,1)S(1)}, bf16[32,64]{1,0:T(8,128)(2,1)}, u32[]{:S(2)}) copy-start(bf16[32,64]{1,0:T(8,128)(2,1)} %a_ref.5) | copy-start | bytes 12292
  22.3 33.1 %copy-start.6 = (bf16[32,2]{0,1:T(2,128)(2,1)S(1)}, bf16[32,2]{0,1:T(2,128)(2,1)}, u32[]{:S(2)}) copy-start(bf16[32,2]{0,1:T(2,128)(2,1)} %param.7) | copy-start | bytes 388
  44.0 12.4 %collective-permute-start.2 = (f32[32,128]{1,0:T(8,128)S(1)}, f32[32,128]{1,0:T(8,128)S(1)}, u32[]{:S(2)}, u32[]{:S(2)}) collective-permute-start(f32[32,128]{1,0:T(8,128)S(1)} %get-tuple-element.25), channel_id=1, source_target_pairs={{0,64},{64,0},{1,65},{65,1},{2,66},{66,2},{3,67},{67,3},{4,68},{68... | collective-permute-start | bytes 49160 | tf_op jit(solution)/shard_map/ppermute | solution.py:441
  51.4 29.4 %copy-start.3 = (bf16[32,128]{1,0:T(8,128)(2,1)S(1)}, bf16[32,128]{1,0:T(8,128)(2,1)}, u32[]{:S(2)}) copy-start(bf16[32,128]{1,0:T(8,128)(2,1)} %b_ref.3) | copy-start | bytes 24580

commit v4 on v3

v4 whole, which is shorter than its diff:
```python
import functools

import jax
import jax.numpy as jnp
from jax import lax
from jax.experimental import pallas as pl
from jax.experimental.pallas import tpu as pltpu
from jax.sharding import Mesh
from jax.sharding import PartitionSpec as P


f32 = jnp.float32
bf16 = jnp.bfloat16
LANES = 128
damping = 1.0
highest = lax.Precision.HIGHEST

WIDE = (4, 2, 4, 2)
NARROW = (4, 2)
NEAR = ("y", "z_near")
LINKS = ("y", "z_far", "z_near")
OTHER = ("x", "z_hi")


def mul(left, right):
    return jnp.dot(left, right, precision=highest, preferred_element_type=f32)


def mul_t(left, right):
    return lax.dot_general(
        left, right, (((1,), (1,)), ((), ())), precision=highest, preferred_element_type=f32
    )


def lane(rows, width):
    return lax.broadcasted_iota(jnp.int32, (rows, width), 1)


def columns_of(row_block):
    count, rank = row_block.shape
    eye = lax.broadcasted_iota(jnp.int32, (rank, rank), 0) == lane(rank, rank)
    return [
        jnp.sum(jnp.where(eye, row_block[k : k + 1, :], 0.0), axis=1, keepdims=True)
        for k in range(count)
    ]


def spread(square):
    rows = square.shape[0] // 4
    return jnp.concatenate([square[k * rows : (k + 1) * rows, :] for k in range(4)], axis=1)


def gather_rows(wide_block):
    width = wide_block.shape[1] // 4
    return jnp.concatenate([wide_block[:, k * width : (k + 1) * width] for k in range(4)], axis=0)


def partial_b_kernel(chunks, place_ref, t_ref, a_ref, ct_ref, keep_ref, send_ref):
    rank, _ = a_ref.shape
    factor_a = a_ref[...]
    float_a = factor_a.astype(f32)
    cols = columns_of(ct_ref[...].astype(f32))
    khatri = jnp.concatenate([col * float_a for col in cols], axis=1).astype(bf16)
    pieces = 4
    width = t_ref.shape[1] // pieces
    first_core = place_ref[0] % 2 == 0
    per = width // LANES
    for piece in range(pieces):
        part = jnp.dot(
            khatri, t_ref[:, piece * width : (piece + 1) * width], preferred_element_type=f32
        )
        for step in range(0, per, 2):
            rows = pl.ds((piece * per + step) // 2 * rank, rank)
            even = part[:, step * LANES : (step + 1) * LANES]
            odd = part[:, (step + 1) * LANES : (step + 2) * LANES]
            keep_ref[rows, :] = jnp.where(first_core, even, odd)
            send_ref[rows, :] = jnp.where(first_core, odd, even)
    gram = spread(
        lax.dot_general(
            factor_a, factor_a, (((1,), (1,)), ((), ())), preferred_element_type=f32
        )
    )
    keep_ref[chunks * rank :, :] = gram
    send_ref[chunks * rank :, :] = gram


def send_near_kernel(nears, place_ref, keep_ref, came_ref, own_ref, far_ref, out_ref):
    rank = own_ref.shape[0]
    near_z = WIDE[2]
    first_far = (place_ref[0] // 2) % 2 == 0
    own_b = own_ref[...].astype(f32)
    far_b = far_ref[...].astype(f32)
    low_b = jnp.where(first_far, own_b, far_b).astype(bf16)
    high_b = jnp.where(first_far, far_b, own_b).astype(bf16)
    last = pl.ds(2 * nears * rank, rank // 4)
    gram = keep_ref[last, :] + came_ref[last, :]
    lead = gram.astype(bf16).astype(f32)
    terms = jnp.concatenate([lead, gram - lead], axis=0).astype(bf16)
    for near in range(nears):
        y, z = divmod(near, near_z)
        for far in range(2):
            rows = pl.ds(((y * 2 + far) * near_z + z) * rank, rank)
            out_ref[near, far * rank : (far + 1) * rank, :] = (
                keep_ref[rows, :] + came_ref[rows, :]
            ).astype(bf16)
        out_ref[near, 2 * rank : 3 * rank, :] = low_b
        out_ref[near, 3 * rank : 4 * rank, :] = high_b
        out_ref[near, 4 * rank :, :] = terms


def sum_b_kernel(nears, place_ref, got_ref, a_ref, b_ref, keep_ref, send_ref, factors_ref):
    rank, _ = a_ref.shape
    slab = rank // 4
    first_far = (place_ref[0] // 2) % 2 == 0

    def summed(rows):
        total = got_ref[0, rows, :].astype(f32)
        for near in range(1, nears):
            total = total + got_ref[near, rows, :].astype(f32)
        return total

    low, high = summed(pl.ds(0, rank)), summed(pl.ds(rank, rank))
    terms = summed(pl.ds(4 * rank, 2 * slab))
    gram = terms[:slab] + terms[slab:]
    keep_ref[:rank, :] = jnp.where(first_far, low, high)
    send_ref[:rank, :] = jnp.where(first_far, high, low)
    keep_ref[rank:, :] = gram
    send_ref[rank:, :] = gram
    float_a = a_ref[...].astype(f32)
    factors_ref[:, :LANES] = b_ref[...]
    factors_ref[:, LANES:] = jnp.concatenate([float_a, float_a], axis=1).astype(bf16)


def partials_kernel(nears, others, place_ref, t_ref, a_ref, ct_ref, both_ref, tile_ref, gram_ref, whole_b):
    rank, i_local = a_ref.shape
    near_z = WIDE[2]
    for core in range(2):
        for near in range(nears):
            y, z = divmod(near, near_z)
            for far in range(2):
                start = (((y * 2 + far) * near_z + z) * 2 + core) * LANES
                whole_b[:, start : start + LANES] = both_ref[
                    core, near, far * rank : (far + 1) * rank, :
                ]
    every_b = whole_b[...]
    contracted = lax.dot_general(
        every_b, t_ref[...], (((1,), (1,)), ((), ())), preferred_element_type=f32
    )
    gram_ref[...] = lax.dot_general(
        every_b, every_b, (((1,), (1,)), ((), ())), preferred_element_type=f32
    )
    first, second = columns_of(ct_ref[...].astype(f32))
    float_a = a_ref[...].astype(f32)
    spot = lane(rank, LANES)
    low_half = spot < i_local
    scaled = contracted * jnp.where(low_half, first, second)
    part_a = scaled + pltpu.roll(scaled, i_local, 1)
    against_a = contracted * jnp.concatenate([float_a, float_a], axis=1)
    c_first = jnp.sum(jnp.where(low_half, against_a, 0.0), axis=1, keepdims=True)
    c_second = jnp.sum(jnp.where(low_half, 0.0, against_a), axis=1, keepdims=True)
    at = i_local + 2 * (place_ref[0] // 4)
    k_all = 2 * others
    tail = jnp.where(spot == at, c_first, 0.0)
    tail = jnp.where(spot == at + 1, c_second, tail)
    tail = jnp.where(spot == at + k_all, first, tail)
    tail = jnp.where(spot == at + k_all + 1, second, tail)
    tile_ref[...] = jnp.where(low_half, part_a, tail)


def send_narrow_kernel(others, keep_ref, came_ref, tile_ref, factors_ref, out_ref, gram_ref):
    rank = tile_ref.shape[0]
    total = keep_ref[...] + came_ref[...]
    gram_ref[...] = gather_rows(total[rank:])
    sum_b = total[:rank]
    tile = tile_ref[...]
    for other in range(others):
        out_ref[other, :, :LANES] = sum_b
        out_ref[other, :, LANES:] = tile


def residual_kernel(others, links, place_ref, got_ref, factors_ref, gram_a_ref, gram_b_ref, out_ref, ra_ref, rb_ref, ha_ref, hb_ref, c_ref):
    rank, i_local = ra_ref.shape
    k_all = 2 * others
    first_core = place_ref[0] % 2 == 0
    gram_a = gram_a_ref[...]
    gram_b = gram_b_ref[...]
    totals = []
    for core in range(2):
        total = got_ref[core, 0]
        for other in range(1, others):
            total = total + got_ref[core, other]
        totals.append(total)
    after = LANES + i_local
    factor_c = totals[0][:, after + k_all : after + 2 * k_all]
    part_c = totals[0][:, after : after + k_all] + totals[1][:, after : after + k_all]
    gram_c = mul_t(factor_c, factor_c)
    had_a = gram_b * gram_c
    had_b = gram_a * gram_c
    sums = [jnp.zeros((rank, 1), f32)] * 4
    cross_a = jnp.zeros((rank, rank), f32)
    cross_b = cross_a
    kept = []
    for core in range(2):
        float_b = factors_ref[core, :, :LANES].astype(f32)
        float_a = factors_ref[core, :, LANES : LANES + i_local].astype(f32)
        own = []
        for mttkrp, factor, had in (
            (totals[core][:, LANES:after], float_a, had_a),
            (totals[core][:, :LANES], float_b, had_b),
        ):
            res = mttkrp - mul(had, factor)
            once = mul(had, res)
            twice = mul(had, once)
            own += [res, once]
            pairs = ((res, res), (res, once), (once, once), (once, twice))
            sums = [
                old + jnp.sum(left * right, axis=1, keepdims=True)
                for old, (left, right) in zip(sums, pairs)
            ]
        cross_a = cross_a + mul_t(float_a, own[0])
        cross_b = cross_b + mul_t(float_b, own[2])
        kept.append(own)
    for ref, one, two in zip((ra_ref, ha_ref, rb_ref, hb_ref), *kept):
        ref[...] = jnp.where(first_core, one, two)
    c_ref[...] = factor_c
    last = spread(
        jnp.concatenate(
            [part_c, *sums, jnp.zeros((rank, rank - k_all - len(sums)), f32)], axis=1
        )
    )
    lead = last.astype(bf16).astype(f32)
    cross = jnp.where(first_core, spread(cross_a), spread(cross_b))
    tail = jnp.where(first_core, lead, last - lead)
    packed = jnp.concatenate([cross, tail], axis=0).astype(bf16)
    for link in range(links):
        out_ref[link] = packed


def step_kernel(others, place_ref, all_ref, a_ref, b_ref, gram_a_ref, gram_b_ref, ra_ref, rb_ref, ha_ref, hb_ref, c_ref, sa_ref, sb_ref, sc_ref):
    rank, _ = a_ref.shape
    k_all = 2 * others
    sums = []
    for core in range(2):
        total_sum = all_ref[core, 0].astype(f32)
        for link in range(1, all_ref.shape[1]):
            total_sum = total_sum + all_ref[core, link].astype(f32)
        sums.append(total_sum)
    slab = rank // 4
    cross_a = gather_rows(sums[0][:slab])
    cross_b = gather_rows(sums[1][:slab])
    last = gather_rows(sums[0][slab:] + sums[1][slab:])
    mttkrp_c = last[:, :k_all]
    gram_a = gram_a_ref[...]
    gram_b = gram_b_ref[...]
    factor_c = c_ref[...]
    gram_c = mul_t(factor_c, factor_c)
    had_a = gram_b * gram_c
    had_b = gram_a * gram_c
    had_c = gram_a * gram_b
    res_c = mttkrp_c - mul(had_c, factor_c)
    once_c = mul(had_c, res_c)
    twice_c = mul(had_c, once_c)
    cross_c = mul_t(factor_c, res_c)

    def total(value):
        return jnp.sum(jnp.sum(value, axis=1, keepdims=True), axis=0, keepdims=True)

    own = [
        total(res_c * res_c),
        total(res_c * once_c),
        total(once_c * once_c),
        total(once_c * twice_c),
    ]
    p0, p1, p2, p3 = [
        total(last[:, k_all + k : k_all + k + 1]) + own[k] for k in range(4)
    ]

    def mixed(xa, xb, xc):
        return (
            xb * gram_c + gram_b * xc,
            xa * gram_c + gram_a * xc,
            xa * gram_b + gram_a * xb,
        )

    eye = (
        lax.broadcasted_iota(jnp.int32, (rank, rank), 0) == lane(rank, rank)
    ).astype(f32)
    grams = (gram_a, gram_b, gram_c)
    shifted = tuple(had + damping * eye for had in (had_a, had_b, had_c))
    crosses = (cross_a, cross_b, cross_c)
    mix = mixed(*crosses)
    mix_gram = [mul(m, g) for m, g in zip(mix, grams)]
    turned = [mul_t(s, x) for s, x in zip(shifted, crosses)]
    twice_turned = [mul(s, t) for s, t in zip(shifted, turned)]
    shifted_mix = [mul(s, m) for s, m in zip(shifted, mix)]
    image_cross_t = [t + mg for t, mg in zip(turned, mix_gram)]
    image_cross = [
        mul(x, s) + mul_t(g, m) for x, s, g, m in zip(crosses, shifted, grams, mix)
    ]
    image_mix = mixed(*image_cross)
    one = damping
    c0 = p0
    k1 = p1 + one * p0
    k2 = p2 + 2.0 * one * p1 + one * one * p0
    k3 = p3 + 3.0 * one * p2 + 3.0 * one * one * p1 + one * one * one * p0
    c1 = k1
    c2 = k2
    c3 = k3
    crosses_t = [mul_t(eye, x) for x in crosses]
    c1 = c1 + total(sum(m * xt for m, xt in zip(mix, crosses_t)))
    c2 = c2 + total(
        sum(2.0 * m * t + mg * m for m, t, mg in zip(mix, turned, mix_gram))
    )
    c3 = c3 + total(
        sum(
            2.0 * m * tt + mg * sm + im * ict
            for m, tt, mg, sm, im, ict in zip(
                mix, twice_turned, mix_gram, shifted_mix, image_mix, image_cross_t
            )
        )
    )
    alpha = c0 / c1
    fresh = c0 - 2.0 * alpha * c1 + alpha * alpha * c2
    beta = fresh / c0
    keep = 1.0 + beta
    curvature = keep * keep * c1 - 2.0 * keep * alpha * c2 + alpha * alpha * c3
    second = fresh / curvature
    on_res = alpha + second * keep
    on_image = -second * alpha
    float_a = a_ref[...].astype(f32)
    float_b = b_ref[...].astype(f32)
    res_a = ra_ref[...]
    res_b = rb_ref[...]
    image_a = damping * res_a + ha_ref[...] + mul(mix[0], float_a)
    image_b = damping * res_b + hb_ref[...] + mul(mix[1], float_b)
    image_c = damping * res_c + once_c + mul(mix[2], factor_c)
    sa_ref[...] = on_res * res_a + on_image * image_a
    sb_ref[...] = on_res * res_b + on_image * image_b
    step_c = on_res * res_c + on_image * image_c
    at = 2 * (place_ref[0] // 4)
    spot = lane(rank, k_all)
    square = lax.broadcasted_iota(jnp.int32, (rank, rank), 0) == lane(rank, rank)
    for k in range(2):
        column = jnp.sum(jnp.where(spot == at + k, step_c, 0.0), axis=1, keepdims=True)
        sc_ref[k : k + 1, :] = jnp.sum(jnp.where(square, column, 0.0), axis=0, keepdims=True)


def call(kernel, out_shape, operands, scalar=False, scratch=()):
    vmem = pl.BlockSpec(memory_space=pltpu.VMEM)
    specs = [vmem] * len(operands)
    if scalar:
        specs[0] = pl.BlockSpec(memory_space=pltpu.SMEM)
    outs = out_shape if isinstance(out_shape, tuple) else (out_shape,)
    result = pl.pallas_call(
        kernel,
        out_shape=outs,
        in_specs=specs,
        out_specs=tuple(vmem for _ in outs),
        scratch_shapes=list(scratch),
        compiler_params=pltpu.CompilerParams(vmem_limit_bytes=16 << 20),
    )(*operands)
    return result if isinstance(out_shape, tuple) else result[0]


def stages(tensor, factor_a, factor_b, factor_c):
    k_local, i_local, j_whole = tensor.shape
    rank = factor_a.shape[0]
    chunks = j_whole // (2 * LANES)
    nears = chunks // 2
    others = lax.axis_size(OTHER)
    like = jax.ShapeDtypeStruct
    flattened = tensor.reshape(k_local * i_local, j_whole)
    turned_c = factor_c.T
    place = (
        lax.axis_index("core") + 2 * lax.axis_index("z_far") + 4 * lax.axis_index(OTHER)
    ).astype(jnp.int32).reshape(1)
    half = rank // 2
    square = like((rank, LANES), f32)
    thin = like((rank, i_local), f32)

    slab = rank // 4
    far = lax.ppermute(factor_b, "z_far", [(0, 1), (1, 0)])
    rows = like((chunks * rank + slab, LANES), f32)
    keep, send = call(
        functools.partial(partial_b_kernel, chunks),
        (rows, rows),
        (place, flattened, factor_a, turned_c),
        scalar=True,
    )
    came = lax.ppermute(send, "core", [(0, 1), (1, 0)])
    near = call(
        functools.partial(send_near_kernel, nears),
        like((nears, 4 * rank + half, LANES), bf16),
        (place, keep, came, factor_b, far),
        scalar=True,
    )
    near = lax.all_to_all(near, NEAR, 0, 0, tiled=True)
    rows = like((rank + slab, LANES), f32)
    keep, send, factors = call(
        functools.partial(sum_b_kernel, nears),
        (rows, rows, like((rank, 2 * LANES), bf16)),
        (place, near, factor_a, factor_b),
        scalar=True,
    )
    came = lax.ppermute(send, "z_far", [(0, 1), (1, 0)])
    both = lax.all_gather(near[:, 2 * rank : 4 * rank, :], "core", axis=0, tiled=False)
    tile, gram_b = call(
        functools.partial(partials_kernel, nears, others),
        (square, like((rank, rank), f32)),
        (place, flattened, factor_a, turned_c, both),
        scalar=True,
        scratch=(pltpu.VMEM((rank, j_whole), bf16),),
    )
    factors = lax.all_gather(factors, "core", axis=0, tiled=False)
    narrow, gram_a = call(
        functools.partial(send_narrow_kernel, others),
        (like((others, rank, 2 * LANES), f32), like((rank, rank), f32)),
        (keep, came, tile, factors),
    )
    narrow = lax.all_to_all(narrow, OTHER, 0, 0, tiled=True)
    narrow = lax.all_gather(narrow, "core", axis=0, tiled=False)
    send, res_a, res_b, once_a, once_b, whole_c = call(
        functools.partial(residual_kernel, others, chunks),
        (like((chunks, half, LANES), bf16), thin, square, thin, square, like((rank, 2 * others), f32)),
        (place, narrow, factors, gram_a, gram_b),
        scalar=True,
    )
    send = lax.all_to_all(send, LINKS, 0, 0, tiled=True)
    every = lax.all_gather(send, "core", axis=0, tiled=False)
    step_a, step_b, turned_step_c = call(
        functools.partial(step_kernel, others),
        (thin, square, like((k_local, rank), f32)),
        (place, every, factor_a, factor_b, gram_a, gram_b, res_a, res_b, once_a, once_b, whole_c),
        scalar=True,
    )
    return step_a, step_b, turned_step_c.T


def solution(mesh):
    wide = ("y", "z_far", "z_near", "core")
    inner = Mesh(mesh.devices.reshape(WIDE + NARROW), wide + OTHER)
    return jax.shard_map(
        stages,
        mesh=inner,
        in_specs=(P(OTHER, wide, None), P(None, wide), P(None, wide), P(None, OTHER)),
        out_specs=(P(None, wide), P(None, wide), P(None, OTHER)),
        check_vma=False,
    )
```

time: 120 us -> 120 us (level)
    psum x1 -> x0, blocking collectives: 7.18 us -> none  [stages(): send = lax.psum(send, 'core')]
    all_gather x1 -> x3, blocking collectives: 3.9 us -> 9.79 us  [the longest x1 4.13 us: stages(): narrow = lax.all_gather(narrow, 'core', axis=0, tiled=False)]
    all_to_all x1, blocking collectives: 23.7 us -> 24.9 us  [stages(): send = lax.all_to_all(send, LINKS, 0, 0, tiled=True)]
    pallas_call x9 -> x7, Pallas kernels: 6.35 us -> 5.51 us  [call(): pl.pallas_call(kernel, out_shape=outs, in_specs=specs, out_specs=tuple((v...]
    unnamed x14 -> x10, local copies, waits for them, and re-layouts: 2.31 us -> 2.95 us
where the time goes in v4:
time: 120 us
  blocking collectives  86.3 us (72%)
  starting transfers between devices  19.5 us (16%)
  Pallas kernels  5.51 us (5%)
  waiting for transfers between devices  4.83 us (4%)
  local copies, waits for them, and re-layouts  2.96 us (2%)
    all_to_all x1, blocking collectives, stages(): send = lax.all_to_all(send, LINKS, 0, 0, tiled=True)  24.9 us
    all_to_all x1, blocking collectives, stages(): narrow = lax.all_to_all(narrow, OTHER, 0, 0, tiled=True)  24.8 us
    all_to_all x1, blocking collectives, stages(): near = lax.all_to_all(near, NEAR, 0, 0, tiled=True)  21.7 us
    ppermute x1, starting transfers between devices, stages(): came = lax.ppermute(send, 'core', [(0, 1), (1, 0)])  8.75 us
    ppermute x1, starting transfers between devices, stages(): came = lax.ppermute(send, 'z_far', [(0, 1), (1, 0)])  7.27 us
    pallas_call x7, Pallas kernels, call(): pl.pallas_call(kernel, out_shape=outs, in_specs=specs, out_specs=tuple((v...  5.51 us
    all_gather x1, blocking collectives, stages(): every = lax.all_gather(send, 'core', axis=0, tiled=False)  5.09 us
    ppermute x1, waiting for transfers between devices, stages(): far = lax.ppermute(factor_b, 'z_far', [(0, 1), (1, 0)])  4.82 us
  transfers between devices with their start and end apart: 3, of which 1 were waited for; matrix products, arithmetic and copies ran while one was open for 0% of the time, Pallas kernels for 1%

profile of v4, /device:TPU:1, one launch (start us, length us, event | category | flops | bytes accessed | tf_op | source)
XLA Modules:
  0.0 119.8 jit_solution(6585540877731860723)
XLA Ops:
  0.6 0.0 copy-start.3
  0.7 0.0 copy-start
  0.7 1.6 %copy-done = bf16[2,64,8192]{2,1,0:T(8,128)(2,1)S(1)} copy-done((bf16[2,64,8192]{2,1,0:T(8,128)(2,1)S(1)}, bf16[2,64,8192]{2,1,0:T(8,128)(2,1)}, u32[]{:S(2)}) %copy-start) | copy-done | bytes 2097176
  2.2 0.0 copy-start.2
  2.2 0.7 copy-done.2
  2.9 0.0 copy-start.4
  2.9 0.7 copy-done.4
  3.6 0.6 shard_map.67
  4.2 8.8 %collective-permute-start = (f32[1032,128]{1,0:T(8,128)S(1)}, f32[1032,128]{1,0:T(8,128)S(1)}, u32[]{:S(2)}, u32[]{:S(2)}) collective-permute-start(f32[1032,128]{1,0:T(8,128)S(1)} %get-tuple-element.22), channel_id=1, source_target_pairs={{0,8},{8,0},{1,9},{9,1},{2,10},{10,2},{3,11},{11,3},{4,12},{12,4},... | collective-permute-start | bytes 1585160 | tf_op jit(solution)/shard_map/ppermute | solution.py:390
  13.0 0.0 copy-done.3
  13.0 3.5 %collective-permute-start.1 = (bf16[32,128]{1,0:T(8,128)(2,1)S(1)}, bf16[32,128]{1,0:T(8,128)(2,1)S(1)}, u32[]{:S(2)}, u32[]{:S(2)}) collective-permute-start(bf16[32,128]{1,0:T(8,128)(2,1)S(1)} %copy-done.3), channel_id=1, source_target_pairs={{0,64},{64,0},{1,65},{65,1},{2,66},{66,2},{3,67},{67,3},{4,68},{68... | collective-permute-start | bytes 24584 | tf_op jit(solution)/shard_map/ppermute | solution.py:382
  16.5 4.8 %collective-permute-done.1.far_ref = bf16[32,128]{1,0:T(8,128)(2,1)S(1)} collective-permute-done((bf16[32,128]{1,0:T(8,128)(2,1)S(1)}, bf16[32,128]{1,0:T(8,128)(2,1)S(1)}, u32[]{:S(2)}, u32[]{:S(2)}) %collective-permute-start.1) | collective-permute-done | bytes 8224 | tf_op jit(solution)/shard_map/ppermute | solution.py:382
  21.3 0.0 collective-permute-done.came_ref
  21.3 0.0 copy-start.1
  21.3 0.1 shard_map.68
  21.4 21.7 %all_to_all.15.got_ref = bf16[16,144,128]{2,1,0:T(8,128)(2,1)S(1)} all-to-all(bf16[16,144,128]{2,1,0:T(8,128)(2,1)S(1)} %shard_map.68), channel_id=1, replica_groups=mesh['y'=4,'z_far'=2,'z_near'=4,'core'=2,'x'=4,'z_hi'=2] {'y','z_near'}, dimensions={0} | all-to-all | bytes 1179648 | tf_op jit(solution)/shard_map/all_to_all | solution.py:397
  43.0 0.1 shard_map.69
  43.1 7.3 %collective-permute-start.2 = (f32[40,128]{1,0:T(8,128)S(1)}, f32[40,128]{1,0:T(8,128)S(1)}, u32[]{:S(2)}, u32[]{:S(2)}) collective-permute-start(f32[40,128]{1,0:T(8,128)S(1)} %get-tuple-element.24), channel_id=1, source_target_pairs={{0,64},{64,0},{1,65},{65,1},{2,66},{66,2},{3,67},{67,3},{4,68},{68... | collective-permute-start | bytes 61448 | tf_op jit(solution)/shard_map/ppermute | solution.py:405
  50.4 3.8 %all-gather = bf16[32,64,128]{2,1,0:T(8,128)(2,1)S(1)} all-gather(bf16[16,64,128]{2,1,0:T(8,128)(2,1)S(1)} %slice.4), channel_id=2, replica_groups=mesh['y'=4,'z_far'=2,'z_near'=4,'core'=2,'x'=4,'z_hi'=2] {'core'}, dimensions={0}, use_global_device_ids=true | all-gather | bytes 786432 | tf_op jit(solution)/shard_map/all_gather | solution.py:406
  54.2 0.0 copy-done.1
  54.2 1.0 shard_map.70
  55.3 1.9 %all-gather.1 = bf16[64,256]{1,0:T(8,128)(2,1)S(1)} all-gather(bf16[32,256]{1,0:T(8,128)(2,1)S(1)} %get-tuple-element.26), channel_id=3, replica_groups=mesh['y'=4,'z_far'=2,'z_near'=4,'core'=2,'x'=4,'z_hi'=2] {'core'}, dimensions={0}, use_global_device_ids=true | all-gather | bytes 49152 | tf_op jit(solution)/shard_map/all_gather | solution.py:414
  57.1 0.0 collective-permute-done.2.came_ref
  57.1 0.1 shard_map.71
  57.2 24.8 %all_to_all.16 = f32[8,32,256]{2,1,0:T(8,128)S(1)} all-to-all(f32[8,32,256]{2,1,0:T(8,128)S(1)} %get-tuple-element.27), channel_id=1, replica_groups=mesh['y'=4,'z_far'=2,'z_near'=4,'core'=2,'x'=4,'z_hi'=2] {'x','z_hi'}, dimensions={0} | all-to-all | bytes 524288 | tf_op jit(solution)/shard_map/all_to_all | solution.py:420
  82.0 4.1 %all-gather.2 = f32[16,32,256]{2,1,0:T(8,128)S(1)} all-gather(f32[8,32,256]{2,1,0:T(8,128)S(1)} %all_to_all.16), channel_id=4, replica_groups=mesh['y'=4,'z_far'=2,'z_near'=4,'core'=2,'x'=4,'z_hi'=2] {'core'}, dimensions={0}, use_global_device_ids=true | all-gather | bytes 786432 | tf_op jit(solution)/shard_map/all_gather | solution.py:421
  86.2 1.5 %shard_map.72 = (bf16[32,16,128]{2,1,0:T(8,128)(2,1)S(1)}, f32[32,64]{1,0:T(8,128)S(1)}, f32[32,128]{1,0:T(8,128)S(1)}, f32[32,64]{1,0:T(8,128)S(1)}, f32[32,128]{1,0:T(8,128)S(1)}, /*index=5*/f32[32,16]{1,0:T(8,128)S(1)}) custom-call(s32[1]{0:T(128)} %bitcast.place_ref, f32[2,8,32,256]{3,2,1,0:T(8,128)S(1)} %bitcast.11, bf16[2,32,256]{2,1,0:T(8,128)(2,1)S(1)} %bitcast.14, ...), custom_call_target="tpu_custom_call" | custom-call | tf_op jit(solution)/shard_map/pallas_call | solution.py:354
  87.7 24.9 %all_to_all.17 = bf16[32,16,128]{2,1,0:T(8,128)(2,1)S(1)} all-to-all(bf16[32,16,128]{2,1,0:T(8,128)(2,1)S(1)} %get-tuple-element.30), channel_id=1, replica_groups=mesh['y'=4,'z_far'=2,'z_near'=4,'core'=2,'x'=4,'z_hi'=2] {'y','z_far','z..., dimensions={0} | all-to-all | bytes 262144 | tf_op jit(solution)/shard_map/all_to_all | solution.py:428
  112.6 5.1 %all-gather.3 = bf16[64,16,128]{2,1,0:T(8,128)(2,1)S(1)} all-gather(bf16[32,16,128]{2,1,0:T(8,128)(2,1)S(1)} %all_to_all.17), channel_id=5, replica_groups=mesh['y'=4,'z_far'=2,'z_near'=4,'core'=2,'x'=4,'z_hi'=2] {'core'}, dimensions={0}, use_global_device_ids=true | all-gather | bytes 393216 | tf_op jit(solution)/shard_map/all_gather | solution.py:429
  117.7 2.1 %shard_map.73 = (f32[32,64]{1,0:T(8,128)}, f32[32,128]{1,0:T(8,128)}, f32[2,32]{1,0:T(2,128)}) custom-call(s32[1]{0:T(128)} %bitcast.place_ref, bf16[2,32,16,128]{3,2,1,0:T(8,128)(2,1)S(1)} %bitcast.12, bf16[32,64]{1,0:T(8,128)(2,1)S(1)} %copy-done.2, bf16[32,128]{1,0:T(8,128)(2,1)S(1)} %copy-done.3, f32[32,32]{1,0:T(8,128)S(1)} %get-tuple-element.28.gram_a_ref, ...), custom_call_target="tpu_custom_call" | custom-call | tf_op jit(solution)/shard_map/pallas_call | solution.py:354
  (1 shorter events, 0.0 us)
Async XLA Ops:
  0.6 12.3 %copy-start.3 = (bf16[32,128]{1,0:T(8,128)(2,1)S(1)}, bf16[32,128]{1,0:T(8,128)(2,1)}, u32[]{:S(2)}) copy-start(bf16[32,128]{1,0:T(8,128)(2,1)} %b_ref.3) | copy-start | bytes 24580
  0.7 1.6 %copy-start = (bf16[2,64,8192]{2,1,0:T(8,128)(2,1)S(1)}, bf16[2,64,8192]{2,1,0:T(8,128)(2,1)}, u32[]{:S(2)}) copy-start(bf16[2,64,8192]{2,1,0:T(8,128)(2,1)} %param.4) | copy-start | bytes 6291460
  2.2 0.7 copy-start.2
  2.9 0.7 copy-start.4
  4.2 17.1 %collective-permute-start = (f32[1032,128]{1,0:T(8,128)S(1)}, f32[1032,128]{1,0:T(8,128)S(1)}, u32[]{:S(2)}, u32[]{:S(2)}) collective-permute-start(f32[1032,128]{1,0:T(8,128)S(1)} %get-tuple-element.22), channel_id=1, source_target_pairs={{0,8},{8,0},{1,9},{9,1},{2,10},{10,2},{3,11},{11,3},{4,12},{12,4},... | collective-permute-start | bytes 1585160 | tf_op jit(solution)/shard_map/ppermute | solution.py:390
  13.0 8.3 %collective-permute-start.1 = (bf16[32,128]{1,0:T(8,128)(2,1)S(1)}, bf16[32,128]{1,0:T(8,128)(2,1)S(1)}, u32[]{:S(2)}, u32[]{:S(2)}) collective-permute-start(bf16[32,128]{1,0:T(8,128)(2,1)S(1)} %copy-done.3), channel_id=1, source_target_pairs={{0,64},{64,0},{1,65},{65,1},{2,66},{66,2},{3,67},{67,3},{4,68},{68... | collective-permute-start | bytes 24584 | tf_op jit(solution)/shard_map/ppermute | solution.py:382
  21.3 33.0 %copy-start.1 = (bf16[2,64,8192]{2,1,0:T(8,128)(2,1)S(1)}, bf16[2,64,8192]{2,1,0:T(8,128)(2,1)}, u32[]{:S(2)}) copy-start(bf16[2,64,8192]{2,1,0:T(8,128)(2,1)} %param.4) | copy-start | bytes 6291460
  43.1 14.0 %collective-permute-start.2 = (f32[40,128]{1,0:T(8,128)S(1)}, f32[40,128]{1,0:T(8,128)S(1)}, u32[]{:S(2)}, u32[]{:S(2)}) collective-permute-start(f32[40,128]{1,0:T(8,128)S(1)} %get-tuple-element.24), channel_id=1, source_target_pairs={{0,64},{64,0},{1,65},{65,1},{2,66},{66,2},{3,67},{67,3},{4,68},{68... | collective-permute-start | bytes 61448 | tf_op jit(solution)/shard_map/ppermute | solution.py:405

commit v5 on v4

--- a/solution.py
+++ b/solution.py
@@ -75,13 +75,16 @@
             odd = part[:, (step + 1) * LANES : (step + 2) * LANES]
             keep_ref[rows, :] = jnp.where(first_core, even, odd)
             send_ref[rows, :] = jnp.where(first_core, odd, even)
-    gram = spread(
-        lax.dot_general(
-            factor_a, factor_a, (((1,), (1,)), ((), ())), preferred_element_type=f32
-        )
-    )
-    keep_ref[chunks * rank :, :] = gram
-    send_ref[chunks * rank :, :] = gram
+    gram = lax.dot_general(
+        factor_a, factor_a, (((1,), (1,)), ((), ())), preferred_element_type=f32
+    )
+    slab = rank // 4
+    blocks = [gram[k * slab : (k + 1) * slab, :] for k in range(4)]
+    blank = jnp.zeros((slab, 2 * rank), f32)
+    even = jnp.concatenate([blocks[0], blocks[1], blank], axis=1)
+    odd = jnp.concatenate([blocks[2], blocks[3], blank], axis=1)
+    keep_ref[chunks * rank :, :] = jnp.where(first_core, even, odd)
+    send_ref[chunks * rank :, :] = jnp.where(first_core, odd, even)
 
 
 def send_near_kernel(nears, place_ref, keep_ref, came_ref, own_ref, far_ref, out_ref):
@@ -93,9 +96,9 @@
     low_b = jnp.where(first_far, own_b, far_b).astype(bf16)
     high_b = jnp.where(first_far, far_b, own_b).astype(bf16)
     last = pl.ds(2 * nears * rank, rank // 4)
-    gram = keep_ref[last, :] + came_ref[last, :]
+    gram = keep_ref[last, : 2 * rank] + came_ref[last, : 2 * rank]
     lead = gram.astype(bf16).astype(f32)
-    terms = jnp.concatenate([lead, gram - lead], axis=0).astype(bf16)
+    terms = jnp.concatenate([lead, gram - lead], axis=1).astype(bf16)
     for near in range(nears):
         y, z = divmod(near, near_z)
         for far in range(2):
@@ -120,8 +123,9 @@
         return total
 
     low, high = summed(pl.ds(0, rank)), summed(pl.ds(rank, rank))
-    terms = summed(pl.ds(4 * rank, 2 * slab))
-    gram = terms[:slab] + terms[slab:]
+    terms = summed(pl.ds(4 * rank, slab))
+    gram = terms[:, : 2 * rank] + terms[:, 2 * rank :]
+    gram = jnp.concatenate([gram, jnp.zeros((slab, LANES - 2 * rank), f32)], axis=1)
     keep_ref[:rank, :] = jnp.where(first_far, low, high)
     send_ref[:rank, :] = jnp.where(first_far, high, low)
     keep_ref[rank:, :] = gram
@@ -167,22 +171,24 @@
     tile_ref[...] = jnp.where(low_half, part_a, tail)
 
 
-def send_narrow_kernel(others, keep_ref, came_ref, tile_ref, factors_ref, out_ref, gram_ref):
+def send_narrow_kernel(others, place_ref, keep_ref, came_ref, tile_ref, factors_ref, out_ref):
     rank = tile_ref.shape[0]
     total = keep_ref[...] + came_ref[...]
-    gram_ref[...] = gather_rows(total[rank:])
     sum_b = total[:rank]
-    tile = tile_ref[...]
+    gram = jnp.concatenate([total[rank:, :rank], total[rank:, rank : 2 * rank]], axis=0)
+    gram = jnp.where(place_ref[0] // 4 == 0, gram, 0.0)
+    gram = jnp.concatenate([gram, jnp.zeros((rank // 2, rank), f32)], axis=0)
+    gram = jnp.concatenate([jnp.zeros((rank, LANES - rank), f32), gram], axis=1)
+    tile = tile_ref[...] + gram
     for other in range(others):
         out_ref[other, :, :LANES] = sum_b
         out_ref[other, :, LANES:] = tile
 
 
-def residual_kernel(others, links, place_ref, got_ref, factors_ref, gram_a_ref, gram_b_ref, out_ref, ra_ref, rb_ref, ha_ref, hb_ref, c_ref):
+def residual_kernel(others, links, place_ref, got_ref, factors_ref, gram_b_ref, out_ref, ra_ref, rb_ref, ha_ref, hb_ref, c_ref, model_c_ref, gram_a_ref, gram_c_ref):
     rank, i_local = ra_ref.shape
     k_all = 2 * others
     first_core = place_ref[0] % 2 == 0
-    gram_a = gram_a_ref[...]
     gram_b = gram_b_ref[...]
     totals = []
     for core in range(2):
@@ -194,8 +200,14 @@
     factor_c = totals[0][:, after + k_all : after + 2 * k_all]
     part_c = totals[0][:, after : after + k_all] + totals[1][:, after : after + k_all]
     gram_c = mul_t(factor_c, factor_c)
+    gram_a = jnp.concatenate(
+        [total[: rank // 2, 2 * LANES - rank :] for total in totals], axis=0
+    )
     had_a = gram_b * gram_c
     had_b = gram_a * gram_c
+    gram_a_ref[...] = gram_a
+    gram_c_ref[...] = gram_c
+    model_c_ref[...] = mul(gram_a * gram_b, factor_c)
     sums = [jnp.zeros((rank, 1), f32)] * 4
     cross_a = jnp.zeros((rank, rank), f32)
     cross_b = cross_a
@@ -236,7 +248,7 @@
         out_ref[link] = packed
 
 
-def step_kernel(others, place_ref, all_ref, a_ref, b_ref, gram_a_ref, gram_b_ref, ra_ref, rb_ref, ha_ref, hb_ref, c_ref, sa_ref, sb_ref, sc_ref):
+def step_kernel(others, place_ref, all_ref, a_ref, b_ref, gram_a_ref, gram_b_ref, ra_ref, rb_ref, ha_ref, hb_ref, c_ref, model_c_ref, gram_c_ref, sa_ref, sb_ref, sc_ref):
     rank, _ = a_ref.shape
     k_all = 2 * others
     sums = []
@@ -253,11 +265,11 @@
     gram_a = gram_a_ref[...]
     gram_b = gram_b_ref[...]
     factor_c = c_ref[...]
-    gram_c = mul_t(factor_c, factor_c)
+    gram_c = gram_c_ref[...]
     had_a = gram_b * gram_c
     had_b = gram_a * gram_c
     had_c = gram_a * gram_b
-    res_c = mttkrp_c - mul(had_c, factor_c)
+    res_c = mttkrp_c - model_c_ref[...]
     once_c = mul(had_c, res_c)
     twice_c = mul(had_c, once_c)
     cross_c = mul_t(factor_c, res_c)
@@ -390,7 +402,7 @@
     came = lax.ppermute(send, "core", [(0, 1), (1, 0)])
     near = call(
         functools.partial(send_near_kernel, nears),
-        like((nears, 4 * rank + half, LANES), bf16),
+        like((nears, 4 * rank + slab, LANES), bf16),
         (place, keep, came, factor_b, far),
         scalar=True,
     )
@@ -412,17 +424,20 @@
         scratch=(pltpu.VMEM((rank, j_whole), bf16),),
     )
     factors = lax.all_gather(factors, "core", axis=0, tiled=False)
-    narrow, gram_a = call(
+    narrow = call(
         functools.partial(send_narrow_kernel, others),
-        (like((others, rank, 2 * LANES), f32), like((rank, rank), f32)),
-        (keep, came, tile, factors),
+        like((others, rank, 2 * LANES), f32),
+        (place, keep, came, tile, factors),
+        scalar=True,
     )
     narrow = lax.all_to_all(narrow, OTHER, 0, 0, tiled=True)
     narrow = lax.all_gather(narrow, "core", axis=0, tiled=False)
-    send, res_a, res_b, once_a, once_b, whole_c = call(
+    low = like((rank, 2 * others), f32)
+    gram = like((rank, rank), f32)
+    send, res_a, res_b, once_a, once_b, whole_c, model_c, gram_a, gram_c = call(
         functools.partial(residual_kernel, others, chunks),
-        (like((chunks, half, LANES), bf16), thin, square, thin, square, like((rank, 2 * others), f32)),
-        (place, narrow, factors, gram_a, gram_b),
+        (like((chunks, half, LANES), bf16), thin, square, thin, square, low, low, gram, gram),
+        (place, narrow, factors, gram_b),
         scalar=True,
     )
     send = lax.all_to_all(send, LINKS, 0, 0, tiled=True)
@@ -430,7 +445,7 @@
     step_a, step_b, turned_step_c = call(
         functools.partial(step_kernel, others),
         (thin, square, like((k_local, rank), f32)),
-        (place, every, factor_a, factor_b, gram_a, gram_b, res_a, res_b, once_a, once_b, whole_c),
+        (place, every, factor_a, factor_b, gram_a, gram_b, res_a, res_b, once_a, once_b, whole_c, model_c, gram_c),
         scalar=True,
     )
     return step_a, step_b, turned_step_c.T

time: 120 us -> 120 us (level)
  no operation moved by 1% of the time
where the time goes in v5:
time: 120 us; the launch traced here: 119 us
  blocking collectives  85.5 us (71%)
  starting transfers between devices  19.5 us (16%)
  Pallas kernels  5.63 us (5%)
  waiting for transfers between devices  4.83 us (4%)
  local copies, waits for them, and re-layouts  2.96 us (2%)
    all_to_all x1, blocking collectives, stages(): narrow = lax.all_to_all(narrow, OTHER, 0, 0, tiled=True)  24.8 us
    all_to_all x1, blocking collectives, stages(): send = lax.all_to_all(send, LINKS, 0, 0, tiled=True)  24.7 us
    all_to_all x1, blocking collectives, stages(): near = lax.all_to_all(near, NEAR, 0, 0, tiled=True)  21 us
    ppermute x1, starting transfers between devices, stages(): came = lax.ppermute(send, 'core', [(0, 1), (1, 0)])  8.75 us
    ppermute x1, starting transfers between devices, stages(): came = lax.ppermute(send, 'z_far', [(0, 1), (1, 0)])  7.27 us
    pallas_call x7, Pallas kernels, call(): pl.pallas_call(kernel, out_shape=outs, in_specs=specs, out_specs=tuple((v...  5.63 us
    all_gather x1, blocking collectives, stages(): every = lax.all_gather(send, 'core', axis=0, tiled=False)  5.09 us
    ppermute x1, waiting for transfers between devices, stages(): far = lax.ppermute(factor_b, 'z_far', [(0, 1), (1, 0)])  4.82 us
  transfers between devices with their start and end apart: 3, of which 1 were waited for; matrix products, arithmetic and copies ran while one was open for 0% of the time, Pallas kernels for 1%

profile of v5, /device:TPU:1, one launch (start us, length us, event | category | flops | bytes accessed | tf_op | source)
XLA Modules:
  0.0 119.1 jit_solution(9804588832416885932)
XLA Ops:
  0.6 0.0 copy-start.3
  0.7 0.0 copy-start
  0.7 1.6 %copy-done = bf16[2,64,8192]{2,1,0:T(8,128)(2,1)S(1)} copy-done((bf16[2,64,8192]{2,1,0:T(8,128)(2,1)S(1)}, bf16[2,64,8192]{2,1,0:T(8,128)(2,1)}, u32[]{:S(2)}) %copy-start) | copy-done | bytes 2097176
  2.2 0.0 copy-start.2
  2.2 0.7 copy-done.2
  2.9 0.0 copy-start.4
  2.9 0.7 copy-done.4
  3.6 0.6 shard_map.67
  4.2 8.7 %collective-permute-start = (f32[1032,128]{1,0:T(8,128)S(1)}, f32[1032,128]{1,0:T(8,128)S(1)}, u32[]{:S(2)}, u32[]{:S(2)}) collective-permute-start(f32[1032,128]{1,0:T(8,128)S(1)} %get-tuple-element.23), channel_id=1, source_target_pairs={{0,8},{8,0},{1,9},{9,1},{2,10},{10,2},{3,11},{11,3},{4,12},{12,4},... | collective-permute-start | bytes 1585160 | tf_op jit(solution)/shard_map/ppermute | solution.py:402
  13.0 0.0 copy-done.3
  13.0 3.5 %collective-permute-start.1 = (bf16[32,128]{1,0:T(8,128)(2,1)S(1)}, bf16[32,128]{1,0:T(8,128)(2,1)S(1)}, u32[]{:S(2)}, u32[]{:S(2)}) collective-permute-start(bf16[32,128]{1,0:T(8,128)(2,1)S(1)} %copy-done.3), channel_id=1, source_target_pairs={{0,64},{64,0},{1,65},{65,1},{2,66},{66,2},{3,67},{67,3},{4,68},{68... | collective-permute-start | bytes 24584 | tf_op jit(solution)/shard_map/ppermute | solution.py:394
  16.5 4.8 %collective-permute-done.1.far_ref = bf16[32,128]{1,0:T(8,128)(2,1)S(1)} collective-permute-done((bf16[32,128]{1,0:T(8,128)(2,1)S(1)}, bf16[32,128]{1,0:T(8,128)(2,1)S(1)}, u32[]{:S(2)}, u32[]{:S(2)}) %collective-permute-start.1) | collective-permute-done | bytes 8224 | tf_op jit(solution)/shard_map/ppermute | solution.py:394
  21.3 0.0 collective-permute-done.came_ref
  21.3 0.0 copy-start.1
  21.3 0.1 shard_map.68
  21.4 21.0 %all_to_all.15.got_ref = bf16[16,136,128]{2,1,0:T(8,128)(2,1)S(1)} all-to-all(bf16[16,136,128]{2,1,0:T(8,128)(2,1)S(1)} %shard_map.68), channel_id=1, replica_groups=mesh['y'=4,'z_far'=2,'z_near'=4,'core'=2,'x'=4,'z_hi'=2] {'y','z_near'}, dimensions={0} | all-to-all | bytes 1114112 | tf_op jit(solution)/shard_map/all_to_all | solution.py:409
  42.3 0.1 shard_map.69
  42.4 7.3 %collective-permute-start.2 = (f32[40,128]{1,0:T(8,128)S(1)}, f32[40,128]{1,0:T(8,128)S(1)}, u32[]{:S(2)}, u32[]{:S(2)}) collective-permute-start(f32[40,128]{1,0:T(8,128)S(1)} %get-tuple-element.25), channel_id=1, source_target_pairs={{0,64},{64,0},{1,65},{65,1},{2,66},{66,2},{3,67},{67,3},{4,68},{68... | collective-permute-start | bytes 61448 | tf_op jit(solution)/shard_map/ppermute | solution.py:417
  49.7 3.9 %all-gather = bf16[32,64,128]{2,1,0:T(8,128)(2,1)S(1)} all-gather(bf16[16,64,128]{2,1,0:T(8,128)(2,1)S(1)} %slice.4), channel_id=2, replica_groups=mesh['y'=4,'z_far'=2,'z_near'=4,'core'=2,'x'=4,'z_hi'=2] {'core'}, dimensions={0}, use_global_device_ids=true | all-gather | bytes 786432 | tf_op jit(solution)/shard_map/all_gather | solution.py:418
  53.6 0.0 copy-done.1
  53.6 1.0 shard_map.70
  54.7 1.9 %all-gather.1 = bf16[64,256]{1,0:T(8,128)(2,1)S(1)} all-gather(bf16[32,256]{1,0:T(8,128)(2,1)S(1)} %get-tuple-element.27), channel_id=3, replica_groups=mesh['y'=4,'z_far'=2,'z_near'=4,'core'=2,'x'=4,'z_hi'=2] {'core'}, dimensions={0}, use_global_device_ids=true | all-gather | bytes 49152 | tf_op jit(solution)/shard_map/all_gather | solution.py:426
  56.5 0.0 collective-permute-done.2.came_ref
  56.5 0.1 shard_map.71
  56.7 24.8 %all_to_all.16 = f32[8,32,256]{2,1,0:T(8,128)S(1)} all-to-all(f32[8,32,256]{2,1,0:T(8,128)S(1)} %shard_map.71), channel_id=1, replica_groups=mesh['y'=4,'z_far'=2,'z_near'=4,'core'=2,'x'=4,'z_hi'=2] {'x','z_hi'}, dimensions={0} | all-to-all | bytes 524288 | tf_op jit(solution)/shard_map/all_to_all | solution.py:433
  81.5 4.1 %all-gather.2 = f32[16,32,256]{2,1,0:T(8,128)S(1)} all-gather(f32[8,32,256]{2,1,0:T(8,128)S(1)} %all_to_all.16), channel_id=4, replica_groups=mesh['y'=4,'z_far'=2,'z_near'=4,'core'=2,'x'=4,'z_hi'=2] {'core'}, dimensions={0}, use_global_device_ids=true | all-gather | bytes 786432 | tf_op jit(solution)/shard_map/all_gather | solution.py:434
  85.6 1.5 %shard_map.72 = (bf16[32,16,128]{2,1,0:T(8,128)(2,1)S(1)}, f32[32,64]{1,0:T(8,128)S(1)}, f32[32,128]{1,0:T(8,128)S(1)}, f32[32,64]{1,0:T(8,128)S(1)}, f32[32,128...) custom-call(s32[1]{0:T(128)} %bitcast.place_ref, ...), custom_call_target="tpu_custom_call" | custom-call | tf_op jit(solution)/shard_map/pallas_call | solution.py:366
  87.1 24.7 %all_to_all.17 = bf16[32,16,128]{2,1,0:T(8,128)(2,1)S(1)} all-to-all(bf16[32,16,128]{2,1,0:T(8,128)(2,1)S(1)} %get-tuple-element.29), channel_id=1, replica_groups=mesh['y'=4,'z_far'=2,'z_near'=4,'core'=2,'x'=4,'z_hi'=2] {'y','z_far','z..., dimensions={0} | all-to-all | bytes 262144 | tf_op jit(solution)/shard_map/all_to_all | solution.py:443
  111.9 5.1 %all-gather.3 = bf16[64,16,128]{2,1,0:T(8,128)(2,1)S(1)} all-gather(bf16[32,16,128]{2,1,0:T(8,128)(2,1)S(1)} %all_to_all.17), channel_id=5, replica_groups=mesh['y'=4,'z_far'=2,'z_near'=4,'core'=2,'x'=4,'z_hi'=2] {'core'}, dimensions={0}, use_global_device_ids=true | all-gather | bytes 393216 | tf_op jit(solution)/shard_map/all_gather | solution.py:444
  117.0 2.2 %shard_map.73 = (f32[32,64]{1,0:T(8,128)}, f32[32,128]{1,0:T(8,128)}, f32[2,32]{1,0:T(2,128)}) custom-call(s32[1]{0:T(128)} %bitcast.place_ref, bf16[2,32,16,128]{3,2,1,0:T(8,128)(2,1)S(1)} %bitcast.12, bf16[32,64]{1,0:T(8,128)(2,1)S(1)} %copy-done.2, bf16[32,128]{1,0:T(8,128)(2,1)S(1)} %copy-done.3, f32[32,32]{1,0:T(8,128)S(1)} %get-tuple-element.30.gram_a_ref, ...), custom_call_target="tpu_custom_call" | custom-call | tf_op jit(solution)/shard_map/pallas_call | solution.py:366
  (1 shorter events, 0.0 us)
Async XLA Ops:
  0.6 12.3 %copy-start.3 = (bf16[32,128]{1,0:T(8,128)(2,1)S(1)}, bf16[32,128]{1,0:T(8,128)(2,1)}, u32[]{:S(2)}) copy-start(bf16[32,128]{1,0:T(8,128)(2,1)} %b_ref.3) | copy-start | bytes 24580
  0.7 1.6 %copy-start = (bf16[2,64,8192]{2,1,0:T(8,128)(2,1)S(1)}, bf16[2,64,8192]{2,1,0:T(8,128)(2,1)}, u32[]{:S(2)}) copy-start(bf16[2,64,8192]{2,1,0:T(8,128)(2,1)} %param.4) | copy-start | bytes 6291460
  2.2 0.7 copy-start.2
  2.9 0.7 copy-start.4
  4.2 17.1 %collective-permute-start = (f32[1032,128]{1,0:T(8,128)S(1)}, f32[1032,128]{1,0:T(8,128)S(1)}, u32[]{:S(2)}, u32[]{:S(2)}) collective-permute-start(f32[1032,128]{1,0:T(8,128)S(1)} %get-tuple-element.23), channel_id=1, source_target_pairs={{0,8},{8,0},{1,9},{9,1},{2,10},{10,2},{3,11},{11,3},{4,12},{12,4},... | collective-permute-start | bytes 1585160 | tf_op jit(solution)/shard_map/ppermute | solution.py:402
  13.0 8.3 %collective-permute-start.1 = (bf16[32,128]{1,0:T(8,128)(2,1)S(1)}, bf16[32,128]{1,0:T(8,128)(2,1)S(1)}, u32[]{:S(2)}, u32[]{:S(2)}) collective-permute-start(bf16[32,128]{1,0:T(8,128)(2,1)S(1)} %copy-done.3), channel_id=1, source_target_pairs={{0,64},{64,0},{1,65},{65,1},{2,66},{66,2},{3,67},{67,3},{4,68},{68... | collective-permute-start | bytes 24584 | tf_op jit(solution)/shard_map/ppermute | solution.py:394
  21.3 32.4 %copy-start.1 = (bf16[2,64,8192]{2,1,0:T(8,128)(2,1)S(1)}, bf16[2,64,8192]{2,1,0:T(8,128)(2,1)}, u32[]{:S(2)}) copy-start(bf16[2,64,8192]{2,1,0:T(8,128)(2,1)} %param.4) | copy-start | bytes 6291460
  42.4 14.1 %collective-permute-start.2 = (f32[40,128]{1,0:T(8,128)S(1)}, f32[40,128]{1,0:T(8,128)S(1)}, u32[]{:S(2)}, u32[]{:S(2)}) collective-permute-start(f32[40,128]{1,0:T(8,128)S(1)} %get-tuple-element.25), channel_id=1, source_target_pairs={{0,64},{64,0},{1,65},{65,1},{2,66},{66,2},{3,67},{67,3},{4,68},{68... | collective-permute-start | bytes 61448 | tf_op jit(solution)/shard_map/ppermute | solution.py:417

commit v6 on v5

--- a/solution.py
+++ b/solution.py
@@ -135,7 +135,7 @@
     factors_ref[:, LANES:] = jnp.concatenate([float_a, float_a], axis=1).astype(bf16)
 
 
-def partials_kernel(nears, others, place_ref, t_ref, a_ref, ct_ref, both_ref, tile_ref, gram_ref, whole_b):
+def partials_kernel(nears, t_ref, a_ref, ct_ref, both_ref, tile_ref, gram_ref, whole_b):
     rank, i_local = a_ref.shape
     near_z = WIDE[2]
     for core in range(2):
@@ -162,27 +162,40 @@
     against_a = contracted * jnp.concatenate([float_a, float_a], axis=1)
     c_first = jnp.sum(jnp.where(low_half, against_a, 0.0), axis=1, keepdims=True)
     c_second = jnp.sum(jnp.where(low_half, 0.0, against_a), axis=1, keepdims=True)
-    at = i_local + 2 * (place_ref[0] // 4)
-    k_all = 2 * others
-    tail = jnp.where(spot == at, c_first, 0.0)
-    tail = jnp.where(spot == at + 1, c_second, tail)
-    tail = jnp.where(spot == at + k_all, first, tail)
-    tail = jnp.where(spot == at + k_all + 1, second, tail)
-    tile_ref[...] = jnp.where(low_half, part_a, tail)
-
-
-def send_narrow_kernel(others, place_ref, keep_ref, came_ref, tile_ref, factors_ref, out_ref):
-    rank = tile_ref.shape[0]
+    square = lax.broadcasted_iota(jnp.int32, (rank, rank), 0) == lane(rank, rank)
+    parts = [jnp.sum(jnp.where(square, c, 0.0), axis=0, keepdims=True) for c in (c_first, c_second)]
+    leads = [part.astype(bf16).astype(f32) for part in parts]
+    rests = [part - lead for part, lead in zip(parts, leads)]
+    own_c = [ct_ref[k : k + 1, :].astype(f32) for k in range(2)]
+    half = rank // 2
+    tile_ref[:half, :] = jnp.where(lane(half, LANES) < i_local, part_a[:half], part_a[half:])
+    tile_ref[half:, :] = jnp.concatenate(
+        [
+            jnp.concatenate(leads + rests, axis=1),
+            jnp.concatenate(own_c + [jnp.zeros((1, 2 * rank), f32)], axis=1),
+            jnp.zeros((6, LANES), f32),
+        ],
+        axis=0,
+    )
+
+
+def send_narrow_kernel(others, keep_ref, came_ref, tile_ref, factors_ref, out_ref):
+    rank = factors_ref.shape[1]
+    half = rank // 2
     total = keep_ref[...] + came_ref[...]
-    sum_b = total[:rank]
-    gram = jnp.concatenate([total[rank:, :rank], total[rank:, rank : 2 * rank]], axis=0)
-    gram = jnp.where(place_ref[0] // 4 == 0, gram, 0.0)
-    gram = jnp.concatenate([gram, jnp.zeros((rank // 2, rank), f32)], axis=0)
-    gram = jnp.concatenate([jnp.zeros((rank, LANES - rank), f32), gram], axis=1)
-    tile = tile_ref[...] + gram
+    gram = total[rank:, : 2 * rank]
+    lead = gram.astype(bf16).astype(f32)
+    packed = jnp.concatenate(
+        [
+            total[:rank],
+            tile_ref[:half, :],
+            jnp.concatenate([lead, gram - lead], axis=1),
+            tile_ref[half:, :],
+        ],
+        axis=0,
+    ).astype(bf16)
     for other in range(others):
-        out_ref[other, :, :LANES] = sum_b
-        out_ref[other, :, LANES:] = tile
+        out_ref[other] = packed
 
 
 def residual_kernel(others, links, place_ref, got_ref, factors_ref, gram_b_ref, out_ref, ra_ref, rb_ref, ha_ref, hb_ref, c_ref, model_c_ref, gram_a_ref, gram_c_ref):
@@ -190,19 +203,44 @@
     k_all = 2 * others
     first_core = place_ref[0] % 2 == 0
     gram_b = gram_b_ref[...]
-    totals = []
+    half = rank // 2
+    slab = rank // 4
+    square = lax.broadcasted_iota(jnp.int32, (rank, rank), 0) == lane(rank, rank)
+    eye = square.astype(f32)
+    spot = lax.broadcasted_iota(jnp.int32, (others, LANES), 0)
+    mttkrps = []
+    grams = []
+    part_c = jnp.zeros((k_all, rank), f32)
     for core in range(2):
-        total = got_ref[core, 0]
-        for other in range(1, others):
-            total = total + got_ref[core, other]
-        totals.append(total)
-    after = LANES + i_local
-    factor_c = totals[0][:, after + k_all : after + 2 * k_all]
-    part_c = totals[0][:, after : after + k_all] + totals[1][:, after : after + k_all]
+
+        def summed(rows):
+            total = got_ref[core, 0, rows, :].astype(f32)
+            for other in range(1, others):
+                total = total + got_ref[core, other, rows, :].astype(f32)
+            return total
+
+        wide_a = summed(pl.ds(rank, half))
+        mttkrps.append(
+            (
+                jnp.concatenate([wide_a[:, :i_local], wide_a[:, i_local:]], axis=0),
+                summed(pl.ds(0, rank)),
+            )
+        )
+        gram = got_ref[core, 0, rank + half : rank + half + slab, :].astype(f32)
+        gram = gram[:, : 2 * rank] + gram[:, 2 * rank :]
+        grams += [gram[:, :rank], gram[:, rank:]]
+        upper = jnp.zeros((others, LANES), f32)
+        lower = upper
+        for other in range(others):
+            block = got_ref[core, other, rank + half + slab :, :].astype(f32)
+            upper = jnp.where(spot == other, block[0:1, :], upper)
+            lower = jnp.where(spot == other, block[1:2, :], lower)
+        upper = upper[:, : 2 * rank] + upper[:, 2 * rank :]
+        part_c = part_c + jnp.concatenate([upper[:, :rank], upper[:, rank:]], axis=0)
+    factor_c = mul_t(eye, jnp.concatenate([lower[:, :rank], lower[:, rank : 2 * rank]], axis=0))
+    part_c = mul_t(eye, part_c)
     gram_c = mul_t(factor_c, factor_c)
-    gram_a = jnp.concatenate(
-        [total[: rank // 2, 2 * LANES - rank :] for total in totals], axis=0
-    )
+    gram_a = jnp.concatenate(grams, axis=0)
     had_a = gram_b * gram_c
     had_b = gram_a * gram_c
     gram_a_ref[...] = gram_a
@@ -217,8 +255,8 @@
         float_a = factors_ref[core, :, LANES : LANES + i_local].astype(f32)
         own = []
         for mttkrp, factor, had in (
-            (totals[core][:, LANES:after], float_a, had_a),
-            (totals[core][:, :LANES], float_b, had_b),
+            (mttkrps[core][0], float_a, had_a),
+            (mttkrps[core][1], float_b, had_b),
         ):
             res = mttkrp - mul(had, factor)
             once = mul(had, res)
@@ -349,11 +387,11 @@
     sa_ref[...] = on_res * res_a + on_image * image_a
     sb_ref[...] = on_res * res_b + on_image * image_b
     step_c = on_res * res_c + on_image * image_c
-    at = 2 * (place_ref[0] // 4)
+    at = place_ref[0] // 4
     spot = lane(rank, k_all)
     square = lax.broadcasted_iota(jnp.int32, (rank, rank), 0) == lane(rank, rank)
     for k in range(2):
-        column = jnp.sum(jnp.where(spot == at + k, step_c, 0.0), axis=1, keepdims=True)
+        column = jnp.sum(jnp.where(spot == at + k * others, step_c, 0.0), axis=1, keepdims=True)
         sc_ref[k : k + 1, :] = jnp.sum(jnp.where(square, column, 0.0), axis=0, keepdims=True)
 
 
@@ -417,18 +455,16 @@
     came = lax.ppermute(send, "z_far", [(0, 1), (1, 0)])
     both = lax.all_gather(near[:, 2 * rank : 4 * rank, :], "core", axis=0, tiled=False)
     tile, gram_b = call(
-        functools.partial(partials_kernel, nears, others),
-        (square, like((rank, rank), f32)),
-        (place, flattened, factor_a, turned_c, both),
-        scalar=True,
+        functools.partial(partials_kernel, nears),
+        (like((half + slab, LANES), f32), like((rank, rank), f32)),
+        (flattened, factor_a, turned_c, both),
         scratch=(pltpu.VMEM((rank, j_whole), bf16),),
     )
     factors = lax.all_gather(factors, "core", axis=0, tiled=False)
     narrow = call(
         functools.partial(send_narrow_kernel, others),
-        like((others, rank, 2 * LANES), f32),
-        (place, keep, came, tile, factors),
-        scalar=True,
+        like((others, rank + half + 2 * slab, LANES), bf16),
+        (keep, came, tile, factors),
     )
     narrow = lax.all_to_all(narrow, OTHER, 0, 0, tiled=True)
     narrow = lax.all_gather(narrow, "core", axis=0, tiled=False)

time: 120 us -> 113 us (0.942)
  blocking collectives: 85.5 us -> 78.6 us
    all_to_all x1, blocking collectives: 24.7 us -> 18.8 us  [stages(): send = lax.all_to_all(send, LINKS, 0, 0, tiled=True)]
    unnamed x10 -> x14, local copies, waits for them, and re-layouts: 2.95 us -> 2.95 us
where the time goes in v6:
time: 113 us; the launch traced here: 112 us
  blocking collectives  78.6 us (70%)
  starting transfers between devices  19.5 us (17%)
  Pallas kernels  5.81 us (5%)
  waiting for transfers between devices  4.83 us (4%)
  local copies, waits for them, and re-layouts  2.97 us (3%)
    all_to_all x1, blocking collectives, stages(): narrow = lax.all_to_all(narrow, OTHER, 0, 0, tiled=True)  24.2 us
    all_to_all x1, blocking collectives, stages(): near = lax.all_to_all(near, NEAR, 0, 0, tiled=True)  21 us
    all_to_all x1, blocking collectives, stages(): send = lax.all_to_all(send, LINKS, 0, 0, tiled=True)  18.8 us
    ppermute x1, starting transfers between devices, stages(): came = lax.ppermute(send, 'core', [(0, 1), (1, 0)])  8.75 us
    ppermute x1, starting transfers between devices, stages(): came = lax.ppermute(send, 'z_far', [(0, 1), (1, 0)])  7.27 us
    pallas_call x7, Pallas kernels, call(): pl.pallas_call(kernel, out_shape=outs, in_specs=specs, out_specs=tuple((v...  5.81 us
    all_gather x1, blocking collectives, stages(): every = lax.all_gather(send, 'core', axis=0, tiled=False)  5.09 us
    ppermute x1, waiting for transfers between devices, stages(): far = lax.ppermute(factor_b, 'z_far', [(0, 1), (1, 0)])  4.82 us
  transfers between devices with their start and end apart: 3, of which 1 were waited for; matrix products, arithmetic and copies ran while one was open for 0% of the time, Pallas kernels for 1%

profile of v6, /device:TPU:1, one launch (start us, length us, event | category | flops | bytes accessed | tf_op | source)
XLA Modules:
  0.0 112.4 jit_solution(11712368078297960364)
XLA Ops:
  0.6 0.0 copy-start.4
  0.7 0.0 copy-start
  0.7 1.6 %copy-done = bf16[2,64,8192]{2,1,0:T(8,128)(2,1)S(1)} copy-done((bf16[2,64,8192]{2,1,0:T(8,128)(2,1)S(1)}, bf16[2,64,8192]{2,1,0:T(8,128)(2,1)}, u32[]{:S(2)}) %copy-start) | copy-done | bytes 2097176
  2.2 0.0 copy-start.2
  2.2 0.7 copy-done.2
  2.9 0.0 copy-start.5
  2.9 0.7 copy-done.5
  3.6 0.6 shard_map.67
  4.2 8.7 %collective-permute-start = (f32[1032,128]{1,0:T(8,128)S(1)}, f32[1032,128]{1,0:T(8,128)S(1)}, u32[]{:S(2)}, u32[]{:S(2)}) collective-permute-start(f32[1032,128]{1,0:T(8,128)S(1)} %get-tuple-element.23), channel_id=1, source_target_pairs={{0,8},{8,0},{1,9},{9,1},{2,10},{10,2},{3,11},{11,3},{4,12},{12,4},... | collective-permute-start | bytes 1585160 | tf_op jit(solution)/shard_map/ppermute | solution.py:440
  13.0 0.0 copy-done.4
  13.0 3.5 %collective-permute-start.1 = (bf16[32,128]{1,0:T(8,128)(2,1)S(1)}, bf16[32,128]{1,0:T(8,128)(2,1)S(1)}, u32[]{:S(2)}, u32[]{:S(2)}) collective-permute-start(bf16[32,128]{1,0:T(8,128)(2,1)S(1)} %copy-done.4), channel_id=1, source_target_pairs={{0,64},{64,0},{1,65},{65,1},{2,66},{66,2},{3,67},{67,3},{4,68},{68... | collective-permute-start | bytes 24584 | tf_op jit(solution)/shard_map/ppermute | solution.py:432
  16.5 4.8 %collective-permute-done.1.far_ref = bf16[32,128]{1,0:T(8,128)(2,1)S(1)} collective-permute-done((bf16[32,128]{1,0:T(8,128)(2,1)S(1)}, bf16[32,128]{1,0:T(8,128)(2,1)S(1)}, u32[]{:S(2)}, u32[]{:S(2)}) %collective-permute-start.1) | collective-permute-done | bytes 8224 | tf_op jit(solution)/shard_map/ppermute | solution.py:432
  21.3 0.0 collective-permute-done.came_ref
  21.3 0.0 copy-start.1
  21.3 0.1 shard_map.68
  21.4 21.0 %all_to_all.15.got_ref = bf16[16,136,128]{2,1,0:T(8,128)(2,1)S(1)} all-to-all(bf16[16,136,128]{2,1,0:T(8,128)(2,1)S(1)} %shard_map.68), channel_id=1, replica_groups=mesh['y'=4,'z_far'=2,'z_near'=4,'core'=2,'x'=4,'z_hi'=2] {'y','z_near'}, dimensions={0} | all-to-all | bytes 1114112 | tf_op jit(solution)/shard_map/all_to_all | solution.py:447
  42.3 0.1 shard_map.69
  42.4 7.3 %collective-permute-start.2 = (f32[40,128]{1,0:T(8,128)S(1)}, f32[40,128]{1,0:T(8,128)S(1)}, u32[]{:S(2)}, u32[]{:S(2)}) collective-permute-start(f32[40,128]{1,0:T(8,128)S(1)} %get-tuple-element.25), channel_id=1, source_target_pairs={{0,64},{64,0},{1,65},{65,1},{2,66},{66,2},{3,67},{67,3},{4,68},{68... | collective-permute-start | bytes 61448 | tf_op jit(solution)/shard_map/ppermute | solution.py:455
  49.7 3.9 %all-gather = bf16[32,64,128]{2,1,0:T(8,128)(2,1)S(1)} all-gather(bf16[16,64,128]{2,1,0:T(8,128)(2,1)S(1)} %slice.4), channel_id=2, replica_groups=mesh['y'=4,'z_far'=2,'z_near'=4,'core'=2,'x'=4,'z_hi'=2] {'core'}, dimensions={0}, use_global_device_ids=true | all-gather | bytes 786432 | tf_op jit(solution)/shard_map/all_gather | solution.py:456
  53.7 0.0 copy-done.1
  53.7 0.0 copy-done.3
  53.7 0.0 copy-done.6
  53.7 1.1 shard_map.70
  54.7 1.9 %all-gather.1 = bf16[64,256]{1,0:T(8,128)(2,1)S(1)} all-gather(bf16[32,256]{1,0:T(8,128)(2,1)S(1)} %get-tuple-element.27), channel_id=3, replica_groups=mesh['y'=4,'z_far'=2,'z_near'=4,'core'=2,'x'=4,'z_hi'=2] {'core'}, dimensions={0}, use_global_device_ids=true | all-gather | bytes 49152 | tf_op jit(solution)/shard_map/all_gather | solution.py:463
  56.6 0.0 collective-permute-done.2.came_ref
  56.6 0.1 shard_map.71
  56.7 24.2 %all_to_all.16 = bf16[8,64,128]{2,1,0:T(8,128)(2,1)S(1)} all-to-all(bf16[8,64,128]{2,1,0:T(8,128)(2,1)S(1)} %shard_map.71), channel_id=1, replica_groups=mesh['y'=4,'z_far'=2,'z_near'=4,'core'=2,'x'=4,'z_hi'=2] {'x','z_hi'}, dimensions={0} | all-to-all | bytes 262144 | tf_op jit(solution)/shard_map/all_to_all | solution.py:469
  80.9 3.7 %all-gather.2 = bf16[16,64,128]{2,1,0:T(8,128)(2,1)S(1)} all-gather(bf16[8,64,128]{2,1,0:T(8,128)(2,1)S(1)} %all_to_all.16), channel_id=4, replica_groups=mesh['y'=4,'z_far'=2,'z_near'=4,'core'=2,'x'=4,'z_hi'=2] {'core'}, dimensions={0}, use_global_device_ids=true | all-gather | bytes 393216 | tf_op jit(solution)/shard_map/all_gather | solution.py:470
  84.6 1.7 %shard_map.72 = (bf16[32,16,128]{2,1,0:T(8,128)(2,1)S(1)}, f32[32,64]{1,0:T(8,128)S(1)}, f32[32,128]{1,0:T(8,128)S(1)}, f32[32,64]{1,0:T(8,128)S(1)}, f32[32,128...) custom-call(s32[1]{0:T(128)} %bitcast.place_ref, ...), custom_call_target="tpu_custom_call" | custom-call | tf_op jit(solution)/shard_map/pallas_call | solution.py:404
  86.3 18.8 %all_to_all.17 = bf16[32,16,128]{2,1,0:T(8,128)(2,1)S(1)} all-to-all(bf16[32,16,128]{2,1,0:T(8,128)(2,1)S(1)} %get-tuple-element.29), channel_id=1, replica_groups=mesh['y'=4,'z_far'=2,'z_near'=4,'core'=2,'x'=4,'z_hi'=2] {'y','z_far','z..., dimensions={0} | all-to-all | bytes 262144 | tf_op jit(solution)/shard_map/all_to_all | solution.py:479
  105.1 5.1 %all-gather.3 = bf16[64,16,128]{2,1,0:T(8,128)(2,1)S(1)} all-gather(bf16[32,16,128]{2,1,0:T(8,128)(2,1)S(1)} %all_to_all.17), channel_id=5, replica_groups=mesh['y'=4,'z_far'=2,'z_near'=4,'core'=2,'x'=4,'z_hi'=2] {'core'}, dimensions={0}, use_global_device_ids=true | all-gather | bytes 393216 | tf_op jit(solution)/shard_map/all_gather | solution.py:480
  110.2 2.2 %shard_map.73 = (f32[32,64]{1,0:T(8,128)}, f32[32,128]{1,0:T(8,128)}, f32[2,32]{1,0:T(2,128)}) custom-call(s32[1]{0:T(128)} %bitcast.place_ref, bf16[2,32,16,128]{3,2,1,0:T(8,128)(2,1)S(1)} %bitcast.12, bf16[32,64]{1,0:T(8,128)(2,1)S(1)} %copy-done.3, bf16[32,128]{1,0:T(8,128)(2,1)S(1)} %copy-done.4, f32[32,32]{1,0:T(8,128)S(1)} %get-tuple-element.30.gram_a_ref, ...), custom_call_target="tpu_custom_call" | custom-call | tf_op jit(solution)/shard_map/pallas_call | solution.py:404
  (3 shorter events, 0.0 us)
Async XLA Ops:
  0.6 12.3 %copy-start.4 = (bf16[32,128]{1,0:T(8,128)(2,1)S(1)}, bf16[32,128]{1,0:T(8,128)(2,1)}, u32[]{:S(2)}) copy-start(bf16[32,128]{1,0:T(8,128)(2,1)} %b_ref.3) | copy-start | bytes 24580
  0.7 1.6 %copy-start = (bf16[2,64,8192]{2,1,0:T(8,128)(2,1)S(1)}, bf16[2,64,8192]{2,1,0:T(8,128)(2,1)}, u32[]{:S(2)}) copy-start(bf16[2,64,8192]{2,1,0:T(8,128)(2,1)} %param.4) | copy-start | bytes 6291460
  2.2 0.7 copy-start.2
  2.9 0.7 copy-start.5
  4.2 17.1 %collective-permute-start = (f32[1032,128]{1,0:T(8,128)S(1)}, f32[1032,128]{1,0:T(8,128)S(1)}, u32[]{:S(2)}, u32[]{:S(2)}) collective-permute-start(f32[1032,128]{1,0:T(8,128)S(1)} %get-tuple-element.23), channel_id=1, source_target_pairs={{0,8},{8,0},{1,9},{9,1},{2,10},{10,2},{3,11},{11,3},{4,12},{12,4},... | collective-permute-start | bytes 1585160 | tf_op jit(solution)/shard_map/ppermute | solution.py:440
  13.0 8.3 %collective-permute-start.1 = (bf16[32,128]{1,0:T(8,128)(2,1)S(1)}, bf16[32,128]{1,0:T(8,128)(2,1)S(1)}, u32[]{:S(2)}, u32[]{:S(2)}) collective-permute-start(bf16[32,128]{1,0:T(8,128)(2,1)S(1)} %copy-done.4), channel_id=1, source_target_pairs={{0,64},{64,0},{1,65},{65,1},{2,66},{66,2},{3,67},{67,3},{4,68},{68... | collective-permute-start | bytes 24584 | tf_op jit(solution)/shard_map/ppermute | solution.py:432
  21.3 32.4 %copy-start.1 = (bf16[2,64,8192]{2,1,0:T(8,128)(2,1)S(1)}, bf16[2,64,8192]{2,1,0:T(8,128)(2,1)}, u32[]{:S(2)}) copy-start(bf16[2,64,8192]{2,1,0:T(8,128)(2,1)} %param.4) | copy-start | bytes 6291460
  21.3 32.4 %copy-start.3 = (bf16[32,64]{1,0:T(8,128)(2,1)S(1)}, bf16[32,64]{1,0:T(8,128)(2,1)}, u32[]{:S(2)}) copy-start(bf16[32,64]{1,0:T(8,128)(2,1)} %a_ref.7) | copy-start | bytes 12292
  21.3 32.4 %copy-start.6 = (bf16[32,2]{0,1:T(2,128)(2,1)S(1)}, bf16[32,2]{0,1:T(2,128)(2,1)}, u32[]{:S(2)}) copy-start(bf16[32,2]{0,1:T(2,128)(2,1)} %param.7) | copy-start | bytes 388
  42.4 14.2 %collective-permute-start.2 = (f32[40,128]{1,0:T(8,128)S(1)}, f32[40,128]{1,0:T(8,128)S(1)}, u32[]{:S(2)}, u32[]{:S(2)}) collective-permute-start(f32[40,128]{1,0:T(8,128)S(1)} %get-tuple-element.25), channel_id=1, source_target_pairs={{0,64},{64,0},{1,65},{65,1},{2,66},{66,2},{3,67},{67,3},{4,68},{68... | collective-permute-start | bytes 61448 | tf_op jit(solution)/shard_map/ppermute | solution.py:455

commit v7 on v6

--- a/solution.py
+++ b/solution.py
@@ -53,6 +53,10 @@
 def gather_rows(wide_block):
     width = wide_block.shape[1] // 4
     return jnp.concatenate([wide_block[:, k * width : (k + 1) * width] for k in range(4)], axis=0)
+
+
+def lead_kernel(place_ref, out_ref):
+    out_ref[0] = place_ref[0]
 
 
 def partial_b_kernel(chunks, place_ref, t_ref, a_ref, ct_ref, keep_ref, send_ref):
@@ -429,6 +433,15 @@
     thin = like((rank, i_local), f32)
 
     slab = rank // 4
+    smem = pl.BlockSpec(memory_space=pltpu.SMEM)
+    place = pl.pallas_call(
+        lead_kernel,
+        out_shape=like((1,), jnp.int32),
+        in_specs=[smem],
+        out_specs=smem,
+        cost_estimate=pl.CostEstimate(flops=10_000_000_000, bytes_accessed=8, transcendentals=0),
+        compiler_params=pltpu.CompilerParams(vmem_limit_bytes=1 << 20),
+    )(place)
     far = lax.ppermute(factor_b, "z_far", [(0, 1), (1, 0)])
     rows = like((chunks * rank + slab, LANES), f32)
     keep, send = call(

time: 113 us -> 114 us (level)
  Pallas kernels: 5.81 us -> 9.43 us
  local copies, waits for them, and re-layouts: 2.97 us -> 1.06 us
    pallas_call x7, Pallas kernels: 5.81 us -> 8.91 us  [call(): pl.pallas_call(kernel, out_shape=outs, in_specs=specs, out_specs=tuple((v...]
    unnamed x14 -> x8, local copies, waits for them, and re-layouts: 2.95 us -> 1.04 us
where the time goes in v7:
time: 114 us; the launch traced here: 113 us
  blocking collectives  77.7 us (68%)
  starting transfers between devices  19.5 us (17%)
  Pallas kernels  9.43 us (8%)
  waiting for transfers between devices  4.83 us (4%)
    all_to_all x1, blocking collectives, stages(): narrow = lax.all_to_all(narrow, OTHER, 0, 0, tiled=True)  24.2 us
    all_to_all x1, blocking collectives, stages(): near = lax.all_to_all(near, NEAR, 0, 0, tiled=True)  20.8 us
    all_to_all x1, blocking collectives, stages(): send = lax.all_to_all(send, LINKS, 0, 0, tiled=True)  18.1 us
    pallas_call x7, Pallas kernels, call(): pl.pallas_call(kernel, out_shape=outs, in_specs=specs, out_specs=tuple((v...  8.91 us
    ppermute x1, starting transfers between devices, stages(): came = lax.ppermute(send, 'core', [(0, 1), (1, 0)])  8.74 us
    ppermute x1, starting transfers between devices, stages(): came = lax.ppermute(send, 'z_far', [(0, 1), (1, 0)])  7.27 us
    all_gather x1, blocking collectives, stages(): every = lax.all_gather(send, 'core', axis=0, tiled=False)  5.09 us
    ppermute x1, waiting for transfers between devices, stages(): far = lax.ppermute(factor_b, 'z_far', [(0, 1), (1, 0)])  4.83 us
  transfers between devices with their start and end apart: 3, of which 1 were waited for; matrix products, arithmetic and copies ran while one was open for 0% of the time, Pallas kernels for 1%

profile of v7, /device:TPU:1, one launch (start us, length us, event | category | flops | bytes accessed | tf_op | source)
XLA Modules:
  0.0 113.3 jit_solution(8736784815803716504)
XLA Ops:
  0.6 0.0 copy-start
  0.7 0.0 copy-start.1
  0.7 0.0 copy-start.3
  0.7 0.5 shard_map.67.place_ref
  1.2 0.0 copy-start.2
  1.2 1.0 copy-done
  2.2 0.0 copy-done.1
  2.2 0.0 copy-done.3
  2.2 1.2 %shard_map.68 = (f32[1032,128]{1,0:T(8,128)S(1)}, f32[1032,128]{1,0:T(8,128)S(1)}) custom-call(s32[1]{0:T(128)} %shard_map.67.place_ref, bf16[128,8192]{1,0:T(8,128)(2,1)S(1)} %bitcast.8, bf16[32,64]{1,0:T(8,128)(2,1)S(1)} %copy-done.1, bf16[2,32]{1,0:T(2,128)(2,1)S(1)} %bitcast.15), custom_call_target="tpu_custom_call" | custom-call | tf_op jit(solution)/shard_map/pallas_call | solution.py:408
  3.5 8.7 %collective-permute-start = (f32[1032,128]{1,0:T(8,128)S(1)}, f32[1032,128]{1,0:T(8,128)S(1)}, u32[]{:S(2)}, u32[]{:S(2)}) collective-permute-start(f32[1032,128]{1,0:T(8,128)S(1)} %get-tuple-element.23), channel_id=1, source_target_pairs={{0,8},{8,0},{1,9},{9,1},{2,10},{10,2},{3,11},{11,3},{4,12},{12,4},... | collective-permute-start | bytes 1585160 | tf_op jit(solution)/shard_map/ppermute | solution.py:453
  12.2 0.0 copy-done.2
  12.2 3.5 %collective-permute-start.1 = (bf16[32,128]{1,0:T(8,128)(2,1)S(1)}, bf16[32,128]{1,0:T(8,128)(2,1)S(1)}, u32[]{:S(2)}, u32[]{:S(2)}) collective-permute-start(bf16[32,128]{1,0:T(8,128)(2,1)S(1)} %copy-done.2), channel_id=1, source_target_pairs={{0,64},{64,0},{1,65},{65,1},{2,66},{66,2},{3,67},{67,3},{4,68},{68... | collective-permute-start | bytes 24584 | tf_op jit(solution)/shard_map/ppermute | solution.py:445
  15.7 4.8 %collective-permute-done.1.far_ref = bf16[32,128]{1,0:T(8,128)(2,1)S(1)} collective-permute-done((bf16[32,128]{1,0:T(8,128)(2,1)S(1)}, bf16[32,128]{1,0:T(8,128)(2,1)S(1)}, u32[]{:S(2)}, u32[]{:S(2)}) %collective-permute-start.1) | collective-permute-done | bytes 8224 | tf_op jit(solution)/shard_map/ppermute | solution.py:445
  20.5 0.0 collective-permute-done.came_ref
  20.5 0.7 shard_map.69
  21.3 20.8 %all_to_all.15.got_ref = bf16[16,136,128]{2,1,0:T(8,128)(2,1)S(1)} all-to-all(bf16[16,136,128]{2,1,0:T(8,128)(2,1)S(1)} %shard_map.69), channel_id=1, replica_groups=mesh['y'=4,'z_far'=2,'z_near'=4,'core'=2,'x'=4,'z_hi'=2] {'y','z_near'}, dimensions={0} | all-to-all | bytes 1114112 | tf_op jit(solution)/shard_map/all_to_all | solution.py:460
  42.1 0.7 shard_map.70
  42.8 7.3 %collective-permute-start.2 = (f32[40,128]{1,0:T(8,128)S(1)}, f32[40,128]{1,0:T(8,128)S(1)}, u32[]{:S(2)}, u32[]{:S(2)}) collective-permute-start(f32[40,128]{1,0:T(8,128)S(1)} %get-tuple-element.25), channel_id=1, source_target_pairs={{0,64},{64,0},{1,65},{65,1},{2,66},{66,2},{3,67},{67,3},{4,68},{68... | collective-permute-start | bytes 61448 | tf_op jit(solution)/shard_map/ppermute | solution.py:468
  50.1 3.9 %all-gather = bf16[32,64,128]{2,1,0:T(8,128)(2,1)S(1)} all-gather(bf16[16,64,128]{2,1,0:T(8,128)(2,1)S(1)} %slice.4), channel_id=2, replica_groups=mesh['y'=4,'z_far'=2,'z_near'=4,'core'=2,'x'=4,'z_hi'=2] {'core'}, dimensions={0}, use_global_device_ids=true | all-gather | bytes 786432 | tf_op jit(solution)/shard_map/all_gather | solution.py:469
  54.0 1.1 shard_map.71
  55.1 1.9 %all-gather.1 = bf16[64,256]{1,0:T(8,128)(2,1)S(1)} all-gather(bf16[32,256]{1,0:T(8,128)(2,1)S(1)} %get-tuple-element.27), channel_id=3, replica_groups=mesh['y'=4,'z_far'=2,'z_near'=4,'core'=2,'x'=4,'z_hi'=2] {'core'}, dimensions={0}, use_global_device_ids=true | all-gather | bytes 49152 | tf_op jit(solution)/shard_map/all_gather | solution.py:476
  56.9 0.0 collective-permute-done.2.came_ref
  57.0 0.1 shard_map.72
  57.0 24.2 %all_to_all.16 = bf16[8,64,128]{2,1,0:T(8,128)(2,1)S(1)} all-to-all(bf16[8,64,128]{2,1,0:T(8,128)(2,1)S(1)} %shard_map.72), channel_id=1, replica_groups=mesh['y'=4,'z_far'=2,'z_near'=4,'core'=2,'x'=4,'z_hi'=2] {'x','z_hi'}, dimensions={0} | all-to-all | bytes 262144 | tf_op jit(solution)/shard_map/all_to_all | solution.py:482
  81.2 3.7 %all-gather.2 = bf16[16,64,128]{2,1,0:T(8,128)(2,1)S(1)} all-gather(bf16[8,64,128]{2,1,0:T(8,128)(2,1)S(1)} %all_to_all.16), channel_id=4, replica_groups=mesh['y'=4,'z_far'=2,'z_near'=4,'core'=2,'x'=4,'z_hi'=2] {'core'}, dimensions={0}, use_global_device_ids=true | all-gather | bytes 393216 | tf_op jit(solution)/shard_map/all_gather | solution.py:483
  84.9 2.3 %shard_map.73 = (bf16[32,16,128]{2,1,0:T(8,128)(2,1)S(1)}, f32[32,64]{1,0:T(8,128)S(1)}, f32[32,128]{1,0:T(8,128)S(1)}, f32[32,64]{1,0:T(8,128)S(1)}, f32[32,128...) custom-call(s32[1]{0:T(128)} %shard_map.67.place_ref, ...), custom_call_target="tpu_custom_call" | custom-call | tf_op jit(solution)/shard_map/pallas_call | solution.py:408
  87.2 18.1 %all_to_all.17 = bf16[32,16,128]{2,1,0:T(8,128)(2,1)S(1)} all-to-all(bf16[32,16,128]{2,1,0:T(8,128)(2,1)S(1)} %get-tuple-element.29), channel_id=1, replica_groups=mesh['y'=4,'z_far'=2,'z_near'=4,'core'=2,'x'=4,'z_hi'=2] {'y','z_far','z..., dimensions={0} | all-to-all | bytes 262144 | tf_op jit(solution)/shard_map/all_to_all | solution.py:492
  105.4 5.1 %all-gather.3 = bf16[64,16,128]{2,1,0:T(8,128)(2,1)S(1)} all-gather(bf16[32,16,128]{2,1,0:T(8,128)(2,1)S(1)} %all_to_all.17), channel_id=5, replica_groups=mesh['y'=4,'z_far'=2,'z_near'=4,'core'=2,'x'=4,'z_hi'=2] {'core'}, dimensions={0}, use_global_device_ids=true | all-gather | bytes 393216 | tf_op jit(solution)/shard_map/all_gather | solution.py:493
  110.5 2.8 %shard_map.74 = (f32[32,64]{1,0:T(8,128)}, f32[32,128]{1,0:T(8,128)}, f32[2,32]{1,0:T(2,128)}) custom-call(s32[1]{0:T(128)} %shard_map.67.place_ref, bf16[2,32,16,128]{3,2,1,0:T(8,128)(2,1)S(1)} %bitcast.12, bf16[32,64]{1,0:T(8,128)(2,1)S(1)} %copy-done.1, bf16[32,128]{1,0:T(8,128)(2,1)S(1)} %copy-done.2, f32[32,32]{1,0:T(8,128)S(1)} %get-tuple-element.30.gram_a_ref, ...), custom_call_target="tpu_custom_call" | custom-call | tf_op jit(solution)/shard_map/pallas_call | solution.py:408
  (1 shorter events, 0.0 us)
Async XLA Ops:
  0.6 1.6 %copy-start = (bf16[2,64,8192]{2,1,0:T(8,128)(2,1)S(1)}, bf16[2,64,8192]{2,1,0:T(8,128)(2,1)}, u32[]{:S(2)}) copy-start(bf16[2,64,8192]{2,1,0:T(8,128)(2,1)} %param.4) | copy-start | bytes 6291460
  0.7 1.6 %copy-start.1 = (bf16[32,64]{1,0:T(8,128)(2,1)S(1)}, bf16[32,64]{1,0:T(8,128)(2,1)}, u32[]{:S(2)}) copy-start(bf16[32,64]{1,0:T(8,128)(2,1)} %a_ref.7) | copy-start | bytes 12292
  0.7 1.6 %copy-start.3 = (bf16[32,2]{0,1:T(2,128)(2,1)S(1)}, bf16[32,2]{0,1:T(2,128)(2,1)}, u32[]{:S(2)}) copy-start(bf16[32,2]{0,1:T(2,128)(2,1)} %param.7) | copy-start | bytes 388
  1.2 11.0 %copy-start.2 = (bf16[32,128]{1,0:T(8,128)(2,1)S(1)}, bf16[32,128]{1,0:T(8,128)(2,1)}, u32[]{:S(2)}) copy-start(bf16[32,128]{1,0:T(8,128)(2,1)} %b_ref.3) | copy-start | bytes 24580
  3.5 17.1 %collective-permute-start = (f32[1032,128]{1,0:T(8,128)S(1)}, f32[1032,128]{1,0:T(8,128)S(1)}, u32[]{:S(2)}, u32[]{:S(2)}) collective-permute-start(f32[1032,128]{1,0:T(8,128)S(1)} %get-tuple-element.23), channel_id=1, source_target_pairs={{0,8},{8,0},{1,9},{9,1},{2,10},{10,2},{3,11},{11,3},{4,12},{12,4},... | collective-permute-start | bytes 1585160 | tf_op jit(solution)/shard_map/ppermute | solution.py:453
  12.2 8.3 %collective-permute-start.1 = (bf16[32,128]{1,0:T(8,128)(2,1)S(1)}, bf16[32,128]{1,0:T(8,128)(2,1)S(1)}, u32[]{:S(2)}, u32[]{:S(2)}) collective-permute-start(bf16[32,128]{1,0:T(8,128)(2,1)S(1)} %copy-done.2), channel_id=1, source_target_pairs={{0,64},{64,0},{1,65},{65,1},{2,66},{66,2},{3,67},{67,3},{4,68},{68... | collective-permute-start | bytes 24584 | tf_op jit(solution)/shard_map/ppermute | solution.py:445
  42.8 14.2 %collective-permute-start.2 = (f32[40,128]{1,0:T(8,128)S(1)}, f32[40,128]{1,0:T(8,128)S(1)}, u32[]{:S(2)}, u32[]{:S(2)}) collective-permute-start(f32[40,128]{1,0:T(8,128)S(1)} %get-tuple-element.25), channel_id=1, source_target_pairs={{0,64},{64,0},{1,65},{65,1},{2,66},{66,2},{3,67},{67,3},{4,68},{68... | collective-permute-start | bytes 61448 | tf_op jit(solution)/shard_map/ppermute | solution.py:468

commit v8 on v7

--- a/solution.py
+++ b/solution.py
@@ -56,10 +56,10 @@
 
 
 def lead_kernel(place_ref, out_ref):
-    out_ref[0] = place_ref[0]
-
-
-def partial_b_kernel(chunks, place_ref, t_ref, a_ref, ct_ref, keep_ref, send_ref):
+    out_ref[...] = jnp.zeros(out_ref.shape, f32) + place_ref[0].astype(f32)
+
+
+def partial_b_kernel(chunks, place_ref, t_ref, a_ref, ct_ref, first_ref, keep_ref, send_ref):
     rank, _ = a_ref.shape
     factor_a = a_ref[...]
     float_a = factor_a.astype(f32)
@@ -434,11 +434,11 @@
 
     slab = rank // 4
     smem = pl.BlockSpec(memory_space=pltpu.SMEM)
-    place = pl.pallas_call(
+    first = pl.pallas_call(
         lead_kernel,
-        out_shape=like((1,), jnp.int32),
+        out_shape=like((8, LANES), f32),
         in_specs=[smem],
-        out_specs=smem,
+        out_specs=pl.BlockSpec(memory_space=pltpu.VMEM),
         cost_estimate=pl.CostEstimate(flops=10_000_000_000, bytes_accessed=8, transcendentals=0),
         compiler_params=pltpu.CompilerParams(vmem_limit_bytes=1 << 20),
     )(place)
@@ -447,7 +447,7 @@
     keep, send = call(
         functools.partial(partial_b_kernel, chunks),
         (rows, rows),
-        (place, flattened, factor_a, turned_c),
+        (place, flattened, factor_a, turned_c, first),
         scalar=True,
     )
     came = lax.ppermute(send, "core", [(0, 1), (1, 0)])

time: 114 us -> 111 us (0.974)
  Pallas kernels: 9.43 us -> 5.81 us
    pallas_call x7, Pallas kernels: 8.91 us -> 5.81 us  [call(): pl.pallas_call(kernel, out_shape=outs, in_specs=specs, out_specs=tuple((v...]
where the time goes in v8:
time: 111 us
  blocking collectives  78.4 us (71%)
  starting transfers between devices  19.5 us (18%)
  Pallas kernels  5.81 us (5%)
  waiting for transfers between devices  4.83 us (4%)
  local copies, waits for them, and re-layouts  1.57 us (1%)
    all_to_all x1, blocking collectives, stages(): narrow = lax.all_to_all(narrow, OTHER, 0, 0, tiled=True)  24.2 us
    all_to_all x1, blocking collectives, stages(): near = lax.all_to_all(near, NEAR, 0, 0, tiled=True)  20.8 us
    all_to_all x1, blocking collectives, stages(): send = lax.all_to_all(send, LINKS, 0, 0, tiled=True)  18.8 us
    ppermute x1, starting transfers between devices, stages(): came = lax.ppermute(send, 'core', [(0, 1), (1, 0)])  8.74 us
    ppermute x1, starting transfers between devices, stages(): came = lax.ppermute(send, 'z_far', [(0, 1), (1, 0)])  7.27 us
    pallas_call x7, Pallas kernels, call(): pl.pallas_call(kernel, out_shape=outs, in_specs=specs, out_specs=tuple((v...  5.81 us
    all_gather x1, blocking collectives, stages(): every = lax.all_gather(send, 'core', axis=0, tiled=False)  5.09 us
    ppermute x1, waiting for transfers between devices, stages(): far = lax.ppermute(factor_b, 'z_far', [(0, 1), (1, 0)])  4.82 us
  transfers between devices with their start and end apart: 3, of which 1 were waited for; matrix products, arithmetic and copies ran while one was open for 0% of the time, Pallas kernels for 1%

profile of v8, /device:TPU:1, one launch (start us, length us, event | category | flops | bytes accessed | tf_op | source)
XLA Modules:
  0.0 110.9 jit_solution(6325194578255924300)
XLA Ops:
  0.6 0.0 copy-start
  0.7 0.0 copy-start.1
  0.7 0.0 copy-start.3
  0.7 0.0 copy-start.2
  0.7 1.5 %copy-done = bf16[2,64,8192]{2,1,0:T(8,128)(2,1)S(1)} copy-done((bf16[2,64,8192]{2,1,0:T(8,128)(2,1)S(1)}, bf16[2,64,8192]{2,1,0:T(8,128)(2,1)}, u32[]{:S(2)}) %copy-start) | copy-done | bytes 2097176
  2.2 0.0 copy-done.1
  2.2 0.0 copy-done.3
  2.2 0.6 shard_map.68
  2.9 8.7 %collective-permute-start = (f32[1032,128]{1,0:T(8,128)S(1)}, f32[1032,128]{1,0:T(8,128)S(1)}, u32[]{:S(2)}, u32[]{:S(2)}) collective-permute-start(f32[1032,128]{1,0:T(8,128)S(1)} %get-tuple-element.23), channel_id=1, source_target_pairs={{0,8},{8,0},{1,9},{9,1},{2,10},{10,2},{3,11},{11,3},{4,12},{12,4},... | collective-permute-start | bytes 1585160 | tf_op jit(solution)/shard_map/ppermute | solution.py:453
  11.6 0.0 copy-done.2
  11.6 3.5 %collective-permute-start.1 = (bf16[32,128]{1,0:T(8,128)(2,1)S(1)}, bf16[32,128]{1,0:T(8,128)(2,1)S(1)}, u32[]{:S(2)}, u32[]{:S(2)}) collective-permute-start(bf16[32,128]{1,0:T(8,128)(2,1)S(1)} %copy-done.2), channel_id=1, source_target_pairs={{0,64},{64,0},{1,65},{65,1},{2,66},{66,2},{3,67},{67,3},{4,68},{68... | collective-permute-start | bytes 24584 | tf_op jit(solution)/shard_map/ppermute | solution.py:445
  15.1 4.8 %collective-permute-done.1.far_ref = bf16[32,128]{1,0:T(8,128)(2,1)S(1)} collective-permute-done((bf16[32,128]{1,0:T(8,128)(2,1)S(1)}, bf16[32,128]{1,0:T(8,128)(2,1)S(1)}, u32[]{:S(2)}, u32[]{:S(2)}) %collective-permute-start.1) | collective-permute-done | bytes 8224 | tf_op jit(solution)/shard_map/ppermute | solution.py:445
  19.9 0.0 collective-permute-done.came_ref
  19.9 0.1 shard_map.69
  20.0 20.8 %all_to_all.15.got_ref = bf16[16,136,128]{2,1,0:T(8,128)(2,1)S(1)} all-to-all(bf16[16,136,128]{2,1,0:T(8,128)(2,1)S(1)} %shard_map.69), channel_id=1, replica_groups=mesh['y'=4,'z_far'=2,'z_near'=4,'core'=2,'x'=4,'z_hi'=2] {'y','z_near'}, dimensions={0} | all-to-all | bytes 1114112 | tf_op jit(solution)/shard_map/all_to_all | solution.py:460
  40.8 0.1 shard_map.70
  40.9 7.3 %collective-permute-start.2 = (f32[40,128]{1,0:T(8,128)S(1)}, f32[40,128]{1,0:T(8,128)S(1)}, u32[]{:S(2)}, u32[]{:S(2)}) collective-permute-start(f32[40,128]{1,0:T(8,128)S(1)} %get-tuple-element.25), channel_id=1, source_target_pairs={{0,64},{64,0},{1,65},{65,1},{2,66},{66,2},{3,67},{67,3},{4,68},{68... | collective-permute-start | bytes 61448 | tf_op jit(solution)/shard_map/ppermute | solution.py:468
  48.2 3.9 %all-gather = bf16[32,64,128]{2,1,0:T(8,128)(2,1)S(1)} all-gather(bf16[16,64,128]{2,1,0:T(8,128)(2,1)S(1)} %slice.4), channel_id=2, replica_groups=mesh['y'=4,'z_far'=2,'z_near'=4,'core'=2,'x'=4,'z_hi'=2] {'core'}, dimensions={0}, use_global_device_ids=true | all-gather | bytes 786432 | tf_op jit(solution)/shard_map/all_gather | solution.py:469
  52.1 1.1 shard_map.71
  53.2 1.8 %all-gather.1 = bf16[64,256]{1,0:T(8,128)(2,1)S(1)} all-gather(bf16[32,256]{1,0:T(8,128)(2,1)S(1)} %get-tuple-element.27), channel_id=3, replica_groups=mesh['y'=4,'z_far'=2,'z_near'=4,'core'=2,'x'=4,'z_hi'=2] {'core'}, dimensions={0}, use_global_device_ids=true | all-gather | bytes 49152 | tf_op jit(solution)/shard_map/all_gather | solution.py:476
  55.1 0.0 collective-permute-done.2.came_ref
  55.1 0.1 shard_map.72
  55.2 24.2 %all_to_all.16 = bf16[8,64,128]{2,1,0:T(8,128)(2,1)S(1)} all-to-all(bf16[8,64,128]{2,1,0:T(8,128)(2,1)S(1)} %shard_map.72), channel_id=1, replica_groups=mesh['y'=4,'z_far'=2,'z_near'=4,'core'=2,'x'=4,'z_hi'=2] {'x','z_hi'}, dimensions={0} | all-to-all | bytes 262144 | tf_op jit(solution)/shard_map/all_to_all | solution.py:482
  79.4 3.7 %all-gather.2 = bf16[16,64,128]{2,1,0:T(8,128)(2,1)S(1)} all-gather(bf16[8,64,128]{2,1,0:T(8,128)(2,1)S(1)} %all_to_all.16), channel_id=4, replica_groups=mesh['y'=4,'z_far'=2,'z_near'=4,'core'=2,'x'=4,'z_hi'=2] {'core'}, dimensions={0}, use_global_device_ids=true | all-gather | bytes 393216 | tf_op jit(solution)/shard_map/all_gather | solution.py:483
  83.1 1.7 %shard_map.73 = (bf16[32,16,128]{2,1,0:T(8,128)(2,1)S(1)}, f32[32,64]{1,0:T(8,128)S(1)}, f32[32,128]{1,0:T(8,128)S(1)}, f32[32,64]{1,0:T(8,128)S(1)}, f32[32,128...) custom-call(s32[1]{0:T(128)} %bitcast.place_ref, ...), custom_call_target="tpu_custom_call" | custom-call | tf_op jit(solution)/shard_map/pallas_call | solution.py:408
  84.7 18.8 %all_to_all.17 = bf16[32,16,128]{2,1,0:T(8,128)(2,1)S(1)} all-to-all(bf16[32,16,128]{2,1,0:T(8,128)(2,1)S(1)} %get-tuple-element.29), channel_id=1, replica_groups=mesh['y'=4,'z_far'=2,'z_near'=4,'core'=2,'x'=4,'z_hi'=2] {'y','z_far','z..., dimensions={0} | all-to-all | bytes 262144 | tf_op jit(solution)/shard_map/all_to_all | solution.py:492
  103.6 5.1 %all-gather.3 = bf16[64,16,128]{2,1,0:T(8,128)(2,1)S(1)} all-gather(bf16[32,16,128]{2,1,0:T(8,128)(2,1)S(1)} %all_to_all.17), channel_id=5, replica_groups=mesh['y'=4,'z_far'=2,'z_near'=4,'core'=2,'x'=4,'z_hi'=2] {'core'}, dimensions={0}, use_global_device_ids=true | all-gather | bytes 393216 | tf_op jit(solution)/shard_map/all_gather | solution.py:493
  108.7 2.2 %shard_map.74 = (f32[32,64]{1,0:T(8,128)}, f32[32,128]{1,0:T(8,128)}, f32[2,32]{1,0:T(2,128)}) custom-call(s32[1]{0:T(128)} %bitcast.place_ref, bf16[2,32,16,128]{3,2,1,0:T(8,128)(2,1)S(1)} %bitcast.12, bf16[32,64]{1,0:T(8,128)(2,1)S(1)} %copy-done.1, bf16[32,128]{1,0:T(8,128)(2,1)S(1)} %copy-done.2, f32[32,32]{1,0:T(8,128)S(1)} %get-tuple-element.30.gram_a_ref, ...), custom_call_target="tpu_custom_call" | custom-call | tf_op jit(solution)/shard_map/pallas_call | solution.py:408
  (2 shorter events, 0.0 us)
Async XLA Ops:
  0.6 1.6 %copy-start = (bf16[2,64,8192]{2,1,0:T(8,128)(2,1)S(1)}, bf16[2,64,8192]{2,1,0:T(8,128)(2,1)}, u32[]{:S(2)}) copy-start(bf16[2,64,8192]{2,1,0:T(8,128)(2,1)} %param.4) | copy-start | bytes 6291460
  0.7 1.6 %copy-start.1 = (bf16[32,64]{1,0:T(8,128)(2,1)S(1)}, bf16[32,64]{1,0:T(8,128)(2,1)}, u32[]{:S(2)}) copy-start(bf16[32,64]{1,0:T(8,128)(2,1)} %a_ref.7) | copy-start | bytes 12292
  0.7 1.6 %copy-start.3 = (bf16[32,2]{0,1:T(2,128)(2,1)S(1)}, bf16[32,2]{0,1:T(2,128)(2,1)}, u32[]{:S(2)}) copy-start(bf16[32,2]{0,1:T(2,128)(2,1)} %param.7) | copy-start | bytes 388
  0.7 10.9 %copy-start.2 = (bf16[32,128]{1,0:T(8,128)(2,1)S(1)}, bf16[32,128]{1,0:T(8,128)(2,1)}, u32[]{:S(2)}) copy-start(bf16[32,128]{1,0:T(8,128)(2,1)} %b_ref.3) | copy-start | bytes 24580
  2.9 17.1 %collective-permute-start = (f32[1032,128]{1,0:T(8,128)S(1)}, f32[1032,128]{1,0:T(8,128)S(1)}, u32[]{:S(2)}, u32[]{:S(2)}) collective-permute-start(f32[1032,128]{1,0:T(8,128)S(1)} %get-tuple-element.23), channel_id=1, source_target_pairs={{0,8},{8,0},{1,9},{9,1},{2,10},{10,2},{3,11},{11,3},{4,12},{12,4},... | collective-permute-start | bytes 1585160 | tf_op jit(solution)/shard_map/ppermute | solution.py:453
  11.6 8.3 %collective-permute-start.1 = (bf16[32,128]{1,0:T(8,128)(2,1)S(1)}, bf16[32,128]{1,0:T(8,128)(2,1)S(1)}, u32[]{:S(2)}, u32[]{:S(2)}) collective-permute-start(bf16[32,128]{1,0:T(8,128)(2,1)S(1)} %copy-done.2), channel_id=1, source_target_pairs={{0,64},{64,0},{1,65},{65,1},{2,66},{66,2},{3,67},{67,3},{4,68},{68... | collective-permute-start | bytes 24584 | tf_op jit(solution)/shard_map/ppermute | solution.py:445
  40.9 14.2 %collective-permute-start.2 = (f32[40,128]{1,0:T(8,128)S(1)}, f32[40,128]{1,0:T(8,128)S(1)}, u32[]{:S(2)}, u32[]{:S(2)}) collective-permute-start(f32[40,128]{1,0:T(8,128)S(1)} %get-tuple-element.25), channel_id=1, source_target_pairs={{0,64},{64,0},{1,65},{65,1},{2,66},{66,2},{3,67},{67,3},{4,68},{68... | collective-permute-start | bytes 61448 | tf_op jit(solution)/shard_map/ppermute | solution.py:468

commit v9 on v8

--- a/solution.py
+++ b/solution.py
@@ -183,21 +183,21 @@
     )
 
 
-def send_narrow_kernel(others, keep_ref, came_ref, tile_ref, factors_ref, out_ref):
+def send_narrow_kernel(others, place_ref, keep_ref, came_ref, tile_ref, factors_ref, out_ref):
     rank = factors_ref.shape[1]
     half = rank // 2
     total = keep_ref[...] + came_ref[...]
     gram = total[rank:, : 2 * rank]
     lead = gram.astype(bf16).astype(f32)
-    packed = jnp.concatenate(
-        [
-            total[:rank],
-            tile_ref[:half, :],
-            jnp.concatenate([lead, gram - lead], axis=1),
-            tile_ref[half:, :],
-        ],
-        axis=0,
-    ).astype(bf16)
+    terms = jnp.concatenate([lead, gram - lead], axis=1)
+    rows = terms.shape[0] // others
+    row = lax.broadcasted_iota(jnp.int32, terms.shape, 0)
+    at = (place_ref[0] // 4) * rows
+    tail = tile_ref[half:, :]
+    for k in range(rows):
+        share = jnp.sum(jnp.where(row == at + k, terms, 0.0), axis=0, keepdims=True)
+        tail = jnp.where(row == 2 + k, share, tail)
+    packed = jnp.concatenate([total[:rank], tile_ref[:half, :], tail], axis=0).astype(bf16)
     for other in range(others):
         out_ref[other] = packed
 
@@ -230,15 +230,19 @@
                 summed(pl.ds(0, rank)),
             )
         )
-        gram = got_ref[core, 0, rank + half : rank + half + slab, :].astype(f32)
-        gram = gram[:, : 2 * rank] + gram[:, 2 * rank :]
-        grams += [gram[:, :rank], gram[:, rank:]]
+        gram = jnp.zeros((slab, LANES), f32)
+        place_of = lax.broadcasted_iota(jnp.int32, (slab, LANES), 0)
+        share = slab // others
         upper = jnp.zeros((others, LANES), f32)
         lower = upper
         for other in range(others):
-            block = got_ref[core, other, rank + half + slab :, :].astype(f32)
+            block = got_ref[core, other, rank + half :, :].astype(f32)
+            for k in range(share):
+                gram = jnp.where(place_of == other * share + k, block[2 + k : 3 + k, :], gram)
             upper = jnp.where(spot == other, block[0:1, :], upper)
             lower = jnp.where(spot == other, block[1:2, :], lower)
+        gram = gram[:, : 2 * rank] + gram[:, 2 * rank :]
+        grams += [gram[:, :rank], gram[:, rank:]]
         upper = upper[:, : 2 * rank] + upper[:, 2 * rank :]
         part_c = part_c + jnp.concatenate([upper[:, :rank], upper[:, rank:]], axis=0)
     factor_c = mul_t(eye, jnp.concatenate([lower[:, :rank], lower[:, rank : 2 * rank]], axis=0))
@@ -476,8 +480,9 @@
     factors = lax.all_gather(factors, "core", axis=0, tiled=False)
     narrow = call(
         functools.partial(send_narrow_kernel, others),
-        like((others, rank + half + 2 * slab, LANES), bf16),
-        (keep, came, tile, factors),
+        like((others, rank + half + slab, LANES), bf16),
+        (place, keep, came, tile, factors),
+        scalar=True,
     )
     narrow = lax.all_to_all(narrow, OTHER, 0, 0, tiled=True)
     narrow = lax.all_gather(narrow, "core", axis=0, tiled=False)

time: 111 us -> 110 us (level)
  blocking collectives: 78.4 us -> 77.2 us
where the time goes in v9:
time: 110 us
  blocking collectives  77.2 us (70%)
  starting transfers between devices  19.5 us (18%)
  Pallas kernels  5.82 us (5%)
  waiting for transfers between devices  4.83 us (4%)
  local copies, waits for them, and re-layouts  1.57 us (1%)
    all_to_all x1, blocking collectives, stages(): narrow = lax.all_to_all(narrow, OTHER, 0, 0, tiled=True)  24 us
    all_to_all x1, blocking collectives, stages(): near = lax.all_to_all(near, NEAR, 0, 0, tiled=True)  20.8 us
    all_to_all x1, blocking collectives, stages(): send = lax.all_to_all(send, LINKS, 0, 0, tiled=True)  17.8 us
    ppermute x1, starting transfers between devices, stages(): came = lax.ppermute(send, 'core', [(0, 1), (1, 0)])  8.74 us
    ppermute x1, starting transfers between devices, stages(): came = lax.ppermute(send, 'z_far', [(0, 1), (1, 0)])  7.27 us
    pallas_call x7, Pallas kernels, call(): pl.pallas_call(kernel, out_shape=outs, in_specs=specs, out_specs=tuple((v...  5.82 us
    all_gather x1, blocking collectives, stages(): every = lax.all_gather(send, 'core', axis=0, tiled=False)  5.09 us
    ppermute x1, waiting for transfers between devices, stages(): far = lax.ppermute(factor_b, 'z_far', [(0, 1), (1, 0)])  4.82 us
  transfers between devices with their start and end apart: 3, of which 1 were waited for; matrix products, arithmetic and copies ran while one was open for 0% of the time, Pallas kernels for 1%

profile of v9, /device:TPU:1, one launch (start us, length us, event | category | flops | bytes accessed | tf_op | source)
XLA Modules:
  0.0 109.6 jit_solution(11173660702605381343)
XLA Ops:
  0.6 0.0 copy-start
  0.7 0.0 copy-start.1
  0.7 0.0 copy-start.3
  0.7 0.0 copy-start.2
  0.7 1.5 %copy-done = bf16[2,64,8192]{2,1,0:T(8,128)(2,1)S(1)} copy-done((bf16[2,64,8192]{2,1,0:T(8,128)(2,1)S(1)}, bf16[2,64,8192]{2,1,0:T(8,128)(2,1)}, u32[]{:S(2)}) %copy-start) | copy-done | bytes 2097176
  2.2 0.0 copy-done.1
  2.2 0.0 copy-done.3
  2.2 0.6 shard_map.68
  2.9 8.7 %collective-permute-start = (f32[1032,128]{1,0:T(8,128)S(1)}, f32[1032,128]{1,0:T(8,128)S(1)}, u32[]{:S(2)}, u32[]{:S(2)}) collective-permute-start(f32[1032,128]{1,0:T(8,128)S(1)} %get-tuple-element.23), channel_id=1, source_target_pairs={{0,8},{8,0},{1,9},{9,1},{2,10},{10,2},{3,11},{11,3},{4,12},{12,4},... | collective-permute-start | bytes 1585160 | tf_op jit(solution)/shard_map/ppermute | solution.py:457
  11.6 0.0 copy-done.2
  11.6 3.5 %collective-permute-start.1 = (bf16[32,128]{1,0:T(8,128)(2,1)S(1)}, bf16[32,128]{1,0:T(8,128)(2,1)S(1)}, u32[]{:S(2)}, u32[]{:S(2)}) collective-permute-start(bf16[32,128]{1,0:T(8,128)(2,1)S(1)} %copy-done.2), channel_id=1, source_target_pairs={{0,64},{64,0},{1,65},{65,1},{2,66},{66,2},{3,67},{67,3},{4,68},{68... | collective-permute-start | bytes 24584 | tf_op jit(solution)/shard_map/ppermute | solution.py:449
  15.1 4.8 %collective-permute-done.1.far_ref = bf16[32,128]{1,0:T(8,128)(2,1)S(1)} collective-permute-done((bf16[32,128]{1,0:T(8,128)(2,1)S(1)}, bf16[32,128]{1,0:T(8,128)(2,1)S(1)}, u32[]{:S(2)}, u32[]{:S(2)}) %collective-permute-start.1) | collective-permute-done | bytes 8224 | tf_op jit(solution)/shard_map/ppermute | solution.py:449
  19.9 0.0 collective-permute-done.came_ref
  19.9 0.1 shard_map.69
  20.0 20.8 %all_to_all.15.got_ref = bf16[16,136,128]{2,1,0:T(8,128)(2,1)S(1)} all-to-all(bf16[16,136,128]{2,1,0:T(8,128)(2,1)S(1)} %shard_map.69), channel_id=1, replica_groups=mesh['y'=4,'z_far'=2,'z_near'=4,'core'=2,'x'=4,'z_hi'=2] {'y','z_near'}, dimensions={0} | all-to-all | bytes 1114112 | tf_op jit(solution)/shard_map/all_to_all | solution.py:464
  40.8 0.1 shard_map.70
  40.9 7.3 %collective-permute-start.2 = (f32[40,128]{1,0:T(8,128)S(1)}, f32[40,128]{1,0:T(8,128)S(1)}, u32[]{:S(2)}, u32[]{:S(2)}) collective-permute-start(f32[40,128]{1,0:T(8,128)S(1)} %get-tuple-element.25), channel_id=1, source_target_pairs={{0,64},{64,0},{1,65},{65,1},{2,66},{66,2},{3,67},{67,3},{4,68},{68... | collective-permute-start | bytes 61448 | tf_op jit(solution)/shard_map/ppermute | solution.py:472
  48.2 3.9 %all-gather = bf16[32,64,128]{2,1,0:T(8,128)(2,1)S(1)} all-gather(bf16[16,64,128]{2,1,0:T(8,128)(2,1)S(1)} %slice.4), channel_id=2, replica_groups=mesh['y'=4,'z_far'=2,'z_near'=4,'core'=2,'x'=4,'z_hi'=2] {'core'}, dimensions={0}, use_global_device_ids=true | all-gather | bytes 786432 | tf_op jit(solution)/shard_map/all_gather | solution.py:473
  52.1 1.1 shard_map.71
  53.2 1.8 %all-gather.1 = bf16[64,256]{1,0:T(8,128)(2,1)S(1)} all-gather(bf16[32,256]{1,0:T(8,128)(2,1)S(1)} %get-tuple-element.27), channel_id=3, replica_groups=mesh['y'=4,'z_far'=2,'z_near'=4,'core'=2,'x'=4,'z_hi'=2] {'core'}, dimensions={0}, use_global_device_ids=true | all-gather | bytes 49152 | tf_op jit(solution)/shard_map/all_gather | solution.py:480
  55.1 0.0 collective-permute-done.2.came_ref
  55.1 0.1 shard_map.72
  55.2 24.0 %all_to_all.16 = bf16[8,56,128]{2,1,0:T(8,128)(2,1)S(1)} all-to-all(bf16[8,56,128]{2,1,0:T(8,128)(2,1)S(1)} %shard_map.72), channel_id=1, replica_groups=mesh['y'=4,'z_far'=2,'z_near'=4,'core'=2,'x'=4,'z_hi'=2] {'x','z_hi'}, dimensions={0} | all-to-all | bytes 229376 | tf_op jit(solution)/shard_map/all_to_all | solution.py:487
  79.1 3.8 %all-gather.2 = bf16[16,56,128]{2,1,0:T(8,128)(2,1)S(1)} all-gather(bf16[8,56,128]{2,1,0:T(8,128)(2,1)S(1)} %all_to_all.16), channel_id=4, replica_groups=mesh['y'=4,'z_far'=2,'z_near'=4,'core'=2,'x'=4,'z_hi'=2] {'core'}, dimensions={0}, use_global_device_ids=true | all-gather | bytes 344064 | tf_op jit(solution)/shard_map/all_gather | solution.py:488
  82.9 1.7 %shard_map.73 = (bf16[32,16,128]{2,1,0:T(8,128)(2,1)S(1)}, f32[32,64]{1,0:T(8,128)S(1)}, f32[32,128]{1,0:T(8,128)S(1)}, f32[32,64]{1,0:T(8,128)S(1)}, f32[32,128...) custom-call(s32[1]{0:T(128)} %bitcast.place_ref, ...), custom_call_target="tpu_custom_call" | custom-call | tf_op jit(solution)/shard_map/pallas_call | solution.py:412
  84.6 17.8 %all_to_all.17 = bf16[32,16,128]{2,1,0:T(8,128)(2,1)S(1)} all-to-all(bf16[32,16,128]{2,1,0:T(8,128)(2,1)S(1)} %get-tuple-element.29), channel_id=1, replica_groups=mesh['y'=4,'z_far'=2,'z_near'=4,'core'=2,'x'=4,'z_hi'=2] {'y','z_far','z..., dimensions={0} | all-to-all | bytes 262144 | tf_op jit(solution)/shard_map/all_to_all | solution.py:497
  102.4 5.1 %all-gather.3 = bf16[64,16,128]{2,1,0:T(8,128)(2,1)S(1)} all-gather(bf16[32,16,128]{2,1,0:T(8,128)(2,1)S(1)} %all_to_all.17), channel_id=5, replica_groups=mesh['y'=4,'z_far'=2,'z_near'=4,'core'=2,'x'=4,'z_hi'=2] {'core'}, dimensions={0}, use_global_device_ids=true | all-gather | bytes 393216 | tf_op jit(solution)/shard_map/all_gather | solution.py:498
  107.4 2.2 %shard_map.74 = (f32[32,64]{1,0:T(8,128)}, f32[32,128]{1,0:T(8,128)}, f32[2,32]{1,0:T(2,128)}) custom-call(s32[1]{0:T(128)} %bitcast.place_ref, bf16[2,32,16,128]{3,2,1,0:T(8,128)(2,1)S(1)} %bitcast.11, bf16[32,64]{1,0:T(8,128)(2,1)S(1)} %copy-done.1, bf16[32,128]{1,0:T(8,128)(2,1)S(1)} %copy-done.2, f32[32,32]{1,0:T(8,128)S(1)} %get-tuple-element.30.gram_a_ref, ...), custom_call_target="tpu_custom_call" | custom-call | tf_op jit(solution)/shard_map/pallas_call | solution.py:412
  (2 shorter events, 0.0 us)
Async XLA Ops:
  0.6 1.6 %copy-start = (bf16[2,64,8192]{2,1,0:T(8,128)(2,1)S(1)}, bf16[2,64,8192]{2,1,0:T(8,128)(2,1)}, u32[]{:S(2)}) copy-start(bf16[2,64,8192]{2,1,0:T(8,128)(2,1)} %param.4) | copy-start | bytes 6291460
  0.7 1.6 %copy-start.1 = (bf16[32,64]{1,0:T(8,128)(2,1)S(1)}, bf16[32,64]{1,0:T(8,128)(2,1)}, u32[]{:S(2)}) copy-start(bf16[32,64]{1,0:T(8,128)(2,1)} %a_ref.7) | copy-start | bytes 12292
  0.7 1.6 %copy-start.3 = (bf16[32,2]{0,1:T(2,128)(2,1)S(1)}, bf16[32,2]{0,1:T(2,128)(2,1)}, u32[]{:S(2)}) copy-start(bf16[32,2]{0,1:T(2,128)(2,1)} %param.7) | copy-start | bytes 388
  0.7 10.9 %copy-start.2 = (bf16[32,128]{1,0:T(8,128)(2,1)S(1)}, bf16[32,128]{1,0:T(8,128)(2,1)}, u32[]{:S(2)}) copy-start(bf16[32,128]{1,0:T(8,128)(2,1)} %b_ref.3) | copy-start | bytes 24580
  2.9 17.1 %collective-permute-start = (f32[1032,128]{1,0:T(8,128)S(1)}, f32[1032,128]{1,0:T(8,128)S(1)}, u32[]{:S(2)}, u32[]{:S(2)}) collective-permute-start(f32[1032,128]{1,0:T(8,128)S(1)} %get-tuple-element.23), channel_id=1, source_target_pairs={{0,8},{8,0},{1,9},{9,1},{2,10},{10,2},{3,11},{11,3},{4,12},{12,4},... | collective-permute-start | bytes 1585160 | tf_op jit(solution)/shard_map/ppermute | solution.py:457
  11.6 8.3 %collective-permute-start.1 = (bf16[32,128]{1,0:T(8,128)(2,1)S(1)}, bf16[32,128]{1,0:T(8,128)(2,1)S(1)}, u32[]{:S(2)}, u32[]{:S(2)}) collective-permute-start(bf16[32,128]{1,0:T(8,128)(2,1)S(1)} %copy-done.2), channel_id=1, source_target_pairs={{0,64},{64,0},{1,65},{65,1},{2,66},{66,2},{3,67},{67,3},{4,68},{68... | collective-permute-start | bytes 24584 | tf_op jit(solution)/shard_map/ppermute | solution.py:449
  40.9 14.2 %collective-permute-start.2 = (f32[40,128]{1,0:T(8,128)S(1)}, f32[40,128]{1,0:T(8,128)S(1)}, u32[]{:S(2)}, u32[]{:S(2)}) collective-permute-start(f32[40,128]{1,0:T(8,128)S(1)} %get-tuple-element.25), channel_id=1, source_target_pairs={{0,64},{64,0},{1,65},{65,1},{2,66},{66,2},{3,67},{67,3},{4,68},{68... | collective-permute-start | bytes 61448 | tf_op jit(solution)/shard_map/ppermute | solution.py:472
